TPU v7x, 1024 devices: a whole 4x4x32 slice. The times are simulated.
1024 devices in a mesh: seq: 64 (over z, core), head: 16 (over x, y).
Axes of the slice: x: 4, y: 4, z: 32, core: 2. Of those that a mesh axis runs over, the one named last changes fastest.
Arguments:
- queries: bfloat16 [16384, 8192], P('seq', 'head'), may hold values from -6 to 6
- key_states: bfloat16 [16384, 1024], P('seq', 'head'), may hold values from -6 to 6
- value_states: bfloat16 [16384, 1024], P('seq', 'head'), may hold values from -6 to 6
- block_picks: int32 [32, 8, 2], replicated, may hold values from 1 to 31, as said below
- grad_output: bfloat16 [16384, 8192], P('seq', 'head'), may hold values from -6 to 6
Outputs:
- attn_output: bfloat16 [16384, 8192], P('seq', 'head')
- grad_queries: float32 [16384, 8192], P('seq', 'head')
- grad_keys: float32 [16384, 1024], P('seq', 'head')
- grad_values: float32 [16384, 1024], P('seq', 'head')
Inputs may be any that keep to these rules, and one draw needn't show every extreme that they name: `block_picks`: for query block b and KV head g the offsets differ from each other and lie in 1 to max(b, 2).
All inputs are finite; a program needn't handle non-finite values.
Results may differ from a plain program's by a relative error of at most 0.0095.
Values may be sent and summed in bfloat16 or wider, within the bound.
No kernel may reach another device: no remote copies, remote signals or barrier semaphores. Data moves between devices by JAX's collectives and lax.ppermute only.
A program may use at most 32 MiB of HBM per device.

v0:
```python
import jax
import jax.numpy as jnp
from jax import lax
from jax.sharding import PartitionSpec as P

BLOCK = 512


NEGATIVE = -1e30


def partner(shard, axis, apart):
    return lax.ppermute(shard, axis, [(i, i ^ 1 << apart) for i in range(lax.axis_size(axis))])


def columns(block_data, which_half, count):
    return lax.dynamic_slice_in_dim(block_data, which_half * count, count, block_data.ndim - 1)


def ordered(own_part, other_part, pair_half):
    return jnp.where(
        pair_half == 0,
        jnp.concatenate([own_part, other_part], -1),
        jnp.concatenate([other_part, own_part], -1),
    )


def local(queries, key_states, value_states, block_picks, grad_output):
    row_count = queries.shape[0]
    half_dim = key_states.shape[1]
    head_dim = 2 * half_dim
    local_heads = queries.shape[1] // head_dim
    seq_count = lax.axis_size("seq")
    seq_index = lax.axis_index("seq")
    pair_half = lax.axis_index("head") % 2
    kv_group = lax.axis_index("head") // 2
    num_blocks = block_picks.shape[0]
    stripe_rows = BLOCK // seq_count
    query_rows = min(row_count, BLOCK)
    query_blocks = row_count // query_rows
    chosen = block_picks.shape[2] + 1
    key_count = chosen * BLOCK
    scaling = head_dim ** (-0.5)
    group_picks = lax.dynamic_index_in_dim(block_picks, kv_group, 1, keepdims=False)
    block_starts = (jnp.arange(seq_count, dtype=jnp.int32) * row_count // BLOCK)[
        :, None
    ] + jnp.arange(query_blocks, dtype=jnp.int32)[None, :]
    wanted = jnp.concatenate(
        [
            block_starts[..., None],
            block_starts[..., None] - jnp.take(group_picks, block_starts, axis=0),
        ],
        -1,
    )
    own_ids = lax.dynamic_index_in_dim(wanted, seq_index, 0, keepdims=False)
    usable = own_ids >= 0
    block_ids = jnp.maximum(wanted, 0).reshape(-1)
    paired = partner(jnp.concatenate([key_states, value_states], 1), "head", 0)
    local_kv = jnp.concatenate(
        [
            ordered(key_states, paired[:, :half_dim], pair_half),
            ordered(value_states, paired[:, half_dim:], pair_half),
        ],
        1,
    )
    col_width = local_kv.shape[1]
    spread = local_kv.reshape(row_count // seq_count, seq_count, col_width)
    banded = lax.all_to_all(spread, "seq", split_axis=1, concat_axis=0, tiled=True).reshape(
        num_blocks, stripe_rows, col_width
    )
    outgoing = jnp.take(banded, block_ids, axis=0).reshape(
        seq_count, query_blocks * chosen, stripe_rows, col_width
    )
    arrived = lax.all_to_all(outgoing, "seq", split_axis=0, concat_axis=0, tiled=True)
    fetched = arrived.transpose(1, 2, 0, 3).reshape(query_blocks, key_count, col_width)
    key_tiles = fetched[..., :head_dim]
    value_tiles = fetched[..., head_dim:]
    q_blocks = queries.reshape(query_blocks, query_rows, local_heads, head_dim)
    g_blocks = grad_output.reshape(query_blocks, query_rows, local_heads, head_dim)
    slot_index = jnp.arange(key_count, dtype=jnp.int32) // BLOCK
    key_place = jnp.arange(key_count, dtype=jnp.int32) % BLOCK
    query_place = (
        (seq_index * row_count + jnp.arange(row_count, dtype=jnp.int32)) % BLOCK
    ).reshape(query_blocks, query_rows)
    allowed = usable[:, slot_index][:, None, :] & (
        (slot_index > 0)[None, None, :] | (key_place[None, None, :] <= query_place[:, :, None])
    )
    scores = (
        jnp.einsum("nrhd,nkd->nhrk", q_blocks, key_tiles, preferred_element_type=jnp.float32)
        * scaling
    )
    scores = jnp.where(allowed[:, None], scores, NEGATIVE)
    row_max = jnp.max(scores, axis=-1, keepdims=True)
    weights = jnp.exp(scores - row_max)
    probs = weights / jnp.sum(weights, axis=-1, keepdims=True)
    probs_low = probs.astype(jnp.bfloat16)
    attended = jnp.einsum(
        "nhrk,nkd->nrhd", probs_low, value_tiles, preferred_element_type=jnp.float32
    )
    attn_output = attended.astype(jnp.bfloat16).reshape(row_count, -1)
    row_delta = jnp.sum(g_blocks.astype(jnp.float32) * attended, axis=-1)
    grad_prob = jnp.einsum(
        "nrhd,nkd->nhrk", g_blocks, value_tiles, preferred_element_type=jnp.float32
    )
    dscore = (probs * (grad_prob - jnp.transpose(row_delta, (0, 2, 1))[..., None])).astype(
        jnp.bfloat16
    )
    grad_queries = (
        jnp.einsum("nhrk,nkd->nrhd", dscore, key_tiles, preferred_element_type=jnp.float32)
        * scaling
    ).reshape(row_count, -1)
    grad_k = (
        jnp.einsum("nhrk,nrhd->nkd", dscore, q_blocks, preferred_element_type=jnp.float32) * scaling
    )
    grad_v = jnp.einsum("nhrk,nrhd->nkd", probs_low, g_blocks, preferred_element_type=jnp.float32)
    returned = jnp.concatenate([grad_k, grad_v], -1)
    ret_width = returned.shape[-1]
    going_out = returned.reshape(
        query_blocks * chosen, stripe_rows, seq_count, ret_width
    ).transpose(2, 0, 1, 3)
    landed = lax.all_to_all(going_out, "seq", split_axis=0, concat_axis=0, tiled=True)
    member = (block_ids[:, None] == jnp.arange(num_blocks, dtype=jnp.int32)[None, :]).astype(
        jnp.float32
    )
    summed = jnp.dot(
        member.T,
        landed.reshape(-1, stripe_rows * ret_width),
        precision=lax.Precision.HIGHEST,
        preferred_element_type=jnp.float32,
    )
    back_rows = summed.reshape(seq_count, row_count // seq_count, 1, ret_width)
    owned_rows = lax.all_to_all(back_rows, "seq", split_axis=0, concat_axis=2, tiled=True).reshape(
        row_count, ret_width
    )
    sent_back = jnp.concatenate(
        [
            columns(owned_rows[:, :head_dim], 1 - pair_half, half_dim),
            columns(owned_rows[:, head_dim:], 1 - pair_half, half_dim),
        ],
        -1,
    )
    partner_sum = partner(sent_back.astype(jnp.bfloat16), "head", 0).astype(sent_back.dtype)
    kept_cols = (
        jnp.concatenate(
            [
                columns(owned_rows[:, :head_dim], pair_half, half_dim),
                columns(owned_rows[:, head_dim:], pair_half, half_dim),
            ],
            -1,
        )
        + partner_sum
    )
    return (attn_output, grad_queries, kept_cols[:, :half_dim], kept_cols[:, half_dim:])


def solution(mesh):
    return jax.shard_map(
        local,
        mesh=mesh,
        in_specs=(P("seq", "head"), P("seq", "head"), P("seq", "head"), P(), P("seq", "head")),
        out_specs=(P("seq", "head"), P("seq", "head"), P("seq", "head"), P("seq", "head")),
        check_vma=False,
    )
```

profile of v0, /device:TPU:6, one launch (start us, length us, event | category | flops | bytes accessed | tf_op | source)
XLA Modules:
  0.0 398.3 jit_solution(16589600597128409764)
XLA Ops:
  0.7 0.8 pad_maximum_fusion.1
  1.5 3.5 collective-permute-start
  5.0 0.9 concatenate.50
  5.9 0.9 concatenate.55
  6.7 0.1 copy.56
  6.9 0.1 copy.60
  7.0 0.7 fusion.32
  7.8 0.1 copy.57
  8.0 0.1 copy.61
  8.2 0.4 maximum_select_fusion
  8.5 0.7 pad_maximum_fusion
  9.2 29.4 %all-to-all-start = ((bf16[4,64,256]{2,0,1:T(4,128)(2,1)}), bf16[4,64,256]{2,0,1:T(4,128)(2,1)S(1)}, u32[]{:S(2)}, u32[]{:S(2)}) async-start(bf16[4,64,256]{2,0,1:T(4,128)(2,1)} %pad_maximum_fusion), calls=%async_computation | async-start | bytes 262144 | tf_op jit(solution)/shard_map/all_to_all | solution.py:68
  38.7 0.6 gather_fusion
  39.6 0.1 reshape.522
  39.7 0.1 copy.55
  39.8 30.3 %all-to-all-done = bf16[4,64,256]{2,0,1:T(4,128)(2,1)S(1)} async-done(((bf16[4,64,256]{2,0,1:T(4,128)(2,1)}), bf16[4,64,256]{2,0,1:T(4,128)(2,1)S(1)}, u32[]{:S(2)}, u32[]{:S(2)}) %all-to-all-start) | async-done | bytes 131104 | tf_op jit(solution)/shard_map/all_to_all | solution.py:68
  70.2 0.8 gather_fusion.1
  71.0 1.2 broadcast_select_fusion
  72.2 4.8 %all-to-all-start.1 = ((bf16[64,3,8,256]{3,2,1,0:T(8,128)(2,1)}), bf16[64,3,8,256]{3,2,1,0:T(8,128)(2,1)S(1)}, u32[]{:S(2)}, u32[]{:S(2)}) async-start(bf16[64,3,8,256]{3,2,1,0:T(8,128)(2,1)} %broadcast_select_fusion), calls=%async_computation.1 | async-start | bytes 1572864 | tf_op jit(solution)/shard_map/all_to_all | solution.py:74
  77.0 0.1 copy.70
  77.2 0.8 reshape.505
  78.0 0.5 fusion.39
  78.5 2.0 select_reduce_fusion
  80.5 1.4 or_and_fusion
  82.0 83.1 %all-to-all-done.1 = bf16[64,3,8,256]{3,2,1,0:T(8,128)(2,1)S(1)} async-done(((bf16[64,3,8,256]{3,2,1,0:T(8,128)(2,1)}), bf16[64,3,8,256]{3,2,1,0:T(8,128)(2,1)S(1)}, u32[]{:S(2)}, u32[]{:S(2)}) %all-to-all-start.1) | async-done | bytes 786464 | tf_op jit(solution)/shard_map/all_to_all | solution.py:74
  165.0 0.2 copy.65
  165.2 1.1 fusion.4
  166.4 1.4 fusion.3
  167.8 1.6 fusion.8
  169.4 1.3 multiply_reduce_fusion
  170.7 3.3 fusion.5
  174.0 1.0 fusion.18
  175.1 1.0 fusion.9
  176.2 0.9 copy.77
  177.1 159.5 %all_to_all.40 = f32[64,3,8,256]{3,2,1,0:T(8,128)S(1)} all-to-all(f32[64,3,8,256]{3,2,1,0:T(8,128)S(1)} %copy.77), channel_id=1, replica_groups=mesh['seq'=64,'head'=16] {'seq'}, dimensions={0} | all-to-all | bytes 3145728 | tf_op jit(solution)/shard_map/all_to_all | solution.py:121
  336.6 0.6 copy.97
  337.2 1.5 fusion.22
  338.7 1.8 reshape.509
  340.5 5.5 %all-to-all-start.3 = ((f32[64,4,1,256]{3,1,2,0:T(4,128)}), f32[64,4,1,256]{3,1,2,0:T(4,128)}, u32[]{:S(2)}, u32[]{:S(2)}) async-start(f32[64,4,1,256]{3,1,2,0:T(4,128)} %bitcast.161), calls=%async_computation.3 | async-start | bytes 524288 | tf_op jit(solution)/shard_map/all_to_all | solution.py:132
  346.0 1.8 copy.80
  347.8 2.4 convolution_multiply_fusion
  350.2 2.0 copy.81
  352.2 36.8 %all-to-all-done.3 = f32[64,4,1,256]{3,1,2,0:T(4,128)} async-done(((f32[64,4,1,256]{3,1,2,0:T(4,128)}), f32[64,4,1,256]{3,1,2,0:T(4,128)}, u32[]{:S(2)}, u32[]{:S(2)}) %all-to-all-start.3) | async-done | bytes 262176 | tf_op jit(solution)/shard_map/all_to_all | solution.py:132
  389.0 1.0 copy.79
  390.5 3.4 collective-permute-start.1
  394.0 2.6 collective-permute-done.1
  396.8 0.7 copy.82
  397.6 0.7 copy.83
  (43 shorter events, 1.6 us)
Async XLA Ops:
  0.6 164.6 %copy-start = (bf16[256,512]{1,0:T(8,128)(2,1)S(1)}, bf16[256,512]{1,0:T(8,128)(2,1)}, u32[]{:S(2)}) copy-start(bf16[256,512]{1,0:T(8,128)(2,1)} %param.5) | copy-start | bytes 786436
  0.6 76.4 %copy-start.3 = (bf16[256,512]{1,0:T(8,128)(2,1)S(1)}, bf16[256,512]{1,0:T(8,128)(2,1)}, u32[]{:S(2)}) copy-start(bf16[256,512]{1,0:T(8,128)(2,1)} %param.9) | copy-start | bytes 786436
  1.5 6.2 %collective-permute-start = (bf16[256,128]{0,1:T(8,128)(2,1)S(1)}, bf16[256,128]{0,1:T(8,128)(2,1)S(1)}, u32[]{:S(2)}, u32[]{:S(2)}) collective-permute-start(bf16[256,128]{0,1:T(8,128)(2,1)S(1)} %pad_maximum_fusion.1), channel_id=1, source_target_pairs={{0,1},{1,0},{2,3},{3,2},{4,5},{5,4},{6,7},{7,6},{8,9},{9,8},{10,11... | collective-permute-start | bytes 196616 | tf_op jit(solution)/shard_map/ppermute | solution.py:13
  9.2 61.0 %all-to-all-start = ((bf16[4,64,256]{2,0,1:T(4,128)(2,1)}), bf16[4,64,256]{2,0,1:T(4,128)(2,1)S(1)}, u32[]{:S(2)}, u32[]{:S(2)}) async-start(bf16[4,64,256]{2,0,1:T(4,128)(2,1)} %pad_maximum_fusion), calls=%async_computation | async-start | bytes 262144 | tf_op jit(solution)/shard_map/all_to_all | solution.py:68
  72.2 92.9 %all-to-all-start.1 = ((bf16[64,3,8,256]{3,2,1,0:T(8,128)(2,1)}), bf16[64,3,8,256]{3,2,1,0:T(8,128)(2,1)S(1)}, u32[]{:S(2)}, u32[]{:S(2)}) async-start(bf16[64,3,8,256]{3,2,1,0:T(8,128)(2,1)} %broadcast_select_fusion), calls=%async_computation.1 | async-start | bytes 1572864 | tf_op jit(solution)/shard_map/all_to_all | solution.py:74
  81.9 85.8 %copy-start.1 = (pred[256,1536]{0,1:T(8,128)(4,1)}, pred[256,1536]{0,1:T(8,128)(4,1)S(1)}, u32[]{:S(2)}) copy-start(pred[256,1536]{0,1:T(8,128)(4,1)S(1)} %or_and_fusion) | copy-start | bytes 1179652
  165.2 5.5 %copy-start.2 = (bf16[3,8,64,256]{3,2,1,0:T(8,128)(2,1)}, bf16[3,8,64,256]{3,2,1,0:T(8,128)(2,1)S(1)}, u32[]{:S(2)}) copy-start(bf16[3,8,64,256]{3,2,1,0:T(8,128)(2,1)S(1)} %copy.65) | copy-start | bytes 2359300
  167.7 3.0 copy-start.4
  170.7 3.3 copy-start.5
  340.5 48.6 %all-to-all-start.3 = ((f32[64,4,1,256]{3,1,2,0:T(4,128)}), f32[64,4,1,256]{3,1,2,0:T(4,128)}, u32[]{:S(2)}, u32[]{:S(2)}) async-start(f32[64,4,1,256]{3,1,2,0:T(4,128)} %bitcast.161), calls=%async_computation.3 | async-start | bytes 524288 | tf_op jit(solution)/shard_map/all_to_all | solution.py:132
  390.5 6.2 %collective-permute-start.1 = (bf16[256,128]{1,0:T(8,128)(2,1)S(1)}, bf16[256,128]{1,0:T(8,128)(2,1)S(1)}, u32[]{:S(2)}, u32[]{:S(2)}) collective-permute-start(bf16[256,128]{1,0:T(8,128)(2,1)S(1)} %pad_maximum_fusion.2), channel_id=1, source_target_pairs={{0,1},{1,0},{2,3},{3,2},{4,5},{5,4},{6,7},{7,6},{8,9},{9,8},{10,11... | collective-permute-start | bytes 196616 | tf_op jit(solution)/shard_map/ppermute | solution.py:13
where the time goes:
time: 399 us; the launch traced here: 398 us
  blocking collectives  159 us (40%)
  waiting for transfers between devices  153 us (38%)
  starting transfers between devices  46.5 us (12%)
  local copies, waits for them, and re-layouts  16.8 us (4%)
  matrix products  11.6 us (3%)
  other arithmetic  9.92 us (2%)
    all_to_all x1, blocking collectives, local(): lax.all_to_all(going_out, 'seq', split_axis=0, concat_axis=0, tiled=True)  159 us
    all_to_all x1, waiting for transfers between devices, local(): lax.all_to_all(outgoing, 'seq', split_axis=0, concat_axis=0, tiled=True)  83.1 us
    all_to_all x1, waiting for transfers between devices, local(): lax.all_to_all(back_rows, 'seq', split_axis=0, concat_axis=2, tiled=True)  36.8 us
    all_to_all x1, waiting for transfers between devices, local(): lax.all_to_all(spread, 'seq', split_axis=1, concat_axis=0, tiled=True)  30.3 us
    all_to_all x1, starting transfers between devices, local(): lax.all_to_all(spread, 'seq', split_axis=1, concat_axis=0, tiled=True)  29.4 us
  transfers between devices with their start and end apart: 5, of which 4 were waited for; matrix products, arithmetic and copies ran while one was open for 4% of the time, Pallas kernels for 0%

commit v1 on v0

v1 whole, which is shorter than its diff:
```python
import jax
import jax.numpy as jnp
from jax import lax
from jax.sharding import Mesh, PartitionSpec as P

BLOCK = 512
NEGATIVE = -1e30
SWAP = [(0, 1), (1, 0)]


def ordered(own_part, other_part, pair):
    return jnp.where(
        pair == 0,
        jnp.concatenate([own_part, other_part], -1),
        jnp.concatenate([other_part, own_part], -1),
    )


def full_features(own, pair):
    other = lax.ppermute(own, "pair", SWAP)
    half = own.shape[-1] // 2
    return jnp.concatenate(
        [
            ordered(own[..., :half], other[..., :half], pair),
            ordered(own[..., half:], other[..., half:], pair),
        ],
        -1,
    )


def local(queries, key_states, value_states, block_picks, grad_output):
    row_count = queries.shape[0]
    half_dim = key_states.shape[1]
    head_dim = 2 * half_dim
    local_heads = queries.shape[1] // head_dim
    z_count = lax.axis_size("z")
    z_index = lax.axis_index("z")
    core = lax.axis_index("core")
    pair = lax.axis_index("pair")
    num_blocks, _, picked = block_picks.shape
    stripe = row_count // z_count
    scaling = head_dim ** (-0.5)
    group_picks = lax.dynamic_index_in_dim(block_picks, lax.axis_index("grp"), 1, keepdims=False)
    wanted = jnp.arange(num_blocks, dtype=jnp.int32)[:, None] - group_picks
    usable = lax.dynamic_index_in_dim(wanted, z_index, 0, keepdims=False) >= 0
    block_ids = jnp.maximum(wanted, 0).reshape(-1)

    own = jnp.concatenate([key_states, value_states], 1)
    banded = lax.all_to_all(
        own.reshape(z_count, stripe, head_dim), "z", split_axis=0, concat_axis=0, tiled=True
    )
    own_full = full_features(own, pair)
    own_pair = jnp.concatenate([own_full, lax.ppermute(own_full, "core", SWAP)], 0)

    outgoing = jnp.take(banded, block_ids, axis=0).reshape(z_count, picked * stripe, head_dim)
    arrived = lax.all_to_all(outgoing, "z", split_axis=0, concat_axis=0, tiled=True)
    fetched = (
        arrived.reshape(z_count, picked, stripe, head_dim)
        .transpose(1, 0, 2, 3)
        .reshape(picked, row_count, head_dim)
    )
    fetched = full_features(fetched, pair)
    fetched = jnp.concatenate([fetched, lax.ppermute(fetched, "core", SWAP)], 1)
    tiles = jnp.concatenate([own_pair[None], fetched], 0).reshape(-1, 2 * head_dim)
    key_tiles = tiles[:, :head_dim]
    value_tiles = tiles[:, head_dim:]
    key_count = tiles.shape[0]

    q_rows = queries.reshape(row_count, local_heads, head_dim)
    g_rows = grad_output.reshape(row_count, local_heads, head_dim)
    spot = jnp.arange(key_count, dtype=jnp.int32)
    place = spot % BLOCK
    key_place = jnp.where(place < row_count, core, 1 - core) * row_count + place % row_count
    query_place = core * row_count + jnp.arange(row_count, dtype=jnp.int32)
    slot_usable = jnp.concatenate([jnp.ones((1,), bool), usable])[spot // BLOCK]
    allowed = slot_usable[None, :] & (
        (spot >= BLOCK)[None, :] | (key_place[None, :] <= query_place[:, None])
    )
    scores = (
        jnp.einsum("rhd,kd->hrk", q_rows, key_tiles, preferred_element_type=jnp.float32) * scaling
    )
    scores = jnp.where(allowed[None], scores, NEGATIVE)
    row_max = jnp.max(scores, axis=-1, keepdims=True)
    weights = jnp.exp(scores - row_max)
    probs = weights / jnp.sum(weights, axis=-1, keepdims=True)
    probs_low = probs.astype(jnp.bfloat16)
    attended = jnp.einsum(
        "hrk,kd->rhd", probs_low, value_tiles, preferred_element_type=jnp.float32
    )
    attn_output = attended.astype(jnp.bfloat16).reshape(row_count, -1)
    row_delta = jnp.sum(g_rows.astype(jnp.float32) * attended, axis=-1)
    grad_prob = jnp.einsum("rhd,kd->hrk", g_rows, value_tiles, preferred_element_type=jnp.float32)
    dscore = (probs * (grad_prob - jnp.transpose(row_delta)[..., None])).astype(jnp.bfloat16)
    grad_queries = (
        jnp.einsum("hrk,kd->rhd", dscore, key_tiles, preferred_element_type=jnp.float32) * scaling
    ).reshape(row_count, -1)
    grad_k = jnp.einsum("hrk,rhd->kd", dscore, q_rows, preferred_element_type=jnp.float32) * scaling
    grad_v = jnp.einsum("hrk,rhd->kd", probs_low, g_rows, preferred_element_type=jnp.float32)

    grads = jnp.concatenate([grad_k, grad_v], -1).reshape(-1, 2, row_count, 2 * head_dim)
    from_core = lax.ppermute(grads[:, 1].astype(jnp.bfloat16), "core", SWAP)
    grads = grads[:, 0] + from_core.astype(jnp.float32)
    quarters = grads.reshape(-1, row_count, 4, half_dim)
    low = jnp.concatenate([quarters[:, :, 0], quarters[:, :, 2]], -1)
    high = jnp.concatenate([quarters[:, :, 1], quarters[:, :, 3]], -1)
    mine = jnp.where(pair == 0, low, high)
    theirs = jnp.where(pair == 0, high, low).astype(jnp.bfloat16)
    mine = mine + lax.ppermute(theirs, "pair", SWAP).astype(jnp.float32)

    going_out = (
        mine[1:]
        .astype(jnp.bfloat16)
        .reshape(picked, z_count, stripe, head_dim)
        .transpose(1, 0, 2, 3)
        .reshape(z_count, picked * stripe, head_dim)
    )
    landed = lax.all_to_all(going_out, "z", split_axis=0, concat_axis=0, tiled=True)
    member = (
        block_ids[None, :] == jnp.arange(num_blocks, dtype=jnp.int32)[:, None]
    ).astype(jnp.bfloat16)
    summed = jnp.dot(
        member,
        landed.reshape(z_count * picked, stripe * head_dim),
        preferred_element_type=jnp.float32,
    )
    back = summed.astype(jnp.bfloat16).reshape(z_count, stripe, head_dim)
    back = lax.all_to_all(back, "z", split_axis=0, concat_axis=0, tiled=True)
    total = mine[0] + back.reshape(row_count, head_dim).astype(jnp.float32)
    return attn_output, grad_queries, total[:, :half_dim], total[:, half_dim:]


def solution(mesh):
    seq, heads = mesh.devices.shape
    split = Mesh(
        mesh.devices.reshape(seq // 2, 2, heads // 2, 2), ("z", "core", "grp", "pair")
    )
    spec = P(("z", "core"), ("grp", "pair"))
    return jax.shard_map(
        local,
        mesh=split,
        in_specs=(spec, spec, spec, P(), spec),
        out_specs=(spec, spec, spec, spec),
        check_vma=False,
    )
```

time: 399 us -> 224 us (0.56)
  blocking collectives: 159 us -> 0 us
  waiting for transfers between devices: 153 us -> 102 us
  local copies, waits for them, and re-layouts: 16.8 us -> 33.8 us
  starting transfers between devices: 46.5 us -> 58.6 us
  other arithmetic: 9.92 us -> 14.3 us
    all_to_all x1 -> x0, blocking collectives: 159 us -> none  [local(): lax.all_to_all(going_out, 'seq', split_axis=0, concat_axis=0, tiled=True)]
    all_to_all x3 -> x4, waiting for transfers between devices: 150 us -> 93.7 us  [the longest x1 29 us: local(): lax.all_to_all(going_out, 'z', split_axis=0, concat_axis=0, tiled=True)]
    ppermute x2 -> x6, starting transfers between devices: 6.91 us -> 16.9 us  [the longest x2 6.97 us: full_features(): other = lax.ppermute(own, 'pair', SWAP)]
    slice x3 -> x8, local copies, waits for them, and re-layouts: 0.12 us -> 9.23 us  [the longest x1 3.1 us: local(): from_core = lax.ppermute(grads[:, 1].astype(jnp.bfloat16), 'core', SWAP)]
    ppermute x2 -> x6, waiting for transfers between devices: 2.62 us -> 8.48 us  [the longest x1 5.21 us: local(): mine = mine + lax.ppermute(theirs, 'pair', SWAP).astype(jnp.float32)]
    unnamed x17 -> x24, local copies, waits for them, and re-layouts: 5.91 us -> 11.7 us
    sub x0 -> x1, matrix products: none -> 4.87 us  [local(): weights = jnp.exp(scores - row_max)]
    reshape x2 -> x5, local copies, waits for them, and re-layouts: 1.86 us -> 6.42 us  [the longest x1 3.08 us: local(): jnp.concatenate([grad_k, grad_v], -1)]
  transfers between devices with their start and end apart: 5 -> 10, of which waited for: 4 -> 6; matrix products, arithmetic and copies ran while one was open for 4% -> 9% of each run, Pallas kernels for 0% -> 0%
where the time goes in v1:
time: 224 us; the launch traced here: 223 us
  waiting for transfers between devices  102 us (46%)
  starting transfers between devices  58.6 us (26%)
  local copies, waits for them, and re-layouts  33.8 us (15%)
  other arithmetic  14.3 us (6%)
  matrix products  12.9 us (6%)
    all_to_all x1, waiting for transfers between devices, local(): lax.all_to_all(going_out, 'z', split_axis=0, concat_axis=0, tiled=True)  29 us
    all_to_all x1, starting transfers between devices, local(): lax.all_to_all(own.reshape(z_count, stripe, head_dim), 'z', split_axis=0,...  28.7 us
    all_to_all x1, waiting for transfers between devices, local(): lax.all_to_all(outgoing, 'z', split_axis=0, concat_axis=0, tiled=True)  25.4 us
    all_to_all x1, waiting for transfers between devices, local(): lax.all_to_all(own.reshape(z_count, stripe, head_dim), 'z', split_axis=0,...  21 us
    all_to_all x1, waiting for transfers between devices, local(): back = lax.all_to_all(back, 'z', split_axis=0, concat_axis=0, tiled=True)  18.3 us
    unnamed x24, local copies, waits for them, and re-layouts  11.7 us
    ppermute x2, starting transfers between devices, full_features(): other = lax.ppermute(own, 'pair', SWAP)  6.97 us
    ppermute x1, waiting for transfers between devices, local(): mine = mine + lax.ppermute(theirs, 'pair', SWAP).astype(jnp.float32)  5.21 us
  transfers between devices with their start and end apart: 10, of which 6 were waited for; matrix products, arithmetic and copies ran while one was open for 9% of the time, Pallas kernels for 0%

profile of v1, /device:TPU:6, one launch (start us, length us, event | category | flops | bytes accessed | tf_op | source)
XLA Modules:
  0.0 222.9 jit_solution(8532026487649826217)
XLA Ops:
  0.7 0.9 copy.59
  1.6 0.9 copy.58
  2.5 0.7 fusion.38
  3.2 28.7 %all-to-all-start = ((bf16[32,8,128]{2,1,0:T(8,128)(2,1)}), bf16[32,8,128]{2,1,0:T(8,128)(2,1)S(1)}, u32[]{:S(2)}, u32[]{:S(2)}) async-start(bf16[32,8,128]{2,1,0:T(8,128)(2,1)} %fusion.38), calls=%async_computation | async-start | bytes 131072 | tf_op jit(solution)/shard_map/all_to_all | solution.py:49
  32.0 3.5 %collective-permute-start = (bf16[256,128]{1,0:T(8,128)(2,1)S(1)}, bf16[256,128]{1,0:T(8,128)(2,1)S(1)}, u32[]{:S(2)}, u32[]{:S(2)}) collective-permute-start(bf16[256,128]{1,0:T(8,128)(2,1)S(1)} %pad_maximum_fusion.5), channel_id=1, source_target_pairs={{0,1},{1,0},{2,3},{3,2},{4,5},{5,4},{6,7},{7,6},{8,9},{9,8},{10,11... | collective-permute-start | bytes 196616 | tf_op jit(solution)/shard_map/ppermute | solution.py:20
  35.5 0.7 maximum_compare_fusion
  36.7 21.0 %all-to-all-done = bf16[32,8,128]{2,1,0:T(8,128)(2,1)S(1)} async-done(((bf16[32,8,128]{2,1,0:T(8,128)(2,1)}), bf16[32,8,128]{2,1,0:T(8,128)(2,1)S(1)}, u32[]{:S(2)}, u32[]{:S(2)}) %all-to-all-start) | async-done | bytes 65568 | tf_op jit(solution)/shard_map/all_to_all | solution.py:49
  58.3 0.8 bitcast_select_fusion.2
  59.1 3.9 %all-to-all-start.1 = ((bf16[32,16,128]{2,1,0:T(8,128)(2,1)}), bf16[32,16,128]{2,1,0:T(8,128)(2,1)S(1)}, u32[]{:S(2)}, u32[]{:S(2)}) async-start(bf16[32,16,128]{2,1,0:T(8,128)(2,1)} %bitcast_select_fusion.2), calls=%async_computation.1 | async-start | bytes 262144 | tf_op jit(solution)/shard_map/all_to_all | solution.py:56
  63.6 1.3 select_reduce_fusion
  65.3 1.9 collective-permute-start.1
  67.2 25.4 %all-to-all-done.1 = bf16[32,16,128]{2,1,0:T(8,128)(2,1)S(1)} async-done(((bf16[32,16,128]{2,1,0:T(8,128)(2,1)}), bf16[32,16,128]{2,1,0:T(8,128)(2,1)S(1)}, u32[]{:S(2)}, u32[]{:S(2)}) %all-to-all-start.1) | async-done | bytes 131104 | tf_op jit(solution)/shard_map/all_to_all | solution.py:56
  92.6 3.5 %collective-permute-start.2 = (bf16[2,256,128]{2,1,0:T(8,128)(2,1)S(1)}, bf16[2,256,128]{2,1,0:T(8,128)(2,1)S(1)}, u32[]{:S(2)}, u32[]{:S(2)}) collective-permute-start(bf16[2,256,128]{2,1,0:T(8,128)(2,1)S(1)} %copy_bitcast_fusion.1), channel_id=1, source_target_pairs={{0,1},{1,0},{2,3},{3,2},{4,5},{5,4},{6,7},{7,6},{8,9},{9,8},{10,11... | collective-permute-start | bytes 393224 | tf_op jit(solution)/shard_map/ppermute | solution.py:20
  96.2 3.3 %collective-permute-done.2 = bf16[2,256,128]{2,1,0:T(8,128)(2,1)S(1)} collective-permute-done((bf16[2,256,128]{2,1,0:T(8,128)(2,1)S(1)}, bf16[2,256,128]{2,1,0:T(8,128)(2,1)S(1)}, u32[]{:S(2)}, u32[]{:S(2)}) %collective-permute-start.2) | collective-permute-done | bytes 131104 | tf_op jit(solution)/shard_map/ppermute | solution.py:20
  99.9 1.9 collective-permute-start.3
  101.9 1.4 or_and_fusion
  103.7 4.9 %fusion.28 = (f32[4,256]{1,0:T(4,128)S(1)}, f32[4,256,1536]{1,2,0:T(8,128)}) fusion(pred[256,1536]{0,1:T(8,128)(4,1)S(1)} %or_and_fusion, bf16[256,4,128]{0,2,1:T(8,128)(2,1)S(1)} %bitcast.135, bf16[1536,256]{1,0:T(8,128)(2,1)S(1)} %bitcast.127), kind=kOutput, calls=%fused_computation.89 | convolution fusion | flops 408946176 | bytes 7344128 | tf_op jit(solution)/shard_map/sub | solution.py:84
  108.6 3.5 %fusion.7 = bf16[4,256,1536]{1,2,0:T(8,128)(2,1)S(1)} fusion(f32[4,256,1536]{1,2,0:T(8,128)} %get-tuple-element.35, f32[4,256]{1,0:T(4,128)S(1)} %get-tuple-element.34), kind=kLoop, calls=%fused_computation.12 | loop fusion | flops 3145728 | bytes 9441280 | tf_op jit(solution)/shard_map/convert_element_type | solution.py:86
  112.1 1.3 multiply_reduce_fusion
  113.4 1.1 convolution_bitcast_fusion
  114.7 1.0 fusion.2
  115.7 1.1 fusion.8
  116.8 1.2 pad_maximum_fusion
  118.1 3.1 %reshape.249 = f32[3,2,256,256]{2,1,0,3:T(2,128)} reshape(f32[1536,256]{0,1:T(8,128)} %pad_maximum_fusion) | data formatting | bytes 3145728 | tf_op jit(solution)/shard_map/reshape | solution.py:100
  121.2 3.1 %slice.93 = bf16[3,1,256,256]{2,1,0,3:T(2,128)(2,1)} slice(f32[3,2,256,256]{2,1,0,3:T(2,128)} %reshape.249), slice={[0:3], [1:2], [0:256], [0:256]} | slice | bytes 786432 | tf_op jit(solution)/shard_map/slice | solution.py:101
  124.3 2.2 copy.102
  126.4 2.6 %collective-permute-start.4 = (bf16[3,256,256]{2,1,0:T(8,128)(2,1)S(1)}, bf16[3,256,256]{2,1,0:T(8,128)(2,1)}, u32[]{:S(2)}, u32[]{:S(2)}) collective-permute-start(bf16[3,256,256]{2,1,0:T(8,128)(2,1)S(1)} %bitcast.138), channel_id=1, source_target_pairs={{0,16},{16,0},{1,17},{17,1},{2,18},{18,2},{3,19},{19,3},{4,20},{20... | collective-permute-start | bytes 1179656 | tf_op jit(solution)/shard_map/ppermute | solution.py:101
  129.0 2.8 %slice.92 = f32[3,1,256,256]{2,1,0,3:T(1,128)} slice(f32[3,2,256,256]{2,1,0,3:T(2,128)} %reshape.249), slice={[0:3], [0:1], [0:256], [0:256]} | slice | bytes 1572864 | tf_op jit(solution)/shard_map/slice | solution.py:102
  131.9 3.0 %copy.101 = f32[3,1,256,256]{3,2,0,1:T(8,128)} copy(f32[3,1,256,256]{2,1,0,3:T(1,128)} %slice.92) | data formatting | bytes 1572864
  134.9 2.2 bitcast_add_fusion
  137.1 2.3 %copy.78 = f32[3,256,256]{1,2,0:T(8,128)} copy(f32[3,256,256]{2,1,0:T(8,128)} %bitcast_add_fusion) | data formatting | bytes 1572864 | tf_op jit(solution)/shard_map/add | solution.py:102
  139.4 1.3 slice_bitcast_fusion.13
  140.7 3.5 %collective-permute-start.5 = (bf16[3,256,128]{1,2,0:T(8,128)(2,1)S(1)}, bf16[3,256,128]{1,2,0:T(8,128)(2,1)S(1)}, u32[]{:S(2)}, u32[]{:S(2)}) collective-permute-start(bf16[3,256,128]{1,2,0:T(8,128)(2,1)S(1)} %select_convert_fusion), channel_id=1, source_target_pairs={{0,1},{1,0},{2,3},{3,2},{4,5},{5,4},{6,7},{7,6},{8,9},{9,8},{10,11... | collective-permute-start | bytes 589832 | tf_op jit(solution)/shard_map/ppermute | solution.py:108
  144.2 5.2 %collective-permute-done.5 = bf16[3,256,128]{1,2,0:T(8,128)(2,1)S(1)} collective-permute-done((bf16[3,256,128]{1,2,0:T(8,128)(2,1)S(1)}, bf16[3,256,128]{1,2,0:T(8,128)(2,1)S(1)}, u32[]{:S(2)}, u32[]{:S(2)}) %collective-permute-start.5) | collective-permute-done | bytes 196640 | tf_op jit(solution)/shard_map/ppermute | solution.py:108
  149.5 0.7 slice.120
  150.2 1.7 copy.83
  151.9 1.6 copy_bitcast_fusion
  153.4 4.6 %all-to-all-start.2 = ((bf16[32,16,128]{2,1,0:T(8,128)(2,1)}), bf16[32,16,128]{2,1,0:T(8,128)(2,1)}, u32[]{:S(2)}, u32[]{:S(2)}) async-start(bf16[32,16,128]{2,1,0:T(8,128)(2,1)} %copy_bitcast_fusion), calls=%async_computation.2 | async-start | bytes 262144 | tf_op jit(solution)/shard_map/all_to_all | solution.py:117
  159.3 0.7 subtract_maximum_fusion
  159.9 29.0 %all-to-all-done.2 = bf16[32,16,128]{2,1,0:T(8,128)(2,1)} async-done(((bf16[32,16,128]{2,1,0:T(8,128)(2,1)}), bf16[32,16,128]{2,1,0:T(8,128)(2,1)}, u32[]{:S(2)}, u32[]{:S(2)}) %all-to-all-start.2) | async-done | bytes 131104 | tf_op jit(solution)/shard_map/all_to_all | solution.py:117
  188.9 1.6 reshape.253
  190.5 1.1 fusion.9
  192.2 4.6 %all-to-all-start.3 = ((bf16[32,8,128]{2,1,0:T(8,128)(2,1)}), bf16[32,8,128]{2,1,0:T(8,128)(2,1)}, u32[]{:S(2)}, u32[]{:S(2)}) async-start(bf16[32,8,128]{2,1,0:T(8,128)(2,1)} %bitcast.139), calls=%async_computation.3 | async-start | bytes 131072 | tf_op jit(solution)/shard_map/all_to_all | solution.py:127
  196.8 2.4 %convolution_multiply_fusion = f32[128,4,256]{2,0,1:T(8,128)} fusion(bf16[4,256,1536]{1,2,0:T(8,128)(2,1)S(1)} %fusion.2, bf16[1536,256]{1,0:T(8,128)(2,1)} %bitcast.129), kind=kOutput, calls=%fused_computation.18 | convolution fusion | flops 402784256 | bytes 4063232 | tf_op jit(solution)/shard_map/hrk,kd->rhd/dot_general | solution.py:95
  199.2 2.0 copy.87
  201.2 1.8 copy.86
  203.0 18.3 %all-to-all-done.3 = bf16[32,8,128]{2,1,0:T(8,128)(2,1)} async-done(((bf16[32,8,128]{2,1,0:T(8,128)(2,1)}), bf16[32,8,128]{2,1,0:T(8,128)(2,1)}, u32[]{:S(2)}, u32[]{:S(2)}) %all-to-all-start.3) | async-done | bytes 65568 | tf_op jit(solution)/shard_map/all_to_all | solution.py:127
  221.3 0.8 bitcast_convert_fusion
  (58 shorter events, 5.8 us)
Async XLA Ops:
  0.6 102.6 %copy-start.4 = (bf16[256,512]{1,0:T(8,128)(2,1)S(1)}, bf16[256,512]{1,0:T(8,128)(2,1)}, u32[]{:S(2)}) copy-start(bf16[256,512]{1,0:T(8,128)(2,1)} %param.9) | copy-start | bytes 786436
  0.6 102.8 %copy-start.5 = (bf16[256,512]{1,0:T(8,128)(2,1)S(1)}, bf16[256,512]{1,0:T(8,128)(2,1)}, u32[]{:S(2)}) copy-start(bf16[256,512]{1,0:T(8,128)(2,1)} %param.5) | copy-start | bytes 786436
  3.2 54.5 %all-to-all-start = ((bf16[32,8,128]{2,1,0:T(8,128)(2,1)}), bf16[32,8,128]{2,1,0:T(8,128)(2,1)S(1)}, u32[]{:S(2)}, u32[]{:S(2)}) async-start(bf16[32,8,128]{2,1,0:T(8,128)(2,1)} %fusion.38), calls=%async_computation | async-start | bytes 131072 | tf_op jit(solution)/shard_map/all_to_all | solution.py:49
  32.0 32.9 %collective-permute-start = (bf16[256,128]{1,0:T(8,128)(2,1)S(1)}, bf16[256,128]{1,0:T(8,128)(2,1)S(1)}, u32[]{:S(2)}, u32[]{:S(2)}) collective-permute-start(bf16[256,128]{1,0:T(8,128)(2,1)S(1)} %pad_maximum_fusion.5), channel_id=1, source_target_pairs={{0,1},{1,0},{2,3},{3,2},{4,5},{5,4},{6,7},{7,6},{8,9},{9,8},{10,11... | collective-permute-start | bytes 196616 | tf_op jit(solution)/shard_map/ppermute | solution.py:20
  59.1 33.5 %all-to-all-start.1 = ((bf16[32,16,128]{2,1,0:T(8,128)(2,1)}), bf16[32,16,128]{2,1,0:T(8,128)(2,1)S(1)}, u32[]{:S(2)}, u32[]{:S(2)}) async-start(bf16[32,16,128]{2,1,0:T(8,128)(2,1)} %bitcast_select_fusion.2), calls=%async_computation.1 | async-start | bytes 262144 | tf_op jit(solution)/shard_map/all_to_all | solution.py:56
  65.3 38.3 %collective-permute-start.1 = (bf16[256,256]{1,0:T(8,128)(2,1)S(1)}, bf16[256,256]{1,0:T(8,128)(2,1)S(1)}, u32[]{:S(2)}, u32[]{:S(2)}) collective-permute-start(bf16[256,256]{1,0:T(8,128)(2,1)S(1)} %pad_maximum_fusion.4), channel_id=1, source_target_pairs={{0,16},{16,0},{1,17},{17,1},{2,18},{18,2},{3,19},{19,3},{4,20},{20... | collective-permute-start | bytes 393224 | tf_op jit(solution)/shard_map/ppermute | solution.py:53
  92.6 6.9 %collective-permute-start.2 = (bf16[2,256,128]{2,1,0:T(8,128)(2,1)S(1)}, bf16[2,256,128]{2,1,0:T(8,128)(2,1)S(1)}, u32[]{:S(2)}, u32[]{:S(2)}) collective-permute-start(bf16[2,256,128]{2,1,0:T(8,128)(2,1)S(1)} %copy_bitcast_fusion.1), channel_id=1, source_target_pairs={{0,1},{1,0},{2,3},{3,2},{4,5},{5,4},{6,7},{7,6},{8,9},{9,8},{10,11... | collective-permute-start | bytes 393224 | tf_op jit(solution)/shard_map/ppermute | solution.py:20
  99.9 3.7 %collective-permute-start.3 = (bf16[2,256,256]{2,1,0:T(8,128)(2,1)S(1)}, bf16[2,256,256]{2,1,0:T(8,128)(2,1)S(1)}, u32[]{:S(2)}, u32[]{:S(2)}) collective-permute-start(bf16[2,256,256]{2,1,0:T(8,128)(2,1)S(1)} %pad_maximum_fusion.3), channel_id=1, source_target_pairs={{0,16},{16,0},{1,17},{17,1},{2,18},{18,2},{3,19},{19,3},{4,20},{20... | collective-permute-start | bytes 786440 | tf_op jit(solution)/shard_map/ppermute | solution.py:63
  103.6 5.0 %copy-start.2 = (bf16[256,512]{0,1:T(8,128)(2,1)}, bf16[256,512]{0,1:T(8,128)(2,1)S(1)}, u32[]{:S(2)}) copy-start(bf16[256,512]{0,1:T(8,128)(2,1)S(1)} %copy.100) | copy-start | bytes 786436
  103.7 8.4 %copy-start = (bf16[3,512,256]{2,1,0:T(8,128)(2,1)}, bf16[3,512,256]{2,1,0:T(8,128)(2,1)S(1)}, u32[]{:S(2)}) copy-start(bf16[3,512,256]{2,1,0:T(8,128)(2,1)S(1)} %maximum_maximum_fusion) | copy-start | bytes 2359300
  108.6 6.0 %slice-start = ((s8[6291456]{0:T(1024)(128)(4,1)}), s8[4194304]{0:T(1024)(128)(4,1)S(1)}, s32[]{:S(2)}) async-start(s8[6291456]{0:T(1024)(128)(4,1)} %bitcast.124), calls=%async_computation.4 | async-start | bytes 8388608
  112.1 2.5 %slice-start.1 = ((s8[6291456]{0:T(1024)(128)(4,1)}), s8[2097152]{0:T(1024)(128)(4,1)S(1)}, s32[]{:S(2)}) async-start(s8[6291456]{0:T(1024)(128)(4,1)} %bitcast.124), calls=%async_computation.5 | async-start | bytes 4194304
  113.4 1.2 copy-start.1
  114.7 1.0 copy-start.3
  126.4 8.4 %collective-permute-start.4 = (bf16[3,256,256]{2,1,0:T(8,128)(2,1)S(1)}, bf16[3,256,256]{2,1,0:T(8,128)(2,1)}, u32[]{:S(2)}, u32[]{:S(2)}) collective-permute-start(bf16[3,256,256]{2,1,0:T(8,128)(2,1)S(1)} %bitcast.138), channel_id=1, source_target_pairs={{0,16},{16,0},{1,17},{17,1},{2,18},{18,2},{3,19},{19,3},{4,20},{20... | collective-permute-start | bytes 1179656 | tf_op jit(solution)/shard_map/ppermute | solution.py:101
  140.7 8.7 %collective-permute-start.5 = (bf16[3,256,128]{1,2,0:T(8,128)(2,1)S(1)}, bf16[3,256,128]{1,2,0:T(8,128)(2,1)S(1)}, u32[]{:S(2)}, u32[]{:S(2)}) collective-permute-start(bf16[3,256,128]{1,2,0:T(8,128)(2,1)S(1)} %select_convert_fusion), channel_id=1, source_target_pairs={{0,1},{1,0},{2,3},{3,2},{4,5},{5,4},{6,7},{7,6},{8,9},{9,8},{10,11... | collective-permute-start | bytes 589832 | tf_op jit(solution)/shard_map/ppermute | solution.py:108
  153.4 35.5 %all-to-all-start.2 = ((bf16[32,16,128]{2,1,0:T(8,128)(2,1)}), bf16[32,16,128]{2,1,0:T(8,128)(2,1)}, u32[]{:S(2)}, u32[]{:S(2)}) async-start(bf16[32,16,128]{2,1,0:T(8,128)(2,1)} %copy_bitcast_fusion), calls=%async_computation.2 | async-start | bytes 262144 | tf_op jit(solution)/shard_map/all_to_all | solution.py:117
  192.2 29.1 %all-to-all-start.3 = ((bf16[32,8,128]{2,1,0:T(8,128)(2,1)}), bf16[32,8,128]{2,1,0:T(8,128)(2,1)}, u32[]{:S(2)}, u32[]{:S(2)}) async-start(bf16[32,8,128]{2,1,0:T(8,128)(2,1)} %bitcast.139), calls=%async_computation.3 | async-start | bytes 131072 | tf_op jit(solution)/shard_map/all_to_all | solution.py:127

commit v2 on v1

v2 whole, which is shorter than its diff:
```python
import functools

import jax
import jax.numpy as jnp
from jax import lax
from jax.experimental import pallas as pl
from jax.experimental.pallas import tpu as pltpu
from jax.sharding import Mesh, PartitionSpec as P

BLOCK = 512
NEGATIVE = -1e30
SWAP = [(0, 1), (1, 0)]
LOG2_E = 1.4426950408889634
F32 = jnp.float32
BF16 = jnp.bfloat16
NT = (((1,), (1,)), ((), ()))
NN = (((1,), (0,)), ((), ()))
LIMIT = 4 << 20


def offset_of(info, picks, block, slot):
    return picks[(block * info[4] + info[2]) * 2 + slot]


def block_of(info, picks, block, slot):
    return jnp.maximum(block - offset_of(info, picks, block, slot), 0)


def dot(a, b, dims=NN):
    return lax.dot_general(a, b, dims, preferred_element_type=F32)


def first_half(shape):
    return lax.broadcasted_iota(jnp.int32, shape, len(shape) - 1) < shape[-1] // 2


def swap_halves(x):
    return pltpu.roll(x, x.shape[-1] // 2, x.ndim - 1)


def attend(
    heads, picked, info, picks, q_ref, g_ref, own_a, own_b, own_c, own_d, x_ref, y_ref, xc_ref, yc_ref,
    out_ref, dq_ref, own_mine, own_theirs, own_away, mine_ref, theirs_ref, away_ref,
    key_scr, value_scr, key_t, value_t, s_scr, dp_scr, low_scr, ds_scr, q_scr, g_scr, dk_scr, dv_scr,
):
    rows = q_ref.shape[0]
    dim = q_ref.shape[1] // heads
    core, pair = info[0], info[1]
    slots = picked + 1
    keys = slots * BLOCK
    scaling = dim ** (-0.5)
    is_low = pair == 0
    stripes = x_ref.shape[0]
    stripe = rows // stripes

    def split(own, other):
        low = jnp.where(is_low, own, other)
        high = jnp.where(is_low, other, own)
        half = first_half(low.shape)
        return jnp.where(half, low, swap_halves(high)), jnp.where(half, swap_halves(low), high)

    def place(at, own, other):
        k, v = split(own, other)
        key_scr[at : at + rows, :] = k.astype(BF16)
        value_scr[at : at + rows, :] = v.astype(BF16)
        key_t[:, at : at + rows] = k.T.astype(BF16)
        value_t[:, at : at + rows] = v.T.astype(BF16)

    place(0, own_a[...].astype(F32), own_b[...].astype(F32))
    place(rows, own_c[...].astype(F32), own_d[...].astype(F32))
    for half, (a_ref, b_ref) in enumerate(((x_ref, y_ref), (xc_ref, yc_ref))):
        a = a_ref[...].astype(F32).reshape(stripes, picked, stripe, dim)
        b = b_ref[...].astype(F32).reshape(stripes, picked, stripe, dim)
        for j in range(picked):
            place(
                (j + 1) * BLOCK + half * rows,
                a[:, j].reshape(rows, dim),
                b[:, j].reshape(rows, dim),
            )

    spans = [(at, at + rows) for at in range(0, keys, rows)]
    for h in range(heads):
        q = q_ref[:, h * dim : (h + 1) * dim]
        g = g_ref[:, h * dim : (h + 1) * dim]
        q_scr[h * rows : (h + 1) * rows, :] = q
        g_scr[h * rows : (h + 1) * rows, :] = g
        top = None
        for i, (lo, hi) in enumerate(spans):
            s = dot(key_scr[lo:hi, :], q, NT)
            if i == 0:
                s = jnp.where(
                    lax.broadcasted_iota(jnp.int32, s.shape, 0)
                    <= lax.broadcasted_iota(jnp.int32, s.shape, 1),
                    s,
                    NEGATIVE,
                )
            elif i == 1:
                s = jnp.where(core == 1, s, NEGATIVE)
            else:
                s = jnp.where(offset_of(info, picks, info[3], (i - 2) // 2) <= info[3], s, NEGATIVE)
            s_scr[lo:hi, :] = s
            m = jnp.max(s, axis=0, keepdims=True)
            top = m if top is None else jnp.maximum(top, m)
        total = jnp.zeros_like(top)
        delta = jnp.zeros_like(top)
        for lo, hi in spans:
            p = jnp.exp2((s_scr[lo:hi, :] - top) * (scaling * LOG2_E))
            dp = dot(value_scr[lo:hi, :], g, NT)
            s_scr[lo:hi, :] = p
            dp_scr[lo:hi, :] = dp
            total = total + jnp.sum(p, axis=0, keepdims=True)
            delta = delta + jnp.sum(p * dp, axis=0, keepdims=True)
        scale = 1.0 / total
        delta = delta * scale
        for lo, hi in spans:
            p = s_scr[lo:hi, :] * scale
            low_scr[lo:hi, h * rows : (h + 1) * rows] = p.astype(BF16)
            ds_scr[lo:hi, h * rows : (h + 1) * rows] = (p * (dp_scr[lo:hi, :] - delta)).astype(BF16)
        out_t = dot(value_t[...], low_scr[:, h * rows : (h + 1) * rows])
        out_ref[:, h * dim : (h + 1) * dim] = out_t.T.astype(BF16)
        dq_t = dot(key_t[...], ds_scr[:, h * rows : (h + 1) * rows])
        dq_ref[:, h * dim : (h + 1) * dim] = dq_t.T * scaling

    for lo, hi in spans:
        dk_scr[lo:hi, :] = dot(ds_scr[lo:hi, :], q_scr[...]) * scaling
        dv_scr[lo:hi, :] = dot(low_scr[lo:hi, :], g_scr[...])

    def parts(at):
        k, v = dk_scr[at : at + rows, :], dv_scr[at : at + rows, :]
        half = first_half(k.shape)
        low = jnp.where(half, k, swap_halves(v))
        high = jnp.where(half, swap_halves(k), v)
        return jnp.where(is_low, low, high), jnp.where(is_low, high, low)

    own_mine[...], own_theirs[...] = parts(0)
    a, b = parts(rows)
    own_away[0] = a.astype(BF16)
    own_away[1] = b.astype(BF16)
    for half in range(2):
        pairs = [parts((j + 1) * BLOCK + half * rows) for j in range(picked)]
        a, b = (
            jnp.concatenate([p[i].reshape(stripes, stripe, dim) for p in pairs], axis=1)
            for i in range(2)
        )
        if half == 0:
            mine_ref[...] = a
            theirs_ref[...] = b
        else:
            away_ref[0] = a.astype(BF16)
            away_ref[1] = b.astype(BF16)


def call(kernel, name, out_shape, scalars, arrays, scratch=(), limit=LIMIT):
    vmem = pl.BlockSpec(memory_space=pltpu.VMEM)
    smem = pl.BlockSpec(memory_space=pltpu.SMEM)
    return pl.pallas_call(
        kernel,
        out_shape=out_shape,
        in_specs=[smem] * len(scalars) + [vmem] * len(arrays),
        out_specs=jax.tree.map(lambda _: vmem, out_shape),
        scratch_shapes=list(scratch),
        compiler_params=pltpu.CompilerParams(vmem_limit_bytes=limit),
        name=name,
    )(*scalars, *arrays)


def attention(info, picks, q, g, own, fetched):
    rows, width = q.shape
    dim = own[0].shape[1]
    heads = width // dim
    striped = fetched[0].shape
    picked = striped[0] * striped[1] // rows
    keys = (picked + 1) * BLOCK
    shape = jax.ShapeDtypeStruct
    return call(
        functools.partial(attend, heads, picked),
        "attend",
        (
            shape((rows, width), BF16),
            shape((rows, width), F32),
            shape((rows, dim), F32),
            shape((rows, dim), F32),
            shape((2, rows, dim), BF16),
            shape(striped, F32),
            shape(striped, F32),
            shape((2, *striped), BF16),
        ),
        (info, picks),
        (q, g, *own, *fetched),
        (
            pltpu.VMEM((keys, dim), BF16),
            pltpu.VMEM((keys, dim), BF16),
            pltpu.VMEM((dim, keys), BF16),
            pltpu.VMEM((dim, keys), BF16),
            pltpu.VMEM((keys, rows), F32),
            pltpu.VMEM((keys, rows), F32),
            pltpu.VMEM((keys, heads * rows), BF16),
            pltpu.VMEM((keys, heads * rows), BF16),
            pltpu.VMEM((heads * rows, dim), BF16),
            pltpu.VMEM((heads * rows, dim), BF16),
            pltpu.VMEM((keys, dim), F32),
            pltpu.VMEM((keys, dim), F32),
        ),
        28 << 20,
    )


def pack(k_ref, v_ref, own_ref, striped_ref):
    both = jnp.concatenate([k_ref[...].astype(F32), v_ref[...].astype(F32)], 0).T
    own_ref[...] = both.astype(BF16)
    striped_ref[...] = both.reshape(striped_ref.shape).astype(BF16)


def gather(info, picks, banded_ref, out_ref, scr):
    scr[...] = banded_ref[...].astype(F32)
    picked = out_ref.shape[1] // scr.shape[1]
    for d in range(out_ref.shape[0]):
        rows = [scr[block_of(info, picks, d, j)] for j in range(picked)]
        out_ref[d] = jnp.concatenate(rows, 0).astype(BF16)


def scatter(info, picks, landed_ref, out_ref, acc):
    acc[...] = jnp.zeros_like(acc)
    stripe = acc.shape[1]
    for d in range(landed_ref.shape[0]):
        rows = landed_ref[d].astype(F32)
        for j in range(rows.shape[0] // stripe):
            at = block_of(info, picks, d, j)
            acc[at] = acc[at] + rows[j * stripe : (j + 1) * stripe]
    out_ref[...] = acc[...].astype(BF16)


def unpack(mine_ref, got_ref, pair_ref, back_ref, gk_ref, gv_ref):
    total = mine_ref[...] + got_ref[0].astype(F32) + pair_ref[...].astype(F32)
    total = total + back_ref[...].astype(F32).reshape(total.shape)
    both = total.T
    gk_ref[...] = both[: gk_ref.shape[0]]
    gv_ref[...] = both[gk_ref.shape[0] :]


def local(queries, key_states, value_states, block_picks, grad_output):
    row_count = queries.shape[0]
    half_dim = key_states.shape[1]
    head_dim = 2 * half_dim
    z_count = lax.axis_size("z")
    picked = block_picks.shape[2]
    stripe = row_count // z_count
    axes = [lax.axis_index(name) for name in ("core", "pair", "grp", "z")]
    info = jnp.stack(axes + [jnp.int32(lax.axis_size("grp"))]).astype(jnp.int32)
    picks = block_picks.reshape(-1)
    shape = jax.ShapeDtypeStruct
    banded_shape = shape((z_count, stripe, head_dim), BF16)
    striped_shape = shape((z_count, picked * stripe, head_dim), BF16)

    def exchange(x):
        other = lax.ppermute(x, "pair", SWAP)
        other_core = lax.ppermute(x, "core", SWAP)
        both = lax.ppermute(x, ("core", "pair"), [(i, 3 - i) for i in range(4)])
        return x, other, other_core, both

    def across(x):
        return lax.all_to_all(x, "z", split_axis=0, concat_axis=0, tiled=True)

    own, striped = call(
        pack,
        "pack",
        (shape((row_count, head_dim), BF16), banded_shape),
        (),
        (key_states.T, value_states.T),
    )
    banded = across(striped)
    own = exchange(own)
    banded, own = lax.optimization_barrier((banded, own))
    scratch = (pltpu.VMEM(banded_shape.shape, F32),)
    outgoing = call(gather, "gather", striped_shape, (info, picks), (banded,), scratch)
    fetched = exchange(across(outgoing))

    out, grad_queries, own_mine, own_theirs, own_away, mine, theirs, away = attention(
        info, picks, queries, grad_output, own, fetched
    )

    def from_partners(theirs, away):
        got = lax.ppermute(away, "core", SWAP)
        summed = (theirs + got[1].astype(F32)).astype(BF16)
        return got, lax.ppermute(summed, "pair", SWAP)

    got, from_pair = from_partners(theirs, away)
    landed = across((mine + got[0].astype(F32) + from_pair.astype(F32)).astype(BF16))
    got, from_pair = from_partners(own_theirs, own_away)
    landed, got, from_pair = lax.optimization_barrier((landed, got, from_pair))
    back = across(call(scatter, "scatter", banded_shape, (info, picks), (landed,), scratch))
    grad_k, grad_v = call(
        unpack,
        "unpack",
        (shape((half_dim, row_count), F32),) * 2,
        (),
        (own_mine, got, from_pair, back),
    )
    return out, grad_queries, grad_k.T, grad_v.T


def solution(mesh):
    seq, heads = mesh.devices.shape
    split = Mesh(
        mesh.devices.reshape(seq // 2, 2, heads // 2, 2), ("z", "core", "grp", "pair")
    )
    spec = P(("z", "core"), ("grp", "pair"))
    return jax.shard_map(
        local,
        mesh=split,
        in_specs=(spec, spec, spec, P(), spec),
        out_specs=(spec, spec, spec, spec),
        check_vma=False,
    )
```

time: 224 us -> 193 us (0.86)
  blocking collectives: 0 us -> 65.4 us
  waiting for transfers between devices: 102 us -> 51.9 us
  local copies, waits for them, and re-layouts: 33.8 us -> 2.58 us
  other arithmetic: 14.3 us -> 0.76 us
  matrix products: 12.9 us -> 0 us
  Pallas kernels: 0 us -> 11.4 us
    all_to_all x0 -> x2, blocking collectives: none -> 65.4 us  [across(): return lax.all_to_all(x, 'z', split_axis=0, concat_axis=0, tiled=True)]
    all_to_all x4 -> x2, waiting for transfers between devices: 93.7 us -> 35.9 us  [across(): return lax.all_to_all(x, 'z', split_axis=0, concat_axis=0, tiled=True)]
    pallas_call x0 -> x5, Pallas kernels: none -> 11.4 us  [call(): pl.pallas_call(kernel, out_shape=out_shape, in_specs=[smem] * len(scalars...]
    ppermute x6 -> x10, starting transfers between devices: 16.9 us -> 26.5 us  [the longest x2 6.97 us: from_partners(): return (got, lax.ppermute(summed, 'pair', SWAP))]
    unnamed x24 -> x11, local copies, waits for them, and re-layouts: 11.7 us -> 2.35 us
    slice x8 -> x0, local copies, waits for them, and re-layouts: 9.23 us -> none  [the longest x1 3.1 us: local(): from_core = lax.ppermute(grads[:, 1].astype(jnp.bfloat16), 'core', SWAP)]
    all_to_all x4 -> x2, starting transfers between devices: 41.7 us -> 32.6 us  [across(): return lax.all_to_all(x, 'z', split_axis=0, concat_axis=0, tiled=True)]
    dot_general x6 -> x0, matrix products: 8.08 us -> none  [the longest x1 2.41 us: local(): jnp.einsum('hrk,kd->rhd', dscore, key_tiles, preferred_element_type=jnp.f...]
  transfers between devices with their start and end apart: 10 -> 12, of which waited for: 6 -> 8; matrix products, arithmetic and copies ran while one was open for 9% -> 0% of each run, Pallas kernels for 0% -> 0%
where the time goes in v2:
time: 193 us; the launch traced here: 192 us
  blocking collectives  65.4 us (34%)
  starting transfers between devices  59.1 us (31%)
  waiting for transfers between devices  51.9 us (27%)
  Pallas kernels  11.4 us (6%)
  local copies, waits for them, and re-layouts  2.58 us (1%)
    all_to_all x2, blocking collectives, across(): return lax.all_to_all(x, 'z', split_axis=0, concat_axis=0, tiled=True)  65.4 us
    all_to_all x2, waiting for transfers between devices, across(): return lax.all_to_all(x, 'z', split_axis=0, concat_axis=0, tiled=True)  35.9 us
    all_to_all x2, starting transfers between devices, across(): return lax.all_to_all(x, 'z', split_axis=0, concat_axis=0, tiled=True)  32.6 us
    pallas_call x5, Pallas kernels, call(): pl.pallas_call(kernel, out_shape=out_shape, in_specs=[smem] * len(scalars...  11.4 us
    ppermute x2, starting transfers between devices, from_partners(): return (got, lax.ppermute(summed, 'pair', SWAP))  6.97 us
    ppermute x2, waiting for transfers between devices, from_partners(): return (got, lax.ppermute(summed, 'pair', SWAP))  6.61 us
    ppermute x2, waiting for transfers between devices, exchange(): other = lax.ppermute(x, 'pair', SWAP)  6.48 us
    ppermute x2, starting transfers between devices, exchange(): other = lax.ppermute(x, 'pair', SWAP)  5.84 us
  transfers between devices with their start and end apart: 12, of which 8 were waited for; matrix products, arithmetic and copies ran while one was open for 0% of the time, Pallas kernels for 0%

profile of v2, /device:TPU:6, one launch (start us, length us, event | category | flops | bytes accessed | tf_op | source)
XLA Modules:
  0.0 191.9 jit_solution(17742190548624492412)
XLA Ops:
  0.6 0.0 copy-start.2
  0.6 0.7 copy-done.2
  1.4 0.0 copy-start.3
  1.4 0.8 copy-done.3
  2.1 0.7 pack.1
  2.9 28.7 %all-to-all-start = ((bf16[32,8,128]{2,1,0:T(8,128)(2,1)}), bf16[32,8,128]{2,1,0:T(8,128)(2,1)S(1)}, u32[]{:S(2)}, u32[]{:S(2)}) async-start(bf16[32,8,128]{2,1,0:T(8,128)(2,1)} %get-tuple-element.24), calls=%async_computation | async-start | bytes 131072 | tf_op jit(solution)/shard_map/all_to_all | solution.py:262
  31.6 2.6 %collective-permute-start.2 = (bf16[256,128]{1,0:T(8,128)(2,1)S(1)}, bf16[256,128]{1,0:T(8,128)(2,1)S(1)}, u32[]{:S(2)}, u32[]{:S(2)}) collective-permute-start(bf16[256,128]{1,0:T(8,128)(2,1)S(1)} %get-tuple-element.26.own_a), channel_id=1, source_target_pairs={{0,17},{1,16},{16,1},{17,0},{2,19},{3,18},{18,3},{19,2},{4,21},{5,... | collective-permute-start | bytes 196616 | tf_op jit(solution)/shard_map/ppermute | solution.py:258
  34.3 2.9 %collective-permute-start.1 = (bf16[256,128]{1,0:T(8,128)(2,1)S(1)}, bf16[256,128]{1,0:T(8,128)(2,1)S(1)}, u32[]{:S(2)}, u32[]{:S(2)}) collective-permute-start(bf16[256,128]{1,0:T(8,128)(2,1)S(1)} %get-tuple-element.26.own_a), channel_id=1, source_target_pairs={{0,16},{16,0},{1,17},{17,1},{2,18},{18,2},{3,19},{19,3},{4,20},{20... | collective-permute-start | bytes 196616 | tf_op jit(solution)/shard_map/ppermute | solution.py:257
  37.1 2.4 %collective-permute-start = (bf16[256,128]{1,0:T(8,128)(2,1)S(1)}, bf16[256,128]{1,0:T(8,128)(2,1)S(1)}, u32[]{:S(2)}, u32[]{:S(2)}) collective-permute-start(bf16[256,128]{1,0:T(8,128)(2,1)S(1)} %get-tuple-element.26.own_a), channel_id=1, source_target_pairs={{0,1},{1,0},{2,3},{3,2},{4,5},{5,4},{6,7},{7,6},{8,9},{9,8},{10,11... | collective-permute-start | bytes 196616 | tf_op jit(solution)/shard_map/ppermute | solution.py:256
  39.5 0.0 copy-start.4
  39.5 0.7 copy-done.4
  40.2 0.1 copy.9
  40.4 0.0 copy-start.1
  40.4 0.1 reshape.17.picks
  40.5 0.0 copy-start
  40.5 0.1 stack.19.info
  40.6 0.0 collective-permute-done.2.own_d
  40.6 0.0 collective-permute-done.1.own_c
  40.6 2.7 %collective-permute-done.own_b = bf16[256,128]{1,0:T(8,128)(2,1)S(1)} collective-permute-done((bf16[256,128]{1,0:T(8,128)(2,1)S(1)}, bf16[256,128]{1,0:T(8,128)(2,1)S(1)}, u32[]{:S(2)}, u32[]{:S(2)}) %collective-permute-start) | collective-permute-done | bytes 65568 | tf_op jit(solution)/shard_map/ppermute | solution.py:256
  43.3 14.1 %all-to-all-done.banded_ref = bf16[32,8,128]{2,1,0:T(8,128)(2,1)S(1)} async-done(((bf16[32,8,128]{2,1,0:T(8,128)(2,1)}), bf16[32,8,128]{2,1,0:T(8,128)(2,1)S(1)}, u32[]{:S(2)}, u32[]{:S(2)}) %all-to-all-start) | async-done | bytes 65568 | tf_op jit(solution)/shard_map/all_to_all | solution.py:262
  57.4 0.7 gather.1
  58.1 37.9 %all_to_all.20.x_ref = bf16[32,16,128]{2,1,0:T(8,128)(2,1)S(1)} all-to-all(bf16[32,16,128]{2,1,0:T(8,128)(2,1)S(1)} %gather.1), channel_id=1, replica_groups=mesh['z'=32,'core'=2,'grp'=8,'pair'=2] {'z'}, dimensions={0} | all-to-all | bytes 262144 | tf_op jit(solution)/shard_map/all_to_all | solution.py:262
  96.0 1.9 collective-permute-start.5
  98.0 2.5 %collective-permute-start.4 = (bf16[32,16,128]{2,1,0:T(8,128)(2,1)S(1)}, bf16[32,16,128]{2,1,0:T(8,128)(2,1)S(1)}, u32[]{:S(2)}, u32[]{:S(2)}) collective-permute-start(bf16[32,16,128]{2,1,0:T(8,128)(2,1)S(1)} %all_to_all.20.x_ref), channel_id=1, source_target_pairs={{0,16},{16,0},{1,17},{17,1},{2,18},{18,2},{3,19},{19,3},{4,20},{20... | collective-permute-start | bytes 393224 | tf_op jit(solution)/shard_map/ppermute | solution.py:257
  100.4 3.5 %collective-permute-start.3 = (bf16[32,16,128]{2,1,0:T(8,128)(2,1)S(1)}, bf16[32,16,128]{2,1,0:T(8,128)(2,1)S(1)}, u32[]{:S(2)}, u32[]{:S(2)}) collective-permute-start(bf16[32,16,128]{2,1,0:T(8,128)(2,1)S(1)} %all_to_all.20.x_ref), channel_id=1, source_target_pairs={{0,1},{1,0},{2,3},{3,2},{4,5},{5,4},{6,7},{7,6},{8,9},{9,8},{10,11... | collective-permute-start | bytes 393224 | tf_op jit(solution)/shard_map/ppermute | solution.py:256
  103.9 0.0 collective-permute-done.5.yc_ref
  103.9 0.0 collective-permute-done.4.xc_ref
  103.9 3.8 %collective-permute-done.3.y_ref = bf16[32,16,128]{2,1,0:T(8,128)(2,1)S(1)} collective-permute-done((bf16[32,16,128]{2,1,0:T(8,128)(2,1)S(1)}, bf16[32,16,128]{2,1,0:T(8,128)(2,1)S(1)}, u32[]{:S(2)}, u32[]{:S(2)}) %collective-permute-start.3) | collective-permute-done | bytes 131104 | tf_op jit(solution)/shard_map/ppermute | solution.py:256
  107.7 0.0 copy-done.1
  107.7 0.0 copy-done
  107.7 8.3 %attend.1 = (bf16[256,512]{1,0:T(8,128)(2,1)}, f32[256,512]{1,0:T(8,128)}, f32[256,128]{1,0:T(8,128)S(1)}, f32[256,128]{1,0:T(8,128)S(1)}, bf16[2,256,128]{2,1,0...) custom-call(s32[5]{0:T(128)S(1)} %stack.19.info, ...), custom_call_target="tpu_custom_call" | custom-call | tf_op jit(solution)/shard_map/attend/pallas_call | solution.py:156
  116.0 1.9 collective-permute-start.6
  118.0 1.5 collective-permute-done.6
  119.5 3.5 %collective-permute-start.7 = (bf16[32,16,128]{2,1,0:T(8,128)(2,1)S(1)}, bf16[32,16,128]{2,1,0:T(8,128)(2,1)S(1)}, u32[]{:S(2)}, u32[]{:S(2)}) collective-permute-start(bf16[32,16,128]{2,1,0:T(8,128)(2,1)S(1)} %fusion), channel_id=1, source_target_pairs={{0,1},{1,0},{2,3},{3,2},{4,5},{5,4},{6,7},{7,6},{8,9},{9,8},{10,11... | collective-permute-start | bytes 393224 | tf_op jit(solution)/shard_map/ppermute | solution.py:285
  123.0 3.9 %collective-permute-done.7 = bf16[32,16,128]{2,1,0:T(8,128)(2,1)S(1)} collective-permute-done((bf16[32,16,128]{2,1,0:T(8,128)(2,1)S(1)}, bf16[32,16,128]{2,1,0:T(8,128)(2,1)S(1)}, u32[]{:S(2)}, u32[]{:S(2)}) %collective-permute-start.7) | collective-permute-done | bytes 131104 | tf_op jit(solution)/shard_map/ppermute | solution.py:285
  126.9 0.7 fusion.2
  127.6 3.8 %all-to-all-start.2 = ((bf16[32,16,128]{2,1,0:T(8,128)(2,1)}), bf16[32,16,128]{2,1,0:T(8,128)(2,1)S(1)}, u32[]{:S(2)}, u32[]{:S(2)}) async-start(bf16[32,16,128]{2,1,0:T(8,128)(2,1)} %fusion.2), calls=%async_computation.2 | async-start | bytes 262144 | tf_op jit(solution)/shard_map/all_to_all | solution.py:262
  131.5 1.9 %collective-permute-start.8 = (bf16[2,256,128]{2,1,0:T(8,128)(2,1)S(1)}, bf16[2,256,128]{2,1,0:T(8,128)(2,1)S(1)}, u32[]{:S(2)}, u32[]{:S(2)}) collective-permute-start(bf16[2,256,128]{2,1,0:T(8,128)(2,1)S(1)} %get-tuple-element.37), channel_id=1, source_target_pairs={{0,16},{16,0},{1,17},{17,1},{2,18},{18,2},{3,19},{19,3},{4,20},{20... | collective-permute-start | bytes 393224 | tf_op jit(solution)/shard_map/ppermute | solution.py:283
  133.4 1.3 collective-permute-done.8.got_ref
  134.8 3.5 %collective-permute-start.9 = (bf16[256,128]{1,0:T(8,128)(2,1)S(1)}, bf16[256,128]{1,0:T(8,128)(2,1)S(1)}, u32[]{:S(2)}, u32[]{:S(2)}) collective-permute-start(bf16[256,128]{1,0:T(8,128)(2,1)S(1)} %fusion.3), channel_id=1, source_target_pairs={{0,1},{1,0},{2,3},{3,2},{4,5},{5,4},{6,7},{7,6},{8,9},{9,8},{10,11... | collective-permute-start | bytes 196616 | tf_op jit(solution)/shard_map/ppermute | solution.py:285
  138.2 2.7 %collective-permute-done.9.pair_ref = bf16[256,128]{1,0:T(8,128)(2,1)S(1)} collective-permute-done((bf16[256,128]{1,0:T(8,128)(2,1)S(1)}, bf16[256,128]{1,0:T(8,128)(2,1)S(1)}, u32[]{:S(2)}, u32[]{:S(2)}) %collective-permute-start.9) | collective-permute-done | bytes 65568 | tf_op jit(solution)/shard_map/ppermute | solution.py:285
  140.9 21.8 %all-to-all-done.2.landed_ref = bf16[32,16,128]{2,1,0:T(8,128)(2,1)S(1)} async-done(((bf16[32,16,128]{2,1,0:T(8,128)(2,1)}), bf16[32,16,128]{2,1,0:T(8,128)(2,1)S(1)}, u32[]{:S(2)}, u32[]{:S(2)}) %all-to-all-start.2) | async-done | bytes 131104 | tf_op jit(solution)/shard_map/all_to_all | solution.py:262
  162.8 0.9 scatter.1
  163.7 27.5 %all_to_all.21.back_ref = bf16[32,8,128]{2,1,0:T(8,128)(2,1)S(1)} all-to-all(bf16[32,8,128]{2,1,0:T(8,128)(2,1)S(1)} %scatter.1), channel_id=1, replica_groups=mesh['z'=32,'core'=2,'grp'=8,'pair'=2] {'z'}, dimensions={0} | all-to-all | bytes 131072 | tf_op jit(solution)/shard_map/all_to_all | solution.py:262
  191.2 0.7 unpack.1
  (2 shorter events, 0.1 us)
Async XLA Ops:
  0.6 0.8 copy-start.2
  1.4 0.8 copy-start.3
  2.9 54.5 %all-to-all-start = ((bf16[32,8,128]{2,1,0:T(8,128)(2,1)}), bf16[32,8,128]{2,1,0:T(8,128)(2,1)S(1)}, u32[]{:S(2)}, u32[]{:S(2)}) async-start(bf16[32,8,128]{2,1,0:T(8,128)(2,1)} %get-tuple-element.24), calls=%async_computation | async-start | bytes 131072 | tf_op jit(solution)/shard_map/all_to_all | solution.py:262
  31.6 9.0 %collective-permute-start.2 = (bf16[256,128]{1,0:T(8,128)(2,1)S(1)}, bf16[256,128]{1,0:T(8,128)(2,1)S(1)}, u32[]{:S(2)}, u32[]{:S(2)}) collective-permute-start(bf16[256,128]{1,0:T(8,128)(2,1)S(1)} %get-tuple-element.26.own_a), channel_id=1, source_target_pairs={{0,17},{1,16},{16,1},{17,0},{2,19},{3,18},{18,3},{19,2},{4,21},{5,... | collective-permute-start | bytes 196616 | tf_op jit(solution)/shard_map/ppermute | solution.py:258
  34.3 6.3 %collective-permute-start.1 = (bf16[256,128]{1,0:T(8,128)(2,1)S(1)}, bf16[256,128]{1,0:T(8,128)(2,1)S(1)}, u32[]{:S(2)}, u32[]{:S(2)}) collective-permute-start(bf16[256,128]{1,0:T(8,128)(2,1)S(1)} %get-tuple-element.26.own_a), channel_id=1, source_target_pairs={{0,16},{16,0},{1,17},{17,1},{2,18},{18,2},{3,19},{19,3},{4,20},{20... | collective-permute-start | bytes 196616 | tf_op jit(solution)/shard_map/ppermute | solution.py:257
  37.1 6.2 %collective-permute-start = (bf16[256,128]{1,0:T(8,128)(2,1)S(1)}, bf16[256,128]{1,0:T(8,128)(2,1)S(1)}, u32[]{:S(2)}, u32[]{:S(2)}) collective-permute-start(bf16[256,128]{1,0:T(8,128)(2,1)S(1)} %get-tuple-element.26.own_a), channel_id=1, source_target_pairs={{0,1},{1,0},{2,3},{3,2},{4,5},{5,4},{6,7},{7,6},{8,9},{9,8},{10,11... | collective-permute-start | bytes 196616 | tf_op jit(solution)/shard_map/ppermute | solution.py:256
  39.5 0.7 copy-start.4
  40.4 67.4 %copy-start.1 = (bf16[256,512]{1,0:T(8,128)(2,1)S(1)}, bf16[256,512]{1,0:T(8,128)(2,1)}, u32[]{:S(2)}) copy-start(bf16[256,512]{1,0:T(8,128)(2,1)} %g_ref.1) | copy-start | bytes 786436
  40.5 67.2 %copy-start = (bf16[256,512]{1,0:T(8,128)(2,1)S(1)}, bf16[256,512]{1,0:T(8,128)(2,1)}, u32[]{:S(2)}) copy-start(bf16[256,512]{1,0:T(8,128)(2,1)} %q_ref.1) | copy-start | bytes 786436
  96.0 7.9 %collective-permute-start.5 = (bf16[32,16,128]{2,1,0:T(8,128)(2,1)S(1)}, bf16[32,16,128]{2,1,0:T(8,128)(2,1)S(1)}, u32[]{:S(2)}, u32[]{:S(2)}) collective-permute-start(bf16[32,16,128]{2,1,0:T(8,128)(2,1)S(1)} %all_to_all.20.x_ref), channel_id=1, source_target_pairs={{0,17},{1,16},{16,1},{17,0},{2,19},{3,18},{18,3},{19,2},{4,21},{5,... | collective-permute-start | bytes 393224 | tf_op jit(solution)/shard_map/ppermute | solution.py:258
  98.0 6.0 %collective-permute-start.4 = (bf16[32,16,128]{2,1,0:T(8,128)(2,1)S(1)}, bf16[32,16,128]{2,1,0:T(8,128)(2,1)S(1)}, u32[]{:S(2)}, u32[]{:S(2)}) collective-permute-start(bf16[32,16,128]{2,1,0:T(8,128)(2,1)S(1)} %all_to_all.20.x_ref), channel_id=1, source_target_pairs={{0,16},{16,0},{1,17},{17,1},{2,18},{18,2},{3,19},{19,3},{4,20},{20... | collective-permute-start | bytes 393224 | tf_op jit(solution)/shard_map/ppermute | solution.py:257
  100.4 7.3 %collective-permute-start.3 = (bf16[32,16,128]{2,1,0:T(8,128)(2,1)S(1)}, bf16[32,16,128]{2,1,0:T(8,128)(2,1)S(1)}, u32[]{:S(2)}, u32[]{:S(2)}) collective-permute-start(bf16[32,16,128]{2,1,0:T(8,128)(2,1)S(1)} %all_to_all.20.x_ref), channel_id=1, source_target_pairs={{0,1},{1,0},{2,3},{3,2},{4,5},{5,4},{6,7},{7,6},{8,9},{9,8},{10,11... | collective-permute-start | bytes 393224 | tf_op jit(solution)/shard_map/ppermute | solution.py:256
  116.0 3.4 %collective-permute-start.6 = (bf16[2,32,16,128]{3,2,1,0:T(8,128)(2,1)S(1)}, bf16[2,32,16,128]{3,2,1,0:T(8,128)(2,1)S(1)}, u32[]{:S(2)}, u32[]{:S(2)}) collective-permute-start(bf16[2,32,16,128]{3,2,1,0:T(8,128)(2,1)S(1)} %get-tuple-element.35), channel_id=1, source_target_pairs={{0,16},{16,0},{1,17},{17,1},{2,18},{18,2},{3,19},{19,3},{4,20},{20... | collective-permute-start | bytes 786440 | tf_op jit(solution)/shard_map/ppermute | solution.py:283
  119.5 7.4 %collective-permute-start.7 = (bf16[32,16,128]{2,1,0:T(8,128)(2,1)S(1)}, bf16[32,16,128]{2,1,0:T(8,128)(2,1)S(1)}, u32[]{:S(2)}, u32[]{:S(2)}) collective-permute-start(bf16[32,16,128]{2,1,0:T(8,128)(2,1)S(1)} %fusion), channel_id=1, source_target_pairs={{0,1},{1,0},{2,3},{3,2},{4,5},{5,4},{6,7},{7,6},{8,9},{9,8},{10,11... | collective-permute-start | bytes 393224 | tf_op jit(solution)/shard_map/ppermute | solution.py:285
  127.6 35.1 %all-to-all-start.2 = ((bf16[32,16,128]{2,1,0:T(8,128)(2,1)}), bf16[32,16,128]{2,1,0:T(8,128)(2,1)S(1)}, u32[]{:S(2)}, u32[]{:S(2)}) async-start(bf16[32,16,128]{2,1,0:T(8,128)(2,1)} %fusion.2), calls=%async_computation.2 | async-start | bytes 262144 | tf_op jit(solution)/shard_map/all_to_all | solution.py:262
  131.5 3.2 %collective-permute-start.8 = (bf16[2,256,128]{2,1,0:T(8,128)(2,1)S(1)}, bf16[2,256,128]{2,1,0:T(8,128)(2,1)S(1)}, u32[]{:S(2)}, u32[]{:S(2)}) collective-permute-start(bf16[2,256,128]{2,1,0:T(8,128)(2,1)S(1)} %get-tuple-element.37), channel_id=1, source_target_pairs={{0,16},{16,0},{1,17},{17,1},{2,18},{18,2},{3,19},{19,3},{4,20},{20... | collective-permute-start | bytes 393224 | tf_op jit(solution)/shard_map/ppermute | solution.py:283
  134.8 6.2 %collective-permute-start.9 = (bf16[256,128]{1,0:T(8,128)(2,1)S(1)}, bf16[256,128]{1,0:T(8,128)(2,1)S(1)}, u32[]{:S(2)}, u32[]{:S(2)}) collective-permute-start(bf16[256,128]{1,0:T(8,128)(2,1)S(1)} %fusion.3), channel_id=1, source_target_pairs={{0,1},{1,0},{2,3},{3,2},{4,5},{5,4},{6,7},{7,6},{8,9},{9,8},{10,11... | collective-permute-start | bytes 196616 | tf_op jit(solution)/shard_map/ppermute | solution.py:285

commit v3 on v2

v3 whole, which is shorter than its diff:
```python
import functools

import jax
import jax.numpy as jnp
from jax import lax
from jax.experimental import pallas as pl
from jax.experimental.pallas import tpu as pltpu
from jax.sharding import Mesh, PartitionSpec as P

BLOCK = 512
NEGATIVE = -1e30
SWAP = [(0, 1), (1, 0)]
LOG2_E = 1.4426950408889634
F32 = jnp.float32
BF16 = jnp.bfloat16
NT = (((1,), (1,)), ((), ()))
NN = (((1,), (0,)), ((), ()))
LIMIT = 4 << 20


def offset_of(info, picks, block, slot):
    return picks[(block * info[4] + info[2]) * 2 + slot]


def block_of(info, picks, block, slot):
    return jnp.maximum(block - offset_of(info, picks, block, slot), 0)


def dot(a, b, dims=NN):
    return lax.dot_general(a, b, dims, preferred_element_type=F32)


def first_half(shape):
    return lax.broadcasted_iota(jnp.int32, shape, len(shape) - 1) < shape[-1] // 2


def swap_halves(x):
    return pltpu.roll(x, x.shape[-1] // 2, x.ndim - 1)


def split_features(is_low, own, other):
    low = jnp.where(is_low, own, other)
    high = jnp.where(is_low, other, own)
    half = first_half(low.shape)
    return jnp.where(half, low, swap_halves(high)), jnp.where(half, swap_halves(low), high)


def join_features(is_low, k, v):
    half = first_half(k.shape)
    low = jnp.where(half, k, swap_halves(v))
    high = jnp.where(half, swap_halves(k), v)
    return jnp.where(is_low, low, high), jnp.where(is_low, high, low)


def load_tiles(pieces, is_low, key_scr, value_scr, key_t, value_t):
    rows = pieces[0][0].shape[0]
    for i, (own, other) in enumerate(pieces):
        k, v = split_features(is_low, own, other)
        at = slice(i * rows, (i + 1) * rows)
        key_scr[at, :] = k.astype(BF16)
        value_scr[at, :] = v.astype(BF16)
        key_t[:, at] = k.T.astype(BF16)
        value_t[:, at] = v.T.astype(BF16)


def spans_of(ref, rows):
    return [slice(at, at + rows) for at in range(0, ref.shape[0], rows)]


def own_scores(
    heads, info, q_ref, g_ref, own_a, own_b, own_c, own_d,
    p_ref, dp_ref, stats, key_t, value_t, q_all, g_all, key_scr, value_scr,
):
    rows = q_ref.shape[0]
    dim = q_ref.shape[1] // heads
    rate = dim ** (-0.5) * LOG2_E
    pieces = [(own_a, own_b), (own_c, own_d)]
    pieces = [tuple(ref[...].astype(F32) for ref in piece) for piece in pieces]
    load_tiles(pieces, info[1] == 0, key_scr, value_scr, key_t, value_t)
    for h in range(heads):
        q = q_ref[:, h * dim : (h + 1) * dim]
        g = g_ref[:, h * dim : (h + 1) * dim]
        col = slice(h * rows, (h + 1) * rows)
        q_all[col, :] = q
        g_all[col, :] = g
        spans = spans_of(key_scr, rows)
        s = dot(key_scr[spans[0], :], q, NT)
        earlier = lax.broadcasted_iota(jnp.int32, s.shape, 0) <= lax.broadcasted_iota(
            jnp.int32, s.shape, 1
        )
        s = jnp.where(earlier, s, NEGATIVE)
        p_ref[spans[0], col] = s
        top = jnp.max(s, axis=0, keepdims=True)
        s = jnp.where(info[0] == 1, dot(key_scr[spans[1], :], q, NT), NEGATIVE)
        p_ref[spans[1], col] = s
        top = jnp.maximum(top, jnp.max(s, axis=0, keepdims=True))
        total = jnp.zeros_like(top)
        delta = jnp.zeros_like(top)
        for span in spans:
            p = jnp.exp2((p_ref[span, col] - top) * rate)
            dp = dot(value_scr[span, :], g, NT)
            p_ref[span, col] = p
            dp_ref[span, col] = dp
            total = total + jnp.sum(p, axis=0, keepdims=True)
            delta = delta + jnp.sum(p * dp, axis=0, keepdims=True)
        stats[0:1, col] = top
        stats[1:2, col] = total
        stats[2:3, col] = delta


def picked_grads(
    heads, picked, info, picks, q_all, g_all, stats, x_ref, y_ref, xc_ref, yc_ref,
    mine_ref, theirs_ref, away_ref, low_ref, ds_ref, key_t, value_t, merged,
    key_scr, value_scr, s_scr, dp_scr,
):
    rows, dim = q_all.shape[0] // heads, q_all.shape[1]
    scaling = dim ** (-0.5)
    rate = scaling * LOG2_E
    is_low = info[1] == 0
    stripes = x_ref.shape[0]
    stripe = rows // stripes
    halves = [
        [ref[...].astype(F32).reshape(stripes, picked, stripe, dim) for ref in refs]
        for refs in ((x_ref, y_ref), (xc_ref, yc_ref))
    ]
    pieces = [
        tuple(part[:, j].reshape(rows, dim) for part in half) for j in range(picked) for half in halves
    ]
    load_tiles(pieces, is_low, key_scr, value_scr, key_t, value_t)
    spans = spans_of(key_scr, rows)
    for h in range(heads):
        col = slice(h * rows, (h + 1) * rows)
        q, g = q_all[col, :], g_all[col, :]
        own_top = stats[0:1, col]
        top = own_top
        for i, span in enumerate(spans):
            s = dot(key_scr[span, :], q, NT)
            s = jnp.where(offset_of(info, picks, info[3], i // 2) <= info[3], s, NEGATIVE)
            s_scr[span, :] = s
            top = jnp.maximum(top, jnp.max(s, axis=0, keepdims=True))
        shift = jnp.exp2((own_top - top) * rate)
        total = stats[1:2, col] * shift
        delta = stats[2:3, col] * shift
        for span in spans:
            p = jnp.exp2((s_scr[span, :] - top) * rate)
            dp = dot(value_scr[span, :], g, NT)
            s_scr[span, :] = p
            dp_scr[span, :] = dp
            total = total + jnp.sum(p, axis=0, keepdims=True)
            delta = delta + jnp.sum(p * dp, axis=0, keepdims=True)
        scale = 1.0 / total
        delta = delta * scale
        merged[0:1, col] = shift * scale
        merged[1:2, col] = delta
        for span in spans:
            p = s_scr[span, :] * scale
            low_ref[span, col] = p.astype(BF16)
            ds_ref[span, col] = (p * (dp_scr[span, :] - delta)).astype(BF16)
    parts = []
    for span in spans:
        k = dot(ds_ref[span, :], q_all[...]) * scaling
        v = dot(low_ref[span, :], g_all[...])
        parts.append(join_features(is_low, k, v))
    for half in range(2):
        a, b = (
            jnp.concatenate(
                [parts[2 * j + half][i].reshape(stripes, stripe, dim) for j in range(picked)], axis=1
            )
            for i in range(2)
        )
        if half == 0:
            mine_ref[...] = a
            theirs_ref[...] = b
        else:
            away_ref[0] = a.astype(BF16)
            away_ref[1] = b.astype(BF16)


def row_outputs(
    heads, info, q_all, g_all, p_ref, dp_ref, merged, own_kt, own_vt, low_ref, ds_ref, key_t, value_t,
    out_ref, dq_ref, own_mine, own_theirs, own_away, low_scr, ds_scr,
):
    rows, dim = q_all.shape[0] // heads, q_all.shape[1]
    scaling = dim ** (-0.5)
    spans = spans_of(p_ref, rows)
    for h in range(heads):
        lane = slice(h * dim, (h + 1) * dim)
        col = slice(h * rows, (h + 1) * rows)
        scale, delta = merged[0:1, col], merged[1:2, col]
        for span in spans:
            p = p_ref[span, col] * scale
            low_scr[span, col] = p.astype(BF16)
            ds_scr[span, col] = (p * (dp_ref[span, col] - delta)).astype(BF16)
        out_t = dot(own_vt[...], low_scr[:, col]) + dot(value_t[...], low_ref[:, col])
        out_ref[:, lane] = out_t.T.astype(BF16)
        dq_t = dot(own_kt[...], ds_scr[:, col]) + dot(key_t[...], ds_ref[:, col])
        dq_ref[:, lane] = dq_t.T * scaling
    for i, span in enumerate(spans):
        k = dot(ds_scr[span, :], q_all[...]) * scaling
        v = dot(low_scr[span, :], g_all[...])
        a, b = join_features(info[1] == 0, k, v)
        if i == 0:
            own_mine[...] = a
            own_theirs[...] = b
        else:
            own_away[0] = a.astype(BF16)
            own_away[1] = b.astype(BF16)


def call(kernel, name, out_shape, scalars, arrays, scratch=(), limit=LIMIT):
    vmem = pl.BlockSpec(memory_space=pltpu.VMEM)
    smem = pl.BlockSpec(memory_space=pltpu.SMEM)
    return pl.pallas_call(
        kernel,
        out_shape=out_shape,
        in_specs=[smem] * len(scalars) + [vmem] * len(arrays),
        out_specs=jax.tree.map(lambda _: vmem, out_shape),
        scratch_shapes=list(scratch),
        compiler_params=pltpu.CompilerParams(vmem_limit_bytes=limit),
        name=name,
    )(*scalars, *arrays)


def pack(k_ref, v_ref, own_ref, striped_ref):
    both = jnp.concatenate([k_ref[...].astype(F32), v_ref[...].astype(F32)], 0).T
    own_ref[...] = both.astype(BF16)
    striped_ref[...] = both.reshape(striped_ref.shape).astype(BF16)


def gather(info, picks, banded_ref, out_ref, scr):
    scr[...] = banded_ref[...].astype(F32)
    picked = out_ref.shape[1] // scr.shape[1]
    for d in range(out_ref.shape[0]):
        rows = [scr[block_of(info, picks, d, j)] for j in range(picked)]
        out_ref[d] = jnp.concatenate(rows, 0).astype(BF16)


def scatter(info, picks, landed_ref, out_ref, acc):
    acc[...] = jnp.zeros_like(acc)
    stripe = acc.shape[1]
    for d in range(landed_ref.shape[0]):
        rows = landed_ref[d].astype(F32)
        for j in range(rows.shape[0] // stripe):
            at = block_of(info, picks, d, j)
            acc[at] = acc[at] + rows[j * stripe : (j + 1) * stripe]
    out_ref[...] = acc[...].astype(BF16)


def unpack(mine_ref, got_ref, pair_ref, back_ref, gk_ref, gv_ref):
    total = mine_ref[...] + got_ref[0].astype(F32) + pair_ref[...].astype(F32)
    total = total + back_ref[...].astype(F32).reshape(total.shape)
    both = total.T
    gk_ref[...] = both[: gk_ref.shape[0]]
    gv_ref[...] = both[gk_ref.shape[0] :]


def local(queries, key_states, value_states, block_picks, grad_output):
    row_count = queries.shape[0]
    half_dim = key_states.shape[1]
    head_dim = 2 * half_dim
    z_count = lax.axis_size("z")
    picked = block_picks.shape[2]
    stripe = row_count // z_count
    axes = [lax.axis_index(name) for name in ("core", "pair", "grp", "z")]
    info = jnp.stack(axes + [jnp.int32(lax.axis_size("grp"))]).astype(jnp.int32)
    picks = block_picks.reshape(-1)
    shape = jax.ShapeDtypeStruct
    banded_shape = shape((z_count, stripe, head_dim), BF16)
    striped_shape = shape((z_count, picked * stripe, head_dim), BF16)

    def exchange(x):
        other_core = lax.ppermute(x, "core", SWAP)
        both = lax.ppermute(x, ("core", "pair"), [(i, 3 - i) for i in range(4)])
        other = lax.ppermute(x, "pair", SWAP)
        return x, other, other_core, both

    def across(x):
        return lax.all_to_all(x, "z", split_axis=0, concat_axis=0, tiled=True)

    own, striped = call(
        pack,
        "pack",
        (shape((row_count, head_dim), BF16), banded_shape),
        (),
        (key_states.T, value_states.T),
    )
    banded = across(striped)
    scratch = (pltpu.VMEM(banded_shape.shape, F32),)
    outgoing = call(gather, "gather", striped_shape, (info, picks), (banded,), scratch)
    own, outgoing = lax.optimization_barrier((own, outgoing))
    own, fetched = lax.optimization_barrier((exchange(own), across(outgoing)))
    fetched = exchange(fetched)

    heads = queries.shape[1] // head_dim
    wide = heads * row_count
    many = picked * BLOCK
    p, dp, stats, own_kt, own_vt, q_all, g_all = call(
        functools.partial(own_scores, heads),
        "own_scores",
        (
            shape((BLOCK, wide), F32),
            shape((BLOCK, wide), F32),
            shape((8, wide), F32),
            shape((head_dim, BLOCK), BF16),
            shape((head_dim, BLOCK), BF16),
            shape((wide, head_dim), BF16),
            shape((wide, head_dim), BF16),
        ),
        (info,),
        (queries, grad_output, *own),
        (pltpu.VMEM((BLOCK, head_dim), BF16), pltpu.VMEM((BLOCK, head_dim), BF16)),
        12 << 20,
    )
    mine, theirs, away, low, ds, key_t, value_t, merged = call(
        functools.partial(picked_grads, heads, picked),
        "picked_grads",
        (
            shape(striped_shape.shape, F32),
            shape(striped_shape.shape, F32),
            shape((2, *striped_shape.shape), BF16),
            shape((many, wide), BF16),
            shape((many, wide), BF16),
            shape((head_dim, many), BF16),
            shape((head_dim, many), BF16),
            shape((8, wide), F32),
        ),
        (info, picks),
        (q_all, g_all, stats, *fetched),
        (
            pltpu.VMEM((many, head_dim), BF16),
            pltpu.VMEM((many, head_dim), BF16),
            pltpu.VMEM((many, row_count), F32),
            pltpu.VMEM((many, row_count), F32),
        ),
        18 << 20,
    )

    def to_core(away):
        return lax.ppermute(away, "core", SWAP)

    def to_pair(theirs, got):
        return lax.ppermute((theirs + got[1].astype(F32)).astype(BF16), "pair", SWAP)

    got = to_core(away)
    from_pair = to_pair(theirs, got)
    out, grad_queries, own_mine, own_theirs, own_away = call(
        functools.partial(row_outputs, heads),
        "row_outputs",
        (
            shape((row_count, heads * head_dim), BF16),
            shape((row_count, heads * head_dim), F32),
            shape((row_count, head_dim), F32),
            shape((row_count, head_dim), F32),
            shape((2, row_count, head_dim), BF16),
        ),
        (info,),
        (q_all, g_all, p, dp, merged, own_kt, own_vt, low, ds, key_t, value_t),
        (
            pltpu.VMEM((BLOCK, wide), BF16),
            pltpu.VMEM((BLOCK, wide), BF16),
        ),
        18 << 20,
    )
    going_out = (mine + got[0].astype(F32) + from_pair.astype(F32)).astype(BF16)
    going_out, own_away = lax.optimization_barrier((going_out, own_away))
    landed = across(going_out)
    got = to_core(own_away)
    from_pair = to_pair(own_theirs, got)
    landed, got, from_pair = lax.optimization_barrier((landed, got, from_pair))
    back = across(call(scatter, "scatter", banded_shape, (info, picks), (landed,), scratch))
    grad_k, grad_v = call(
        unpack,
        "unpack",
        (shape((half_dim, row_count), F32),) * 2,
        (),
        (own_mine, got, from_pair, back),
    )
    return out, grad_queries, grad_k.T, grad_v.T


def solution(mesh):
    seq, heads = mesh.devices.shape
    split = Mesh(
        mesh.devices.reshape(seq // 2, 2, heads // 2, 2), ("z", "core", "grp", "pair")
    )
    spec = P(("z", "core"), ("grp", "pair"))
    return jax.shard_map(
        local,
        mesh=split,
        in_specs=(spec, spec, spec, P(), spec),
        out_specs=(spec, spec, spec, spec),
        check_vma=False,
    )
```

time: 193 us -> 187 us (0.969)
  blocking collectives: 65.4 us -> 27.6 us
  waiting for transfers between devices: 51.9 us -> 77.9 us
  Pallas kernels: 11.4 us -> 13.8 us
  starting transfers between devices: 59.1 us -> 61.2 us
    all_to_all x2 -> x1, blocking collectives: 65.4 us -> 27.6 us  [across(): return lax.all_to_all(x, 'z', split_axis=0, concat_axis=0, tiled=True)]
    all_to_all x2 -> x3, waiting for transfers between devices: 35.9 us -> 65.4 us  [across(): return lax.all_to_all(x, 'z', split_axis=0, concat_axis=0, tiled=True)]
    ppermute x2, waiting for transfers between devices: 6.48 us -> 0.01 us  [exchange(): other = lax.ppermute(x, 'pair', SWAP)]
    ppermute x2, waiting for transfers between devices: 0.01 us -> 4.1 us  [exchange(): both = lax.ppermute(x, ('core', 'pair'), [(i, 3 - i) for i in range(4)])]
    all_to_all x2 -> x3, starting transfers between devices: 32.6 us -> 36.4 us  [across(): return lax.all_to_all(x, 'z', split_axis=0, concat_axis=0, tiled=True)]
    pallas_call x5 -> x7, Pallas kernels: 11.4 us -> 13.8 us  [call(): pl.pallas_call(kernel, out_shape=out_shape, in_specs=[smem] * len(scalars...]
    unnamed x11 -> x9, local copies, waits for them, and re-layouts: 2.35 us -> 4.24 us
  transfers between devices with their start and end apart: 12 -> 13, of which waited for: 8 -> 9; matrix products, arithmetic and copies ran while one was open for 0% -> 1% of each run, Pallas kernels for 0% -> 3%
where the time goes in v3:
time: 187 us; the launch traced here: 186 us
  waiting for transfers between devices  77.9 us (42%)
  starting transfers between devices  61.2 us (33%)
  blocking collectives  27.6 us (15%)
  Pallas kernels  13.8 us (7%)
  local copies, waits for them, and re-layouts  4.46 us (2%)
    all_to_all x3, waiting for transfers between devices, across(): return lax.all_to_all(x, 'z', split_axis=0, concat_axis=0, tiled=True)  65.4 us
    all_to_all x3, starting transfers between devices, across(): return lax.all_to_all(x, 'z', split_axis=0, concat_axis=0, tiled=True)  36.4 us
    all_to_all x1, blocking collectives, across(): return lax.all_to_all(x, 'z', split_axis=0, concat_axis=0, tiled=True)  27.6 us
    pallas_call x7, Pallas kernels, call(): pl.pallas_call(kernel, out_shape=out_shape, in_specs=[smem] * len(scalars...  13.8 us
    ppermute x2, starting transfers between devices, exchange(): other = lax.ppermute(x, 'pair', SWAP)  6.96 us
    ppermute x2, waiting for transfers between devices, to_pair(): lax.ppermute((theirs + got[1].astype(F32)).astype(BF16), 'pair', SWAP)  5.93 us
    ppermute x2, starting transfers between devices, exchange(): both = lax.ppermute(x, ('core', 'pair'), [(i, 3 - i) for i in range(4)])  4.92 us
    ppermute x2, starting transfers between devices, to_pair(): lax.ppermute((theirs + got[1].astype(F32)).astype(BF16), 'pair', SWAP)  4.75 us
  transfers between devices with their start and end apart: 13, of which 9 were waited for; matrix products, arithmetic and copies ran while one was open for 1% of the time, Pallas kernels for 3%

profile of v3, /device:TPU:6, one launch (start us, length us, event | category | flops | bytes accessed | tf_op | source)
XLA Modules:
  0.0 186.4 jit_solution(5262667196907334473)
XLA Ops:
  0.6 0.0 copy-start.2
  0.6 0.7 copy-done.2
  1.4 0.0 copy-start.3
  1.4 0.8 copy-done.3
  2.1 0.7 pack.1
  2.9 28.7 %all-to-all-start = ((bf16[32,8,128]{2,1,0:T(8,128)(2,1)}), bf16[32,8,128]{2,1,0:T(8,128)(2,1)S(1)}, u32[]{:S(2)}, u32[]{:S(2)}) async-start(bf16[32,8,128]{2,1,0:T(8,128)(2,1)} %get-tuple-element.41), calls=%async_computation | async-start | bytes 131072 | tf_op jit(solution)/shard_map/all_to_all | solution.py:278
  31.6 0.8 copy.9
  32.5 0.1 reshape.17.picks
  32.6 0.1 stack.19.info
  32.7 24.7 %all-to-all-done.banded_ref = bf16[32,8,128]{2,1,0:T(8,128)(2,1)S(1)} async-done(((bf16[32,8,128]{2,1,0:T(8,128)(2,1)}), bf16[32,8,128]{2,1,0:T(8,128)(2,1)S(1)}, u32[]{:S(2)}, u32[]{:S(2)}) %all-to-all-start) | async-done | bytes 65568 | tf_op jit(solution)/shard_map/all_to_all | solution.py:278
  57.4 1.4 gather.1
  58.8 3.9 %all-to-all-start.1 = ((bf16[32,16,128]{2,1,0:T(8,128)(2,1)}), bf16[32,16,128]{2,1,0:T(8,128)(2,1)S(1)}, u32[]{:S(2)}, u32[]{:S(2)}) async-start(bf16[32,16,128]{2,1,0:T(8,128)(2,1)} %gather.1), calls=%async_computation.1 | async-start | bytes 262144 | tf_op jit(solution)/shard_map/all_to_all | solution.py:278
  62.6 3.5 %collective-permute-start = (bf16[256,128]{1,0:T(8,128)(2,1)S(1)}, bf16[256,128]{1,0:T(8,128)(2,1)S(1)}, u32[]{:S(2)}, u32[]{:S(2)}) collective-permute-start(bf16[256,128]{1,0:T(8,128)(2,1)S(1)} %get-tuple-element.44.own_a), channel_id=1, source_target_pairs={{0,1},{1,0},{2,3},{3,2},{4,5},{5,4},{6,7},{7,6},{8,9},{9,8},{10,11... | collective-permute-start | bytes 196616 | tf_op jit(solution)/shard_map/ppermute | solution.py:274
  66.1 1.9 %collective-permute-start.1 = (bf16[256,128]{1,0:T(8,128)(2,1)S(1)}, bf16[256,128]{1,0:T(8,128)(2,1)S(1)}, u32[]{:S(2)}, u32[]{:S(2)}) collective-permute-start(bf16[256,128]{1,0:T(8,128)(2,1)S(1)} %get-tuple-element.44.own_a), channel_id=1, source_target_pairs={{0,16},{16,0},{1,17},{17,1},{2,18},{18,2},{3,19},{19,3},{4,20},{20... | collective-permute-start | bytes 196616 | tf_op jit(solution)/shard_map/ppermute | solution.py:272
  68.1 2.5 %collective-permute-start.2 = (bf16[256,128]{1,0:T(8,128)(2,1)S(1)}, bf16[256,128]{1,0:T(8,128)(2,1)S(1)}, u32[]{:S(2)}, u32[]{:S(2)}) collective-permute-start(bf16[256,128]{1,0:T(8,128)(2,1)S(1)} %get-tuple-element.44.own_a), channel_id=1, source_target_pairs={{0,17},{1,16},{16,1},{17,0},{2,19},{3,18},{18,3},{19,2},{4,21},{5,... | collective-permute-start | bytes 196616 | tf_op jit(solution)/shard_map/ppermute | solution.py:273
  70.5 0.0 collective-permute-done.own_b
  70.5 0.0 collective-permute-done.1.own_c
  70.5 3.1 %collective-permute-done.2.own_d = bf16[256,128]{1,0:T(8,128)(2,1)S(1)} collective-permute-done((bf16[256,128]{1,0:T(8,128)(2,1)S(1)}, bf16[256,128]{1,0:T(8,128)(2,1)S(1)}, u32[]{:S(2)}, u32[]{:S(2)}) %collective-permute-start.2) | collective-permute-done | bytes 65568 | tf_op jit(solution)/shard_map/ppermute | solution.py:273
  73.7 18.6 %all-to-all-done.1.x_ref = bf16[32,16,128]{2,1,0:T(8,128)(2,1)S(1)} async-done(((bf16[32,16,128]{2,1,0:T(8,128)(2,1)}), bf16[32,16,128]{2,1,0:T(8,128)(2,1)S(1)}, u32[]{:S(2)}, u32[]{:S(2)}) %all-to-all-start.1) | async-done | bytes 131104 | tf_op jit(solution)/shard_map/all_to_all | solution.py:278
  92.2 3.5 %collective-permute-start.3 = (bf16[32,16,128]{2,1,0:T(8,128)(2,1)S(1)}, bf16[32,16,128]{2,1,0:T(8,128)(2,1)S(1)}, u32[]{:S(2)}, u32[]{:S(2)}) collective-permute-start(bf16[32,16,128]{2,1,0:T(8,128)(2,1)S(1)} %all-to-all-done.1.x_ref), channel_id=1, source_target_pairs={{0,1},{1,0},{2,3},{3,2},{4,5},{5,4},{6,7},{7,6},{8,9},{9,8},{10,11... | collective-permute-start | bytes 393224 | tf_op jit(solution)/shard_map/ppermute | solution.py:274
  95.7 1.9 %collective-permute-start.4 = (bf16[32,16,128]{2,1,0:T(8,128)(2,1)S(1)}, bf16[32,16,128]{2,1,0:T(8,128)(2,1)S(1)}, u32[]{:S(2)}, u32[]{:S(2)}) collective-permute-start(bf16[32,16,128]{2,1,0:T(8,128)(2,1)S(1)} %all-to-all-done.1.x_ref), channel_id=1, source_target_pairs={{0,16},{16,0},{1,17},{17,1},{2,18},{18,2},{3,19},{19,3},{4,20},{20... | collective-permute-start | bytes 393224 | tf_op jit(solution)/shard_map/ppermute | solution.py:272
  97.6 2.5 %collective-permute-start.5 = (bf16[32,16,128]{2,1,0:T(8,128)(2,1)S(1)}, bf16[32,16,128]{2,1,0:T(8,128)(2,1)S(1)}, u32[]{:S(2)}, u32[]{:S(2)}) collective-permute-start(bf16[32,16,128]{2,1,0:T(8,128)(2,1)S(1)} %all-to-all-done.1.x_ref), channel_id=1, source_target_pairs={{0,17},{1,16},{16,1},{17,0},{2,19},{3,18},{18,3},{19,2},{4,21},{5,... | collective-permute-start | bytes 393224 | tf_op jit(solution)/shard_map/ppermute | solution.py:273
  100.1 0.0 copy-start
  100.1 0.9 copy-done
  101.1 0.0 copy-start.1
  101.1 0.9 copy-done.1
  102.0 1.6 own_scores.1
  103.6 0.0 collective-permute-done.3.y_ref
  103.7 0.0 collective-permute-done.4.xc_ref
  103.7 1.0 collective-permute-done.5.yc_ref
  104.7 5.2 %picked_grads.1 = (f32[32,16,128]{2,1,0:T(8,128)S(1)}, f32[32,16,128]{2,1,0:T(8,128)S(1)}, bf16[2,32,16,128]{3,2,1,0:T(8,128)(2,1)S(1)}, bf16[1024,1024]{1,0:T(8...) custom-call(s32[5]{0:T(128)S(1)} %stack.19.info, ...), custom_call_target="tpu_custom_call" | custom-call | tf_op jit(solution)/shard_map/picked_grads/pallas_call | solution.py:213
  109.9 2.4 %collective-permute-start.6 = (bf16[2,32,16,128]{3,2,1,0:T(8,128)(2,1)S(1)}, bf16[2,32,16,128]{3,2,1,0:T(8,128)(2,1)S(1)}, u32[]{:S(2)}, u32[]{:S(2)}) collective-permute-start(bf16[2,32,16,128]{3,2,1,0:T(8,128)(2,1)S(1)} %get-tuple-element.65), channel_id=1, source_target_pairs={{0,16},{16,0},{1,17},{17,1},{2,18},{18,2},{3,19},{19,3},{4,20},{20... | collective-permute-start | bytes 786440 | tf_op jit(solution)/shard_map/ppermute | solution.py:339
  112.3 1.1 collective-permute-done.6
  113.5 2.4 %collective-permute-start.7 = (bf16[32,16,128]{2,1,0:T(8,128)(2,1)S(1)}, bf16[32,16,128]{2,1,0:T(8,128)(2,1)S(1)}, u32[]{:S(2)}, u32[]{:S(2)}) collective-permute-start(bf16[32,16,128]{2,1,0:T(8,128)(2,1)S(1)} %fusion), channel_id=1, source_target_pairs={{0,1},{1,0},{2,3},{3,2},{4,5},{5,4},{6,7},{7,6},{8,9},{9,8},{10,11... | collective-permute-start | bytes 393224 | tf_op jit(solution)/shard_map/ppermute | solution.py:342
  115.9 3.1 %row_outputs.1 = (bf16[256,512]{1,0:T(8,128)(2,1)}, f32[256,512]{1,0:T(8,128)}, f32[256,128]{1,0:T(8,128)S(1)}, f32[256,128]{1,0:T(8,128)S(1)}, bf16[2,256,128]{2,1,0:T(8,128)(2,1)S(1)}) custom-call(s32[5]{0:T(128)S(1)} %stack.19.info, bf16[1024,128]{1,0:T(8,128)(2,1)S(1)} %get-tuple-element.48.q_all, bf16[1024,128]{1,0:T(8,128)(2,1)S(1)} %get-tuple-element.49.g_all, ...), custom_call_target="tpu_custom_call" | custom-call | tf_op jit(solution)/shard_map/row_outputs/pallas_call | solution.py:213
  119.0 2.1 %collective-permute-done.7 = bf16[32,16,128]{2,1,0:T(8,128)(2,1)S(1)} collective-permute-done((bf16[32,16,128]{2,1,0:T(8,128)(2,1)S(1)}, bf16[32,16,128]{2,1,0:T(8,128)(2,1)S(1)}, u32[]{:S(2)}, u32[]{:S(2)}) %collective-permute-start.7) | collective-permute-done | bytes 131104 | tf_op jit(solution)/shard_map/ppermute | solution.py:342
  121.2 0.7 fusion.2
  121.8 3.8 %all-to-all-start.2 = ((bf16[32,16,128]{2,1,0:T(8,128)(2,1)}), bf16[32,16,128]{2,1,0:T(8,128)(2,1)S(1)}, u32[]{:S(2)}, u32[]{:S(2)}) async-start(bf16[32,16,128]{2,1,0:T(8,128)(2,1)} %fusion.2), calls=%async_computation.2 | async-start | bytes 262144 | tf_op jit(solution)/shard_map/all_to_all | solution.py:278
  125.7 1.9 %collective-permute-start.8 = (bf16[2,256,128]{2,1,0:T(8,128)(2,1)S(1)}, bf16[2,256,128]{2,1,0:T(8,128)(2,1)S(1)}, u32[]{:S(2)}, u32[]{:S(2)}) collective-permute-start(bf16[2,256,128]{2,1,0:T(8,128)(2,1)S(1)} %get-tuple-element.69), channel_id=1, source_target_pairs={{0,16},{16,0},{1,17},{17,1},{2,18},{18,2},{3,19},{19,3},{4,20},{20... | collective-permute-start | bytes 393224 | tf_op jit(solution)/shard_map/ppermute | solution.py:339
  127.6 1.3 collective-permute-done.8.got_ref
  129.0 2.4 %collective-permute-start.9 = (bf16[256,128]{1,0:T(8,128)(2,1)S(1)}, bf16[256,128]{1,0:T(8,128)(2,1)S(1)}, u32[]{:S(2)}, u32[]{:S(2)}) collective-permute-start(bf16[256,128]{1,0:T(8,128)(2,1)S(1)} %fusion.3), channel_id=1, source_target_pairs={{0,1},{1,0},{2,3},{3,2},{4,5},{5,4},{6,7},{7,6},{8,9},{9,8},{10,11... | collective-permute-start | bytes 196616 | tf_op jit(solution)/shard_map/ppermute | solution.py:342
  131.3 3.8 %collective-permute-done.9.pair_ref = bf16[256,128]{1,0:T(8,128)(2,1)S(1)} collective-permute-done((bf16[256,128]{1,0:T(8,128)(2,1)S(1)}, bf16[256,128]{1,0:T(8,128)(2,1)S(1)}, u32[]{:S(2)}, u32[]{:S(2)}) %collective-permute-start.9) | collective-permute-done | bytes 65568 | tf_op jit(solution)/shard_map/ppermute | solution.py:342
  135.1 22.1 %all-to-all-done.2.landed_ref = bf16[32,16,128]{2,1,0:T(8,128)(2,1)S(1)} async-done(((bf16[32,16,128]{2,1,0:T(8,128)(2,1)}), bf16[32,16,128]{2,1,0:T(8,128)(2,1)S(1)}, u32[]{:S(2)}, u32[]{:S(2)}) %all-to-all-start.2) | async-done | bytes 131104 | tf_op jit(solution)/shard_map/all_to_all | solution.py:278
  157.2 0.9 scatter.1
  158.1 27.6 %all_to_all.20.back_ref = bf16[32,8,128]{2,1,0:T(8,128)(2,1)S(1)} all-to-all(bf16[32,8,128]{2,1,0:T(8,128)(2,1)S(1)} %scatter.1), channel_id=1, replica_groups=mesh['z'=32,'core'=2,'grp'=8,'pair'=2] {'z'}, dimensions={0} | all-to-all | bytes 131072 | tf_op jit(solution)/shard_map/all_to_all | solution.py:278
  185.7 0.7 unpack.1
  (2 shorter events, 0.0 us)
Async XLA Ops:
  0.6 0.8 copy-start.2
  1.4 0.8 copy-start.3
  2.9 54.5 %all-to-all-start = ((bf16[32,8,128]{2,1,0:T(8,128)(2,1)}), bf16[32,8,128]{2,1,0:T(8,128)(2,1)S(1)}, u32[]{:S(2)}, u32[]{:S(2)}) async-start(bf16[32,8,128]{2,1,0:T(8,128)(2,1)} %get-tuple-element.41), calls=%async_computation | async-start | bytes 131072 | tf_op jit(solution)/shard_map/all_to_all | solution.py:278
  58.8 33.5 %all-to-all-start.1 = ((bf16[32,16,128]{2,1,0:T(8,128)(2,1)}), bf16[32,16,128]{2,1,0:T(8,128)(2,1)S(1)}, u32[]{:S(2)}, u32[]{:S(2)}) async-start(bf16[32,16,128]{2,1,0:T(8,128)(2,1)} %gather.1), calls=%async_computation.1 | async-start | bytes 262144 | tf_op jit(solution)/shard_map/all_to_all | solution.py:278
  62.6 7.9 %collective-permute-start = (bf16[256,128]{1,0:T(8,128)(2,1)S(1)}, bf16[256,128]{1,0:T(8,128)(2,1)S(1)}, u32[]{:S(2)}, u32[]{:S(2)}) collective-permute-start(bf16[256,128]{1,0:T(8,128)(2,1)S(1)} %get-tuple-element.44.own_a), channel_id=1, source_target_pairs={{0,1},{1,0},{2,3},{3,2},{4,5},{5,4},{6,7},{7,6},{8,9},{9,8},{10,11... | collective-permute-start | bytes 196616 | tf_op jit(solution)/shard_map/ppermute | solution.py:274
  66.1 4.4 %collective-permute-start.1 = (bf16[256,128]{1,0:T(8,128)(2,1)S(1)}, bf16[256,128]{1,0:T(8,128)(2,1)S(1)}, u32[]{:S(2)}, u32[]{:S(2)}) collective-permute-start(bf16[256,128]{1,0:T(8,128)(2,1)S(1)} %get-tuple-element.44.own_a), channel_id=1, source_target_pairs={{0,16},{16,0},{1,17},{17,1},{2,18},{18,2},{3,19},{19,3},{4,20},{20... | collective-permute-start | bytes 196616 | tf_op jit(solution)/shard_map/ppermute | solution.py:272
  68.1 5.6 %collective-permute-start.2 = (bf16[256,128]{1,0:T(8,128)(2,1)S(1)}, bf16[256,128]{1,0:T(8,128)(2,1)S(1)}, u32[]{:S(2)}, u32[]{:S(2)}) collective-permute-start(bf16[256,128]{1,0:T(8,128)(2,1)S(1)} %get-tuple-element.44.own_a), channel_id=1, source_target_pairs={{0,17},{1,16},{16,1},{17,0},{2,19},{3,18},{18,3},{19,2},{4,21},{5,... | collective-permute-start | bytes 196616 | tf_op jit(solution)/shard_map/ppermute | solution.py:273
  92.2 11.4 %collective-permute-start.3 = (bf16[32,16,128]{2,1,0:T(8,128)(2,1)S(1)}, bf16[32,16,128]{2,1,0:T(8,128)(2,1)S(1)}, u32[]{:S(2)}, u32[]{:S(2)}) collective-permute-start(bf16[32,16,128]{2,1,0:T(8,128)(2,1)S(1)} %all-to-all-done.1.x_ref), channel_id=1, source_target_pairs={{0,1},{1,0},{2,3},{3,2},{4,5},{5,4},{6,7},{7,6},{8,9},{9,8},{10,11... | collective-permute-start | bytes 393224 | tf_op jit(solution)/shard_map/ppermute | solution.py:274
  95.7 7.9 %collective-permute-start.4 = (bf16[32,16,128]{2,1,0:T(8,128)(2,1)S(1)}, bf16[32,16,128]{2,1,0:T(8,128)(2,1)S(1)}, u32[]{:S(2)}, u32[]{:S(2)}) collective-permute-start(bf16[32,16,128]{2,1,0:T(8,128)(2,1)S(1)} %all-to-all-done.1.x_ref), channel_id=1, source_target_pairs={{0,16},{16,0},{1,17},{17,1},{2,18},{18,2},{3,19},{19,3},{4,20},{20... | collective-permute-start | bytes 393224 | tf_op jit(solution)/shard_map/ppermute | solution.py:272
  97.6 7.0 %collective-permute-start.5 = (bf16[32,16,128]{2,1,0:T(8,128)(2,1)S(1)}, bf16[32,16,128]{2,1,0:T(8,128)(2,1)S(1)}, u32[]{:S(2)}, u32[]{:S(2)}) collective-permute-start(bf16[32,16,128]{2,1,0:T(8,128)(2,1)S(1)} %all-to-all-done.1.x_ref), channel_id=1, source_target_pairs={{0,17},{1,16},{16,1},{17,0},{2,19},{3,18},{18,3},{19,2},{4,21},{5,... | collective-permute-start | bytes 393224 | tf_op jit(solution)/shard_map/ppermute | solution.py:273
  100.1 1.0 copy-start
  101.1 0.9 copy-start.1
  109.9 3.6 %collective-permute-start.6 = (bf16[2,32,16,128]{3,2,1,0:T(8,128)(2,1)S(1)}, bf16[2,32,16,128]{3,2,1,0:T(8,128)(2,1)S(1)}, u32[]{:S(2)}, u32[]{:S(2)}) collective-permute-start(bf16[2,32,16,128]{3,2,1,0:T(8,128)(2,1)S(1)} %get-tuple-element.65), channel_id=1, source_target_pairs={{0,16},{16,0},{1,17},{17,1},{2,18},{18,2},{3,19},{19,3},{4,20},{20... | collective-permute-start | bytes 786440 | tf_op jit(solution)/shard_map/ppermute | solution.py:339
  113.5 7.7 %collective-permute-start.7 = (bf16[32,16,128]{2,1,0:T(8,128)(2,1)S(1)}, bf16[32,16,128]{2,1,0:T(8,128)(2,1)S(1)}, u32[]{:S(2)}, u32[]{:S(2)}) collective-permute-start(bf16[32,16,128]{2,1,0:T(8,128)(2,1)S(1)} %fusion), channel_id=1, source_target_pairs={{0,1},{1,0},{2,3},{3,2},{4,5},{5,4},{6,7},{7,6},{8,9},{9,8},{10,11... | collective-permute-start | bytes 393224 | tf_op jit(solution)/shard_map/ppermute | solution.py:342
  121.8 35.4 %all-to-all-start.2 = ((bf16[32,16,128]{2,1,0:T(8,128)(2,1)}), bf16[32,16,128]{2,1,0:T(8,128)(2,1)S(1)}, u32[]{:S(2)}, u32[]{:S(2)}) async-start(bf16[32,16,128]{2,1,0:T(8,128)(2,1)} %fusion.2), calls=%async_computation.2 | async-start | bytes 262144 | tf_op jit(solution)/shard_map/all_to_all | solution.py:278
  125.7 3.2 %collective-permute-start.8 = (bf16[2,256,128]{2,1,0:T(8,128)(2,1)S(1)}, bf16[2,256,128]{2,1,0:T(8,128)(2,1)S(1)}, u32[]{:S(2)}, u32[]{:S(2)}) collective-permute-start(bf16[2,256,128]{2,1,0:T(8,128)(2,1)S(1)} %get-tuple-element.69), channel_id=1, source_target_pairs={{0,16},{16,0},{1,17},{17,1},{2,18},{18,2},{3,19},{19,3},{4,20},{20... | collective-permute-start | bytes 393224 | tf_op jit(solution)/shard_map/ppermute | solution.py:339
  129.0 6.2 %collective-permute-start.9 = (bf16[256,128]{1,0:T(8,128)(2,1)S(1)}, bf16[256,128]{1,0:T(8,128)(2,1)S(1)}, u32[]{:S(2)}, u32[]{:S(2)}) collective-permute-start(bf16[256,128]{1,0:T(8,128)(2,1)S(1)} %fusion.3), channel_id=1, source_target_pairs={{0,1},{1,0},{2,3},{3,2},{4,5},{5,4},{6,7},{7,6},{8,9},{9,8},{10,11... | collective-permute-start | bytes 196616 | tf_op jit(solution)/shard_map/ppermute | solution.py:342

commit v4 on v3

--- a/solution.py
+++ b/solution.py
@@ -9,6 +9,7 @@
 
 BLOCK = 512
 NEGATIVE = -1e30
+NO_KEY = -1e4
 SWAP = [(0, 1), (1, 0)]
 LOG2_E = 1.4426950408889634
 F32 = jnp.float32
@@ -52,15 +53,13 @@
     return jnp.where(is_low, low, high), jnp.where(is_low, high, low)
 
 
-def load_tiles(pieces, is_low, key_scr, value_scr, key_t, value_t):
+def load_tiles(pieces, is_low, key_scr, value_scr):
     rows = pieces[0][0].shape[0]
     for i, (own, other) in enumerate(pieces):
         k, v = split_features(is_low, own, other)
         at = slice(i * rows, (i + 1) * rows)
         key_scr[at, :] = k.astype(BF16)
         value_scr[at, :] = v.astype(BF16)
-        key_t[:, at] = k.T.astype(BF16)
-        value_t[:, at] = v.T.astype(BF16)
 
 
 def spans_of(ref, rows):
@@ -68,21 +67,17 @@
 
 
 def own_scores(
-    heads, info, q_ref, g_ref, own_a, own_b, own_c, own_d,
-    p_ref, dp_ref, stats, key_t, value_t, q_all, g_all, key_scr, value_scr,
+    heads, info, q_all, g_all, own_a, own_b, own_c, own_d,
+    p_ref, stats, key_scr, value_scr,
 ):
-    rows = q_ref.shape[0]
-    dim = q_ref.shape[1] // heads
+    rows, dim = q_all.shape[0] // heads, q_all.shape[1]
     rate = dim ** (-0.5) * LOG2_E
     pieces = [(own_a, own_b), (own_c, own_d)]
     pieces = [tuple(ref[...].astype(F32) for ref in piece) for piece in pieces]
-    load_tiles(pieces, info[1] == 0, key_scr, value_scr, key_t, value_t)
+    load_tiles(pieces, info[1] == 0, key_scr, value_scr)
     for h in range(heads):
-        q = q_ref[:, h * dim : (h + 1) * dim]
-        g = g_ref[:, h * dim : (h + 1) * dim]
         col = slice(h * rows, (h + 1) * rows)
-        q_all[col, :] = q
-        g_all[col, :] = g
+        q, g = q_all[col, :], g_all[col, :]
         spans = spans_of(key_scr, rows)
         s = dot(key_scr[spans[0], :], q, NT)
         earlier = lax.broadcasted_iota(jnp.int32, s.shape, 0) <= lax.broadcasted_iota(
@@ -100,7 +95,6 @@
             p = jnp.exp2((p_ref[span, col] - top) * rate)
             dp = dot(value_scr[span, :], g, NT)
             p_ref[span, col] = p
-            dp_ref[span, col] = dp
             total = total + jnp.sum(p, axis=0, keepdims=True)
             delta = delta + jnp.sum(p * dp, axis=0, keepdims=True)
         stats[0:1, col] = top
@@ -110,8 +104,7 @@
 
 def picked_grads(
     heads, picked, info, picks, q_all, g_all, stats, x_ref, y_ref, xc_ref, yc_ref,
-    mine_ref, theirs_ref, away_ref, low_ref, ds_ref, key_t, value_t, merged,
-    key_scr, value_scr, s_scr, dp_scr,
+    mine_ref, theirs_ref, away_ref, low_ref, ds_ref, key_scr, value_scr, merged, s_scr, dp_scr,
 ):
     rows, dim = q_all.shape[0] // heads, q_all.shape[1]
     scaling = dim ** (-0.5)
@@ -126,8 +119,9 @@
     pieces = [
         tuple(part[:, j].reshape(rows, dim) for part in half) for j in range(picked) for half in halves
     ]
-    load_tiles(pieces, is_low, key_scr, value_scr, key_t, value_t)
+    load_tiles(pieces, is_low, key_scr, value_scr)
     spans = spans_of(key_scr, rows)
+    usable = [offset_of(info, picks, info[3], i // 2) <= info[3] for i in range(len(spans))]
     for h in range(heads):
         col = slice(h * rows, (h + 1) * rows)
         q, g = q_all[col, :], g_all[col, :]
@@ -135,14 +129,16 @@
         top = own_top
         for i, span in enumerate(spans):
             s = dot(key_scr[span, :], q, NT)
-            s = jnp.where(offset_of(info, picks, info[3], i // 2) <= info[3], s, NEGATIVE)
             s_scr[span, :] = s
-            top = jnp.maximum(top, jnp.max(s, axis=0, keepdims=True))
+            most = jnp.max(s, axis=0, keepdims=True)
+            top = jnp.where(usable[i], jnp.maximum(top, most), top)
         shift = jnp.exp2((own_top - top) * rate)
         total = stats[1:2, col] * shift
         delta = stats[2:3, col] * shift
-        for span in spans:
-            p = jnp.exp2((s_scr[span, :] - top) * rate)
+        for i, span in enumerate(spans):
+            slope = jnp.where(usable[i], rate, 0.0)
+            floor = jnp.where(usable[i], top * -rate, NO_KEY)
+            p = jnp.exp2(s_scr[span, :] * slope + floor)
             dp = dot(value_scr[span, :], g, NT)
             s_scr[span, :] = p
             dp_scr[span, :] = dp
@@ -177,23 +173,25 @@
 
 
 def row_outputs(
-    heads, info, q_all, g_all, p_ref, dp_ref, merged, own_kt, own_vt, low_ref, ds_ref, key_t, value_t,
+    heads, info, q_all, g_all, p_ref, merged, own_keys, own_values, low_ref, ds_ref, keys, values,
     out_ref, dq_ref, own_mine, own_theirs, own_away, low_scr, ds_scr,
 ):
     rows, dim = q_all.shape[0] // heads, q_all.shape[1]
     scaling = dim ** (-0.5)
     spans = spans_of(p_ref, rows)
+    own_kt, own_vt, key_t, value_t = (ref[...].T for ref in (own_keys, own_values, keys, values))
     for h in range(heads):
         lane = slice(h * dim, (h + 1) * dim)
         col = slice(h * rows, (h + 1) * rows)
         scale, delta = merged[0:1, col], merged[1:2, col]
         for span in spans:
             p = p_ref[span, col] * scale
+            dp = dot(own_values[span, :], g_all[col, :], NT)
             low_scr[span, col] = p.astype(BF16)
-            ds_scr[span, col] = (p * (dp_ref[span, col] - delta)).astype(BF16)
-        out_t = dot(own_vt[...], low_scr[:, col]) + dot(value_t[...], low_ref[:, col])
+            ds_scr[span, col] = (p * (dp - delta)).astype(BF16)
+        out_t = dot(own_vt, low_scr[:, col]) + dot(value_t, low_ref[:, col])
         out_ref[:, lane] = out_t.T.astype(BF16)
-        dq_t = dot(own_kt[...], ds_scr[:, col]) + dot(key_t[...], ds_ref[:, col])
+        dq_t = dot(own_kt, ds_scr[:, col]) + dot(key_t, ds_ref[:, col])
         dq_ref[:, lane] = dq_t.T * scaling
     for i, span in enumerate(spans):
         k = dot(ds_scr[span, :], q_all[...]) * scaling
@@ -207,13 +205,13 @@
             own_away[1] = b.astype(BF16)
 
 
-def call(kernel, name, out_shape, scalars, arrays, scratch=(), limit=LIMIT):
+def call(kernel, name, out_shape, scalars, arrays, scratch=(), limit=LIMIT, space=pltpu.VMEM):
     vmem = pl.BlockSpec(memory_space=pltpu.VMEM)
     smem = pl.BlockSpec(memory_space=pltpu.SMEM)
     return pl.pallas_call(
         kernel,
         out_shape=out_shape,
-        in_specs=[smem] * len(scalars) + [vmem] * len(arrays),
+        in_specs=[smem] * len(scalars) + [pl.BlockSpec(memory_space=space)] * len(arrays),
         out_specs=jax.tree.map(lambda _: vmem, out_shape),
         scratch_shapes=list(scratch),
         compiler_params=pltpu.CompilerParams(vmem_limit_bytes=limit),
@@ -221,10 +219,36 @@
     )(*scalars, *arrays)
 
 
-def pack(k_ref, v_ref, own_ref, striped_ref):
-    both = jnp.concatenate([k_ref[...].astype(F32), v_ref[...].astype(F32)], 0).T
+def pack(k_ref, v_ref, own_ref, striped_ref, k_scr, v_scr, sems):
+    copies = [
+        pltpu.make_async_copy(k_ref, k_scr, sems.at[0]),
+        pltpu.make_async_copy(v_ref, v_scr, sems.at[1]),
+    ]
+    for copy in copies:
+        copy.start()
+    for copy in copies:
+        copy.wait()
+    both = jnp.concatenate([k_scr[...].astype(F32), v_scr[...].astype(F32)], 0).T
     own_ref[...] = both.astype(BF16)
     striped_ref[...] = both.reshape(striped_ref.shape).astype(BF16)
+
+
+def stack_heads(q_ref, g_ref, q_all, g_all, sems):
+    rows, dim = q_ref.shape[0], q_all.shape[1]
+    heads = q_all.shape[0] // rows
+    copies = [
+        pltpu.make_async_copy(
+            whole.at[:, pl.ds(h * dim, dim)],
+            stacked.at[pl.ds(h * rows, rows), :],
+            sems.at[i * heads + h],
+        )
+        for i, (whole, stacked) in enumerate(((q_ref, q_all), (g_ref, g_all)))
+        for h in range(heads)
+    ]
+    for copy in copies:
+        copy.start()
+    for copy in copies:
+        copy.wait()
 
 
 def gather(info, picks, banded_ref, out_ref, scr):
@@ -268,11 +292,14 @@
     banded_shape = shape((z_count, stripe, head_dim), BF16)
     striped_shape = shape((z_count, picked * stripe, head_dim), BF16)
 
-    def exchange(x):
-        other_core = lax.ppermute(x, "core", SWAP)
-        both = lax.ppermute(x, ("core", "pair"), [(i, 3 - i) for i in range(4)])
-        other = lax.ppermute(x, "pair", SWAP)
-        return x, other, other_core, both
+    def in_hbm(x):
+        return pltpu.with_memory_space_constraint(x, pltpu.HBM)
+
+    def to_pair(x):
+        return lax.ppermute(x, "pair", SWAP)
+
+    def to_core(x):
+        return lax.ppermute(x, "core", SWAP)
 
     def across(x):
         return lax.all_to_all(x, "z", split_axis=0, concat_axis=0, tiled=True)
@@ -282,36 +309,52 @@
         "pack",
         (shape((row_count, head_dim), BF16), banded_shape),
         (),
-        (key_states.T, value_states.T),
-    )
-    banded = across(striped)
-    scratch = (pltpu.VMEM(banded_shape.shape, F32),)
-    outgoing = call(gather, "gather", striped_shape, (info, picks), (banded,), scratch)
-    own, outgoing = lax.optimization_barrier((own, outgoing))
-    own, fetched = lax.optimization_barrier((exchange(own), across(outgoing)))
-    fetched = exchange(fetched)
-
+        tuple(in_hbm(x.T) for x in (key_states, value_states)),
+        (
+            pltpu.VMEM((half_dim, row_count), BF16),
+            pltpu.VMEM((half_dim, row_count), BF16),
+            pltpu.SemaphoreType.DMA((2,)),
+        ),
+        space=pltpu.HBM,
+    )
     heads = queries.shape[1] // head_dim
     wide = heads * row_count
     many = picked * BLOCK
-    p, dp, stats, own_kt, own_vt, q_all, g_all = call(
+    banded = across(striped)
+    own_pair = to_pair(own)
+    q_all, g_all = call(
+        stack_heads,
+        "stack_heads",
+        (shape((wide, head_dim), BF16),) * 2,
+        (),
+        tuple(in_hbm(x) for x in (queries, grad_output)),
+        (pltpu.SemaphoreType.DMA((2 * heads,)),),
+        space=pltpu.HBM,
+    )
+    banded, own, own_pair, q_all, g_all = lax.optimization_barrier(
+        (banded, own, own_pair, q_all, g_all)
+    )
+    scratch = (pltpu.VMEM(banded_shape.shape, F32),)
+    outgoing = call(gather, "gather", striped_shape, (info, picks), (banded,), scratch)
+    outgoing, own, own_pair = lax.optimization_barrier((outgoing, own, own_pair))
+    fetched = across(outgoing)
+    own_block = call(
         functools.partial(own_scores, heads),
         "own_scores",
         (
             shape((BLOCK, wide), F32),
-            shape((BLOCK, wide), F32),
             shape((8, wide), F32),
-            shape((head_dim, BLOCK), BF16),
-            shape((head_dim, BLOCK), BF16),
-            shape((wide, head_dim), BF16),
-            shape((wide, head_dim), BF16),
+            shape((BLOCK, head_dim), BF16),
+            shape((BLOCK, head_dim), BF16),
         ),
         (info,),
-        (queries, grad_output, *own),
-        (pltpu.VMEM((BLOCK, head_dim), BF16), pltpu.VMEM((BLOCK, head_dim), BF16)),
-        12 << 20,
-    )
-    mine, theirs, away, low, ds, key_t, value_t, merged = call(
+        (q_all, g_all, own, own_pair, to_core(own), to_core(own_pair)),
+        limit=6 << 20,
+    )
+    fetched, (p, stats, own_keys, own_values) = lax.optimization_barrier((fetched, own_block))
+    fetched_pair = to_pair(fetched)
+    fetched = (fetched, fetched_pair, to_core(fetched), to_core(fetched_pair))
+    mine, theirs, away, low, ds, keys, values, merged = call(
         functools.partial(picked_grads, heads, picked),
         "picked_grads",
         (
@@ -320,29 +363,24 @@
             shape((2, *striped_shape.shape), BF16),
             shape((many, wide), BF16),
             shape((many, wide), BF16),
-            shape((head_dim, many), BF16),
-            shape((head_dim, many), BF16),
+            shape((many, head_dim), BF16),
+            shape((many, head_dim), BF16),
             shape((8, wide), F32),
         ),
         (info, picks),
         (q_all, g_all, stats, *fetched),
         (
-            pltpu.VMEM((many, head_dim), BF16),
-            pltpu.VMEM((many, head_dim), BF16),
             pltpu.VMEM((many, row_count), F32),
             pltpu.VMEM((many, row_count), F32),
         ),
-        18 << 20,
-    )
-
-    def to_core(away):
-        return lax.ppermute(away, "core", SWAP)
-
-    def to_pair(theirs, got):
-        return lax.ppermute((theirs + got[1].astype(F32)).astype(BF16), "pair", SWAP)
+        8 << 20,
+    )
+
+    def summed(theirs, got):
+        return (theirs + got[1].astype(F32)).astype(BF16)
 
     got = to_core(away)
-    from_pair = to_pair(theirs, got)
+    from_pair = to_pair(summed(theirs, got))
     out, grad_queries, own_mine, own_theirs, own_away = call(
         functools.partial(row_outputs, heads),
         "row_outputs",
@@ -354,18 +392,18 @@
             shape((2, row_count, head_dim), BF16),
         ),
         (info,),
-        (q_all, g_all, p, dp, merged, own_kt, own_vt, low, ds, key_t, value_t),
+        (q_all, g_all, p, merged, own_keys, own_values, low, ds, keys, values),
         (
             pltpu.VMEM((BLOCK, wide), BF16),
             pltpu.VMEM((BLOCK, wide), BF16),
         ),
-        18 << 20,
+        8 << 20,
     )
     going_out = (mine + got[0].astype(F32) + from_pair.astype(F32)).astype(BF16)
     going_out, own_away = lax.optimization_barrier((going_out, own_away))
     landed = across(going_out)
     got = to_core(own_away)
-    from_pair = to_pair(own_theirs, got)
+    from_pair = to_pair(summed(own_theirs, got))
     landed, got, from_pair = lax.optimization_barrier((landed, got, from_pair))
     back = across(call(scatter, "scatter", banded_shape, (info, picks), (landed,), scratch))
     grad_k, grad_v = call(

time: 187 us -> 184 us (0.984)
  waiting for transfers between devices: 77.9 us -> 74.4 us
  local copies, waits for them, and re-layouts: 4.46 us -> 1.06 us
  Pallas kernels: 13.8 us -> 15.9 us
    unnamed x9 -> x1, local copies, waits for them, and re-layouts: 4.24 us -> 0.83 us
    ppermute x10, waiting for transfers between devices: 12.5 us -> 9.78 us  [the longest x4 4.93 us: to_pair(): return lax.ppermute(x, 'pair', SWAP)]
    pallas_call x7 -> x8, Pallas kernels: 13.8 us -> 15.9 us  [call(): pl.pallas_call(kernel, out_shape=out_shape, in_specs=[smem] * len(scalars...]
  transfers between devices with their start and end apart: 13 -> 13, of which waited for: 9 -> 11; matrix products, arithmetic and copies ran while one was open for 1% -> 1% of each run, Pallas kernels for 3% -> 3%
where the time goes in v4:
time: 184 us; the launch traced here: 183 us
  waiting for transfers between devices  74.4 us (40%)
  starting transfers between devices  62.5 us (34%)
  blocking collectives  27.6 us (15%)
  Pallas kernels  15.9 us (9%)
    all_to_all x3, waiting for transfers between devices, across(): return lax.all_to_all(x, 'z', split_axis=0, concat_axis=0, tiled=True)  64.6 us
    all_to_all x3, starting transfers between devices, across(): return lax.all_to_all(x, 'z', split_axis=0, concat_axis=0, tiled=True)  36.4 us
    all_to_all x1, blocking collectives, across(): return lax.all_to_all(x, 'z', split_axis=0, concat_axis=0, tiled=True)  27.6 us
    pallas_call x8, Pallas kernels, call(): pl.pallas_call(kernel, out_shape=out_shape, in_specs=[smem] * len(scalars...  15.9 us
    ppermute x4, starting transfers between devices, to_pair(): return lax.ppermute(x, 'pair', SWAP)  13.9 us
    ppermute x6, starting transfers between devices, to_core(): return lax.ppermute(x, 'core', SWAP)  12.1 us
    ppermute x4, waiting for transfers between devices, to_pair(): return lax.ppermute(x, 'pair', SWAP)  4.93 us
    ppermute x6, waiting for transfers between devices, to_core(): return lax.ppermute(x, 'core', SWAP)  4.86 us
  transfers between devices with their start and end apart: 13, of which 11 were waited for; matrix products, arithmetic and copies ran while one was open for 1% of the time, Pallas kernels for 3%

profile of v4, /device:TPU:6, one launch (start us, length us, event | category | flops | bytes accessed | tf_op | source)
XLA Modules:
  0.0 183.0 jit_solution(1392293896069016990)
XLA Ops:
  0.6 1.5 pack.1
  2.2 28.7 %all-to-all-start = ((bf16[32,8,128]{2,1,0:T(8,128)(2,1)}), bf16[32,8,128]{2,1,0:T(8,128)(2,1)S(1)}, u32[]{:S(2)}, u32[]{:S(2)}) async-start(bf16[32,8,128]{2,1,0:T(8,128)(2,1)} %get-tuple-element.45), calls=%async_computation | async-start | bytes 131072 | tf_op jit(solution)/shard_map/all_to_all | solution.py:305
  30.9 3.5 %collective-permute-start = (bf16[256,128]{1,0:T(8,128)(2,1)S(1)}, bf16[256,128]{1,0:T(8,128)(2,1)S(1)}, u32[]{:S(2)}, u32[]{:S(2)}) collective-permute-start(bf16[256,128]{1,0:T(8,128)(2,1)S(1)} %get-tuple-element.55.own_a), channel_id=1, source_target_pairs={{0,1},{1,0},{2,3},{3,2},{4,5},{5,4},{6,7},{7,6},{8,9},{9,8},{10,11... | collective-permute-start | bytes 196616 | tf_op jit(solution)/shard_map/ppermute | solution.py:299
  34.4 0.8 copy.9
  35.2 0.1 reshape.17.picks
  35.4 1.1 stack_heads.1
  36.5 0.1 stack.19.info
  36.6 0.4 collective-permute-done.own_b
  37.1 19.6 %all-to-all-done.banded_ref = bf16[32,8,128]{2,1,0:T(8,128)(2,1)S(1)} async-done(((bf16[32,8,128]{2,1,0:T(8,128)(2,1)}), bf16[32,8,128]{2,1,0:T(8,128)(2,1)S(1)}, u32[]{:S(2)}, u32[]{:S(2)}) %all-to-all-start) | async-done | bytes 65568 | tf_op jit(solution)/shard_map/all_to_all | solution.py:305
  56.7 1.4 gather.1
  58.1 3.9 %all-to-all-start.1 = ((bf16[32,16,128]{2,1,0:T(8,128)(2,1)}), bf16[32,16,128]{2,1,0:T(8,128)(2,1)S(1)}, u32[]{:S(2)}, u32[]{:S(2)}) async-start(bf16[32,16,128]{2,1,0:T(8,128)(2,1)} %gather.1), calls=%async_computation.1 | async-start | bytes 262144 | tf_op jit(solution)/shard_map/all_to_all | solution.py:305
  61.9 1.9 %collective-permute-start.1 = (bf16[256,128]{1,0:T(8,128)(2,1)S(1)}, bf16[256,128]{1,0:T(8,128)(2,1)S(1)}, u32[]{:S(2)}, u32[]{:S(2)}) collective-permute-start(bf16[256,128]{1,0:T(8,128)(2,1)S(1)} %get-tuple-element.55.own_a), channel_id=1, source_target_pairs={{0,16},{16,0},{1,17},{17,1},{2,18},{18,2},{3,19},{19,3},{4,20},{20... | collective-permute-start | bytes 196616 | tf_op jit(solution)/shard_map/ppermute | solution.py:302
  63.9 2.4 %collective-permute-start.2 = (bf16[256,128]{1,0:T(8,128)(2,1)S(1)}, bf16[256,128]{1,0:T(8,128)(2,1)S(1)}, u32[]{:S(2)}, u32[]{:S(2)}) collective-permute-start(bf16[256,128]{1,0:T(8,128)(2,1)S(1)} %collective-permute-done.own_b), channel_id=1, source_target_pairs={{0,16},{16,0},{1,17},{17,1},{2,18},{18,2},{3,19},{19,3},{4,20},{20... | collective-permute-start | bytes 196616 | tf_op jit(solution)/shard_map/ppermute | solution.py:302
  66.3 0.0 collective-permute-done.1.own_c
  66.3 0.9 collective-permute-done.2.own_d
  67.2 1.5 own_scores.1
  68.6 22.9 %all-to-all-done.1.x_ref = bf16[32,16,128]{2,1,0:T(8,128)(2,1)S(1)} async-done(((bf16[32,16,128]{2,1,0:T(8,128)(2,1)}), bf16[32,16,128]{2,1,0:T(8,128)(2,1)S(1)}, u32[]{:S(2)}, u32[]{:S(2)}) %all-to-all-start.1) | async-done | bytes 131104 | tf_op jit(solution)/shard_map/all_to_all | solution.py:305
  91.5 3.5 %collective-permute-start.3 = (bf16[32,16,128]{2,1,0:T(8,128)(2,1)S(1)}, bf16[32,16,128]{2,1,0:T(8,128)(2,1)S(1)}, u32[]{:S(2)}, u32[]{:S(2)}) collective-permute-start(bf16[32,16,128]{2,1,0:T(8,128)(2,1)S(1)} %all-to-all-done.1.x_ref), channel_id=1, source_target_pairs={{0,1},{1,0},{2,3},{3,2},{4,5},{5,4},{6,7},{7,6},{8,9},{9,8},{10,11... | collective-permute-start | bytes 393224 | tf_op jit(solution)/shard_map/ppermute | solution.py:299
  95.0 1.9 %collective-permute-start.4 = (bf16[32,16,128]{2,1,0:T(8,128)(2,1)S(1)}, bf16[32,16,128]{2,1,0:T(8,128)(2,1)S(1)}, u32[]{:S(2)}, u32[]{:S(2)}) collective-permute-start(bf16[32,16,128]{2,1,0:T(8,128)(2,1)S(1)} %all-to-all-done.1.x_ref), channel_id=1, source_target_pairs={{0,16},{16,0},{1,17},{17,1},{2,18},{18,2},{3,19},{19,3},{4,20},{20... | collective-permute-start | bytes 393224 | tf_op jit(solution)/shard_map/ppermute | solution.py:302
  96.9 1.4 collective-permute-done.3.y_ref
  98.4 1.9 %collective-permute-start.5 = (bf16[32,16,128]{2,1,0:T(8,128)(2,1)S(1)}, bf16[32,16,128]{2,1,0:T(8,128)(2,1)S(1)}, u32[]{:S(2)}, u32[]{:S(2)}) collective-permute-start(bf16[32,16,128]{2,1,0:T(8,128)(2,1)S(1)} %collective-permute-done.3.y_ref), channel_id=1, source_target_pairs={{0,16},{16,0},{1,17},{17,1},{2,18},{18,2},{3,19},{19,3},{4,20},{20... | collective-permute-start | bytes 393224 | tf_op jit(solution)/shard_map/ppermute | solution.py:302
  100.3 0.0 collective-permute-done.4.xc_ref
  100.3 1.3 collective-permute-done.5.yc_ref
  101.6 5.2 %picked_grads.1 = (f32[32,16,128]{2,1,0:T(8,128)S(1)}, f32[32,16,128]{2,1,0:T(8,128)S(1)}, bf16[2,32,16,128]{3,2,1,0:T(8,128)(2,1)S(1)}, bf16[1024,1024]{1,0:T(8...) custom-call(s32[5]{0:T(128)S(1)} %stack.19.info, ...), custom_call_target="tpu_custom_call" | custom-call | tf_op jit(solution)/shard_map/picked_grads/pallas_call | solution.py:211
  106.8 2.1 %collective-permute-start.6 = (bf16[2,32,16,128]{3,2,1,0:T(8,128)(2,1)S(1)}, bf16[2,32,16,128]{3,2,1,0:T(8,128)(2,1)S(1)}, u32[]{:S(2)}, u32[]{:S(2)}) collective-permute-start(bf16[2,32,16,128]{3,2,1,0:T(8,128)(2,1)S(1)} %get-tuple-element.75), channel_id=1, source_target_pairs={{0,16},{16,0},{1,17},{17,1},{2,18},{18,2},{3,19},{19,3},{4,20},{20... | collective-permute-start | bytes 786440 | tf_op jit(solution)/shard_map/ppermute | solution.py:302
  108.9 1.4 collective-permute-done.6
  110.3 3.5 %collective-permute-start.7 = (bf16[32,16,128]{2,1,0:T(8,128)(2,1)S(1)}, bf16[32,16,128]{2,1,0:T(8,128)(2,1)S(1)}, u32[]{:S(2)}, u32[]{:S(2)}) collective-permute-start(bf16[32,16,128]{2,1,0:T(8,128)(2,1)S(1)} %fusion), channel_id=1, source_target_pairs={{0,1},{1,0},{2,3},{3,2},{4,5},{5,4},{6,7},{7,6},{8,9},{9,8},{10,11... | collective-permute-start | bytes 393224 | tf_op jit(solution)/shard_map/ppermute | solution.py:299
  113.7 3.6 %row_outputs.1 = (bf16[256,512]{1,0:T(8,128)(2,1)}, f32[256,512]{1,0:T(8,128)}, f32[256,128]{1,0:T(8,128)S(1)}, f32[256,128]{1,0:T(8,128)S(1)}, bf16[2,256,128]{2,1,0:T(8,128)(2,1)S(1)}) custom-call(s32[5]{0:T(128)S(1)} %stack.19.info, bf16[1024,128]{1,0:T(8,128)(2,1)S(1)} %get-tuple-element.49.q_all, bf16[1024,128]{1,0:T(8,128)(2,1)S(1)} %get-tuple-element.50.g_all, ...), custom_call_target="tpu_custom_call" | custom-call | tf_op jit(solution)/shard_map/row_outputs/pallas_call | solution.py:211
  117.3 0.4 collective-permute-done.7
  117.7 0.7 fusion.2
  118.4 3.8 %all-to-all-start.2 = ((bf16[32,16,128]{2,1,0:T(8,128)(2,1)}), bf16[32,16,128]{2,1,0:T(8,128)(2,1)S(1)}, u32[]{:S(2)}, u32[]{:S(2)}) async-start(bf16[32,16,128]{2,1,0:T(8,128)(2,1)} %fusion.2), calls=%async_computation.2 | async-start | bytes 262144 | tf_op jit(solution)/shard_map/all_to_all | solution.py:305
  122.3 1.9 %collective-permute-start.8 = (bf16[2,256,128]{2,1,0:T(8,128)(2,1)S(1)}, bf16[2,256,128]{2,1,0:T(8,128)(2,1)S(1)}, u32[]{:S(2)}, u32[]{:S(2)}) collective-permute-start(bf16[2,256,128]{2,1,0:T(8,128)(2,1)S(1)} %get-tuple-element.79), channel_id=1, source_target_pairs={{0,16},{16,0},{1,17},{17,1},{2,18},{18,2},{3,19},{19,3},{4,20},{20... | collective-permute-start | bytes 393224 | tf_op jit(solution)/shard_map/ppermute | solution.py:302
  124.2 1.3 collective-permute-done.8.got_ref
  125.5 3.5 %collective-permute-start.9 = (bf16[256,128]{1,0:T(8,128)(2,1)S(1)}, bf16[256,128]{1,0:T(8,128)(2,1)S(1)}, u32[]{:S(2)}, u32[]{:S(2)}) collective-permute-start(bf16[256,128]{1,0:T(8,128)(2,1)S(1)} %fusion.3), channel_id=1, source_target_pairs={{0,1},{1,0},{2,3},{3,2},{4,5},{5,4},{6,7},{7,6},{8,9},{9,8},{10,11... | collective-permute-start | bytes 196616 | tf_op jit(solution)/shard_map/ppermute | solution.py:299
  129.0 2.7 %collective-permute-done.9.pair_ref = bf16[256,128]{1,0:T(8,128)(2,1)S(1)} collective-permute-done((bf16[256,128]{1,0:T(8,128)(2,1)S(1)}, bf16[256,128]{1,0:T(8,128)(2,1)S(1)}, u32[]{:S(2)}, u32[]{:S(2)}) %collective-permute-start.9) | collective-permute-done | bytes 65568 | tf_op jit(solution)/shard_map/ppermute | solution.py:299
  131.7 22.1 %all-to-all-done.2.landed_ref = bf16[32,16,128]{2,1,0:T(8,128)(2,1)S(1)} async-done(((bf16[32,16,128]{2,1,0:T(8,128)(2,1)}), bf16[32,16,128]{2,1,0:T(8,128)(2,1)S(1)}, u32[]{:S(2)}, u32[]{:S(2)}) %all-to-all-start.2) | async-done | bytes 131104 | tf_op jit(solution)/shard_map/all_to_all | solution.py:305
  153.8 0.9 scatter.1
  154.7 27.6 %all_to_all.20.back_ref = bf16[32,8,128]{2,1,0:T(8,128)(2,1)S(1)} all-to-all(bf16[32,8,128]{2,1,0:T(8,128)(2,1)S(1)} %scatter.1), channel_id=1, replica_groups=mesh['z'=32,'core'=2,'grp'=8,'pair'=2] {'z'}, dimensions={0} | all-to-all | bytes 131072 | tf_op jit(solution)/shard_map/all_to_all | solution.py:305
  182.2 0.7 unpack.1
  (2 shorter events, 0.1 us)
Async XLA Ops:
  2.2 54.5 %all-to-all-start = ((bf16[32,8,128]{2,1,0:T(8,128)(2,1)}), bf16[32,8,128]{2,1,0:T(8,128)(2,1)S(1)}, u32[]{:S(2)}, u32[]{:S(2)}) async-start(bf16[32,8,128]{2,1,0:T(8,128)(2,1)} %get-tuple-element.45), calls=%async_computation | async-start | bytes 131072 | tf_op jit(solution)/shard_map/all_to_all | solution.py:305
  30.9 6.2 %collective-permute-start = (bf16[256,128]{1,0:T(8,128)(2,1)S(1)}, bf16[256,128]{1,0:T(8,128)(2,1)S(1)}, u32[]{:S(2)}, u32[]{:S(2)}) collective-permute-start(bf16[256,128]{1,0:T(8,128)(2,1)S(1)} %get-tuple-element.55.own_a), channel_id=1, source_target_pairs={{0,1},{1,0},{2,3},{3,2},{4,5},{5,4},{6,7},{7,6},{8,9},{9,8},{10,11... | collective-permute-start | bytes 196616 | tf_op jit(solution)/shard_map/ppermute | solution.py:299
  58.1 33.5 %all-to-all-start.1 = ((bf16[32,16,128]{2,1,0:T(8,128)(2,1)}), bf16[32,16,128]{2,1,0:T(8,128)(2,1)S(1)}, u32[]{:S(2)}, u32[]{:S(2)}) async-start(bf16[32,16,128]{2,1,0:T(8,128)(2,1)} %gather.1), calls=%async_computation.1 | async-start | bytes 262144 | tf_op jit(solution)/shard_map/all_to_all | solution.py:305
  61.9 4.3 %collective-permute-start.1 = (bf16[256,128]{1,0:T(8,128)(2,1)S(1)}, bf16[256,128]{1,0:T(8,128)(2,1)S(1)}, u32[]{:S(2)}, u32[]{:S(2)}) collective-permute-start(bf16[256,128]{1,0:T(8,128)(2,1)S(1)} %get-tuple-element.55.own_a), channel_id=1, source_target_pairs={{0,16},{16,0},{1,17},{17,1},{2,18},{18,2},{3,19},{19,3},{4,20},{20... | collective-permute-start | bytes 196616 | tf_op jit(solution)/shard_map/ppermute | solution.py:302
  63.9 3.3 %collective-permute-start.2 = (bf16[256,128]{1,0:T(8,128)(2,1)S(1)}, bf16[256,128]{1,0:T(8,128)(2,1)S(1)}, u32[]{:S(2)}, u32[]{:S(2)}) collective-permute-start(bf16[256,128]{1,0:T(8,128)(2,1)S(1)} %collective-permute-done.own_b), channel_id=1, source_target_pairs={{0,16},{16,0},{1,17},{17,1},{2,18},{18,2},{3,19},{19,3},{4,20},{20... | collective-permute-start | bytes 196616 | tf_op jit(solution)/shard_map/ppermute | solution.py:302
  91.5 6.8 %collective-permute-start.3 = (bf16[32,16,128]{2,1,0:T(8,128)(2,1)S(1)}, bf16[32,16,128]{2,1,0:T(8,128)(2,1)S(1)}, u32[]{:S(2)}, u32[]{:S(2)}) collective-permute-start(bf16[32,16,128]{2,1,0:T(8,128)(2,1)S(1)} %all-to-all-done.1.x_ref), channel_id=1, source_target_pairs={{0,1},{1,0},{2,3},{3,2},{4,5},{5,4},{6,7},{7,6},{8,9},{9,8},{10,11... | collective-permute-start | bytes 393224 | tf_op jit(solution)/shard_map/ppermute | solution.py:299
  95.0 5.3 %collective-permute-start.4 = (bf16[32,16,128]{2,1,0:T(8,128)(2,1)S(1)}, bf16[32,16,128]{2,1,0:T(8,128)(2,1)S(1)}, u32[]{:S(2)}, u32[]{:S(2)}) collective-permute-start(bf16[32,16,128]{2,1,0:T(8,128)(2,1)S(1)} %all-to-all-done.1.x_ref), channel_id=1, source_target_pairs={{0,16},{16,0},{1,17},{17,1},{2,18},{18,2},{3,19},{19,3},{4,20},{20... | collective-permute-start | bytes 393224 | tf_op jit(solution)/shard_map/ppermute | solution.py:302
  98.4 3.2 %collective-permute-start.5 = (bf16[32,16,128]{2,1,0:T(8,128)(2,1)S(1)}, bf16[32,16,128]{2,1,0:T(8,128)(2,1)S(1)}, u32[]{:S(2)}, u32[]{:S(2)}) collective-permute-start(bf16[32,16,128]{2,1,0:T(8,128)(2,1)S(1)} %collective-permute-done.3.y_ref), channel_id=1, source_target_pairs={{0,16},{16,0},{1,17},{17,1},{2,18},{18,2},{3,19},{19,3},{4,20},{20... | collective-permute-start | bytes 393224 | tf_op jit(solution)/shard_map/ppermute | solution.py:302
  106.8 3.4 %collective-permute-start.6 = (bf16[2,32,16,128]{3,2,1,0:T(8,128)(2,1)S(1)}, bf16[2,32,16,128]{3,2,1,0:T(8,128)(2,1)S(1)}, u32[]{:S(2)}, u32[]{:S(2)}) collective-permute-start(bf16[2,32,16,128]{3,2,1,0:T(8,128)(2,1)S(1)} %get-tuple-element.75), channel_id=1, source_target_pairs={{0,16},{16,0},{1,17},{17,1},{2,18},{18,2},{3,19},{19,3},{4,20},{20... | collective-permute-start | bytes 786440 | tf_op jit(solution)/shard_map/ppermute | solution.py:302
  110.3 7.4 %collective-permute-start.7 = (bf16[32,16,128]{2,1,0:T(8,128)(2,1)S(1)}, bf16[32,16,128]{2,1,0:T(8,128)(2,1)S(1)}, u32[]{:S(2)}, u32[]{:S(2)}) collective-permute-start(bf16[32,16,128]{2,1,0:T(8,128)(2,1)S(1)} %fusion), channel_id=1, source_target_pairs={{0,1},{1,0},{2,3},{3,2},{4,5},{5,4},{6,7},{7,6},{8,9},{9,8},{10,11... | collective-permute-start | bytes 393224 | tf_op jit(solution)/shard_map/ppermute | solution.py:299
  118.4 35.3 %all-to-all-start.2 = ((bf16[32,16,128]{2,1,0:T(8,128)(2,1)}), bf16[32,16,128]{2,1,0:T(8,128)(2,1)S(1)}, u32[]{:S(2)}, u32[]{:S(2)}) async-start(bf16[32,16,128]{2,1,0:T(8,128)(2,1)} %fusion.2), calls=%async_computation.2 | async-start | bytes 262144 | tf_op jit(solution)/shard_map/all_to_all | solution.py:305
  122.3 3.2 %collective-permute-start.8 = (bf16[2,256,128]{2,1,0:T(8,128)(2,1)S(1)}, bf16[2,256,128]{2,1,0:T(8,128)(2,1)S(1)}, u32[]{:S(2)}, u32[]{:S(2)}) collective-permute-start(bf16[2,256,128]{2,1,0:T(8,128)(2,1)S(1)} %get-tuple-element.79), channel_id=1, source_target_pairs={{0,16},{16,0},{1,17},{17,1},{2,18},{18,2},{3,19},{19,3},{4,20},{20... | collective-permute-start | bytes 393224 | tf_op jit(solution)/shard_map/ppermute | solution.py:302
  125.5 6.2 %collective-permute-start.9 = (bf16[256,128]{1,0:T(8,128)(2,1)S(1)}, bf16[256,128]{1,0:T(8,128)(2,1)S(1)}, u32[]{:S(2)}, u32[]{:S(2)}) collective-permute-start(bf16[256,128]{1,0:T(8,128)(2,1)S(1)} %fusion.3), channel_id=1, source_target_pairs={{0,1},{1,0},{2,3},{3,2},{4,5},{5,4},{6,7},{7,6},{8,9},{9,8},{10,11... | collective-permute-start | bytes 196616 | tf_op jit(solution)/shard_map/ppermute | solution.py:299

commit v5 on v4

--- a/solution.py
+++ b/solution.py
@@ -19,12 +19,19 @@
 LIMIT = 4 << 20
 
 
+def first_rank(count):
+    return count * 5 // 8
+
+
 def offset_of(info, picks, block, slot):
     return picks[(block * info[4] + info[2]) * 2 + slot]
 
 
-def block_of(info, picks, block, slot):
-    return jnp.maximum(block - offset_of(info, picks, block, slot), 0)
+def rank_of_pick(info, picks, rank, slot, count):
+    first = first_rank(count)
+    block = (first + rank) % count
+    picked = jnp.maximum(block - offset_of(info, picks, block, slot), 0)
+    return jnp.where(picked >= first, picked - first, picked - first + count)
 
 
 def dot(a, b, dims=NN):
@@ -254,18 +261,20 @@
 def gather(info, picks, banded_ref, out_ref, scr):
     scr[...] = banded_ref[...].astype(F32)
     picked = out_ref.shape[1] // scr.shape[1]
-    for d in range(out_ref.shape[0]):
-        rows = [scr[block_of(info, picks, d, j)] for j in range(picked)]
-        out_ref[d] = jnp.concatenate(rows, 0).astype(BF16)
+    count = out_ref.shape[0]
+    for rank in range(count):
+        rows = [scr[rank_of_pick(info, picks, rank, j, count)] for j in range(picked)]
+        out_ref[rank] = jnp.concatenate(rows, 0).astype(BF16)
 
 
 def scatter(info, picks, landed_ref, out_ref, acc):
     acc[...] = jnp.zeros_like(acc)
     stripe = acc.shape[1]
-    for d in range(landed_ref.shape[0]):
-        rows = landed_ref[d].astype(F32)
+    count = landed_ref.shape[0]
+    for rank in range(count):
+        rows = landed_ref[rank].astype(F32)
         for j in range(rows.shape[0] // stripe):
-            at = block_of(info, picks, d, j)
+            at = rank_of_pick(info, picks, rank, j, count)
             acc[at] = acc[at] + rows[j * stripe : (j + 1) * stripe]
     out_ref[...] = acc[...].astype(BF16)
 
@@ -302,7 +311,10 @@
         return lax.ppermute(x, "core", SWAP)
 
     def across(x):
-        return lax.all_to_all(x, "z", split_axis=0, concat_axis=0, tiled=True)
+        order = [(first_rank(z_count) + i) % z_count for i in range(z_count)]
+        return lax.all_to_all(
+            x, "z", split_axis=0, concat_axis=0, axis_index_groups=[order], tiled=True
+        )
 
     own, striped = call(
         pack,

time: 184 us -> 171 us (0.929)
  waiting for transfers between devices: 74.4 us -> 29.8 us
  starting transfers between devices: 62.5 us -> 94.2 us
    all_to_all x3, waiting for transfers between devices: 64.6 us -> 20 us  [across(): lax.all_to_all(x, 'z', split_axis=0, concat_axis=0, axis_index_groups=[or...]
    all_to_all x3, starting transfers between devices: 36.4 us -> 68.1 us  [across(): lax.all_to_all(x, 'z', split_axis=0, concat_axis=0, axis_index_groups=[or...]
  transfers between devices with their start and end apart: 13 -> 13, of which waited for: 11 -> 11; matrix products, arithmetic and copies ran while one was open for 1% -> 1% of each run, Pallas kernels for 3% -> 4%
where the time goes in v5:
time: 171 us; the launch traced here: 170 us
  starting transfers between devices  94.2 us (55%)
  waiting for transfers between devices  29.8 us (17%)
  blocking collectives  27.8 us (16%)
  Pallas kernels  16 us (9%)
    all_to_all x3, starting transfers between devices, across(): lax.all_to_all(x, 'z', split_axis=0, concat_axis=0, axis_index_groups=[or...  68.1 us
    all_to_all x1, blocking collectives, across(): lax.all_to_all(x, 'z', split_axis=0, concat_axis=0, axis_index_groups=[or...  27.8 us
    all_to_all x3, waiting for transfers between devices, across(): lax.all_to_all(x, 'z', split_axis=0, concat_axis=0, axis_index_groups=[or...  20 us
    pallas_call x8, Pallas kernels, call(): pl.pallas_call(kernel, out_shape=out_shape, in_specs=[smem] * len(scalars...  16 us
    ppermute x4, starting transfers between devices, to_pair(): return lax.ppermute(x, 'pair', SWAP)  13.9 us
    ppermute x6, starting transfers between devices, to_core(): return lax.ppermute(x, 'core', SWAP)  12.1 us
    ppermute x4, waiting for transfers between devices, to_pair(): return lax.ppermute(x, 'pair', SWAP)  4.92 us
    ppermute x6, waiting for transfers between devices, to_core(): return lax.ppermute(x, 'core', SWAP)  4.86 us
  transfers between devices with their start and end apart: 13, of which 11 were waited for; matrix products, arithmetic and copies ran while one was open for 1% of the time, Pallas kernels for 4%

profile of v5, /device:TPU:6, one launch (start us, length us, event | category | flops | bytes accessed | tf_op | source)
XLA Modules:
  0.0 170.4 jit_solution(10642949790647579852)
XLA Ops:
  0.6 1.5 pack.1
  2.2 31.1 %all-to-all-start = ((bf16[32,8,128]{2,1,0:T(8,128)(2,1)}), bf16[32,8,128]{2,1,0:T(8,128)(2,1)S(1)}, u32[]{:S(2)}, u32[]{:S(2)}) async-start(bf16[32,8,128]{2,1,0:T(8,128)(2,1)} %get-tuple-element.45), calls=%async_computation | async-start | bytes 131072 | tf_op jit(solution)/shard_map/all_to_all | solution.py:315
  33.3 3.5 %collective-permute-start = (bf16[256,128]{1,0:T(8,128)(2,1)S(1)}, bf16[256,128]{1,0:T(8,128)(2,1)S(1)}, u32[]{:S(2)}, u32[]{:S(2)}) collective-permute-start(bf16[256,128]{1,0:T(8,128)(2,1)S(1)} %get-tuple-element.55.own_a), channel_id=1, source_target_pairs={{0,1},{1,0},{2,3},{3,2},{4,5},{5,4},{6,7},{7,6},{8,9},{9,8},{10,11... | collective-permute-start | bytes 196616 | tf_op jit(solution)/shard_map/ppermute | solution.py:308
  36.8 0.8 copy.9
  37.6 0.1 reshape.17.picks
  37.7 1.1 stack_heads.1
  38.9 0.1 stack.19.info
  39.0 0.4 collective-permute-done.own_b
  39.4 4.9 %all-to-all-done.banded_ref = bf16[32,8,128]{2,1,0:T(8,128)(2,1)S(1)} async-done(((bf16[32,8,128]{2,1,0:T(8,128)(2,1)}), bf16[32,8,128]{2,1,0:T(8,128)(2,1)S(1)}, u32[]{:S(2)}, u32[]{:S(2)}) %all-to-all-start) | async-done | bytes 65568 | tf_op jit(solution)/shard_map/all_to_all | solution.py:315
  44.3 1.4 gather.1
  45.7 18.6 %all-to-all-start.1 = ((bf16[32,16,128]{2,1,0:T(8,128)(2,1)}), bf16[32,16,128]{2,1,0:T(8,128)(2,1)S(1)}, u32[]{:S(2)}, u32[]{:S(2)}) async-start(bf16[32,16,128]{2,1,0:T(8,128)(2,1)} %gather.1), calls=%async_computation.1 | async-start | bytes 262144 | tf_op jit(solution)/shard_map/all_to_all | solution.py:315
  64.3 1.9 %collective-permute-start.1 = (bf16[256,128]{1,0:T(8,128)(2,1)S(1)}, bf16[256,128]{1,0:T(8,128)(2,1)S(1)}, u32[]{:S(2)}, u32[]{:S(2)}) collective-permute-start(bf16[256,128]{1,0:T(8,128)(2,1)S(1)} %get-tuple-element.55.own_a), channel_id=1, source_target_pairs={{0,16},{16,0},{1,17},{17,1},{2,18},{18,2},{3,19},{19,3},{4,20},{20... | collective-permute-start | bytes 196616 | tf_op jit(solution)/shard_map/ppermute | solution.py:311
  66.2 2.4 %collective-permute-start.2 = (bf16[256,128]{1,0:T(8,128)(2,1)S(1)}, bf16[256,128]{1,0:T(8,128)(2,1)S(1)}, u32[]{:S(2)}, u32[]{:S(2)}) collective-permute-start(bf16[256,128]{1,0:T(8,128)(2,1)S(1)} %collective-permute-done.own_b), channel_id=1, source_target_pairs={{0,16},{16,0},{1,17},{17,1},{2,18},{18,2},{3,19},{19,3},{4,20},{20... | collective-permute-start | bytes 196616 | tf_op jit(solution)/shard_map/ppermute | solution.py:311
  68.7 0.0 collective-permute-done.1.own_c
  68.7 0.9 collective-permute-done.2.own_d
  69.5 1.5 own_scores.1
  71.0 8.3 %all-to-all-done.1.x_ref = bf16[32,16,128]{2,1,0:T(8,128)(2,1)S(1)} async-done(((bf16[32,16,128]{2,1,0:T(8,128)(2,1)}), bf16[32,16,128]{2,1,0:T(8,128)(2,1)S(1)}, u32[]{:S(2)}, u32[]{:S(2)}) %all-to-all-start.1) | async-done | bytes 131104 | tf_op jit(solution)/shard_map/all_to_all | solution.py:315
  79.3 3.5 %collective-permute-start.3 = (bf16[32,16,128]{2,1,0:T(8,128)(2,1)S(1)}, bf16[32,16,128]{2,1,0:T(8,128)(2,1)S(1)}, u32[]{:S(2)}, u32[]{:S(2)}) collective-permute-start(bf16[32,16,128]{2,1,0:T(8,128)(2,1)S(1)} %all-to-all-done.1.x_ref), channel_id=1, source_target_pairs={{0,1},{1,0},{2,3},{3,2},{4,5},{5,4},{6,7},{7,6},{8,9},{9,8},{10,11... | collective-permute-start | bytes 393224 | tf_op jit(solution)/shard_map/ppermute | solution.py:308
  82.8 1.9 %collective-permute-start.4 = (bf16[32,16,128]{2,1,0:T(8,128)(2,1)S(1)}, bf16[32,16,128]{2,1,0:T(8,128)(2,1)S(1)}, u32[]{:S(2)}, u32[]{:S(2)}) collective-permute-start(bf16[32,16,128]{2,1,0:T(8,128)(2,1)S(1)} %all-to-all-done.1.x_ref), channel_id=1, source_target_pairs={{0,16},{16,0},{1,17},{17,1},{2,18},{18,2},{3,19},{19,3},{4,20},{20... | collective-permute-start | bytes 393224 | tf_op jit(solution)/shard_map/ppermute | solution.py:311
  84.7 1.4 collective-permute-done.3.y_ref
  86.2 1.9 %collective-permute-start.5 = (bf16[32,16,128]{2,1,0:T(8,128)(2,1)S(1)}, bf16[32,16,128]{2,1,0:T(8,128)(2,1)S(1)}, u32[]{:S(2)}, u32[]{:S(2)}) collective-permute-start(bf16[32,16,128]{2,1,0:T(8,128)(2,1)S(1)} %collective-permute-done.3.y_ref), channel_id=1, source_target_pairs={{0,16},{16,0},{1,17},{17,1},{2,18},{18,2},{3,19},{19,3},{4,20},{20... | collective-permute-start | bytes 393224 | tf_op jit(solution)/shard_map/ppermute | solution.py:311
  88.1 0.0 collective-permute-done.4.xc_ref
  88.1 1.3 collective-permute-done.5.yc_ref
  89.4 5.2 %picked_grads.1 = (f32[32,16,128]{2,1,0:T(8,128)S(1)}, f32[32,16,128]{2,1,0:T(8,128)S(1)}, bf16[2,32,16,128]{3,2,1,0:T(8,128)(2,1)S(1)}, bf16[1024,1024]{1,0:T(8...) custom-call(s32[5]{0:T(128)S(1)} %stack.19.info, ...), custom_call_target="tpu_custom_call" | custom-call | tf_op jit(solution)/shard_map/picked_grads/pallas_call | solution.py:218
  94.6 2.1 %collective-permute-start.6 = (bf16[2,32,16,128]{3,2,1,0:T(8,128)(2,1)S(1)}, bf16[2,32,16,128]{3,2,1,0:T(8,128)(2,1)S(1)}, u32[]{:S(2)}, u32[]{:S(2)}) collective-permute-start(bf16[2,32,16,128]{3,2,1,0:T(8,128)(2,1)S(1)} %get-tuple-element.75), channel_id=1, source_target_pairs={{0,16},{16,0},{1,17},{17,1},{2,18},{18,2},{3,19},{19,3},{4,20},{20... | collective-permute-start | bytes 786440 | tf_op jit(solution)/shard_map/ppermute | solution.py:311
  96.6 1.4 collective-permute-done.6
  98.0 3.5 %collective-permute-start.7 = (bf16[32,16,128]{2,1,0:T(8,128)(2,1)S(1)}, bf16[32,16,128]{2,1,0:T(8,128)(2,1)S(1)}, u32[]{:S(2)}, u32[]{:S(2)}) collective-permute-start(bf16[32,16,128]{2,1,0:T(8,128)(2,1)S(1)} %fusion), channel_id=1, source_target_pairs={{0,1},{1,0},{2,3},{3,2},{4,5},{5,4},{6,7},{7,6},{8,9},{9,8},{10,11... | collective-permute-start | bytes 393224 | tf_op jit(solution)/shard_map/ppermute | solution.py:308
  101.5 3.6 %row_outputs.1 = (bf16[256,512]{1,0:T(8,128)(2,1)}, f32[256,512]{1,0:T(8,128)}, f32[256,128]{1,0:T(8,128)S(1)}, f32[256,128]{1,0:T(8,128)S(1)}, bf16[2,256,128]{2,1,0:T(8,128)(2,1)S(1)}) custom-call(s32[5]{0:T(128)S(1)} %stack.19.info, bf16[1024,128]{1,0:T(8,128)(2,1)S(1)} %get-tuple-element.49.q_all, bf16[1024,128]{1,0:T(8,128)(2,1)S(1)} %get-tuple-element.50.g_all, ...), custom_call_target="tpu_custom_call" | custom-call | tf_op jit(solution)/shard_map/row_outputs/pallas_call | solution.py:218
  105.1 0.4 collective-permute-done.7
  105.5 0.7 fusion.2
  106.2 18.4 %all-to-all-start.2 = ((bf16[32,16,128]{2,1,0:T(8,128)(2,1)}), bf16[32,16,128]{2,1,0:T(8,128)(2,1)S(1)}, u32[]{:S(2)}, u32[]{:S(2)}) async-start(bf16[32,16,128]{2,1,0:T(8,128)(2,1)} %fusion.2), calls=%async_computation.2 | async-start | bytes 262144 | tf_op jit(solution)/shard_map/all_to_all | solution.py:315
  124.6 1.9 %collective-permute-start.8 = (bf16[2,256,128]{2,1,0:T(8,128)(2,1)S(1)}, bf16[2,256,128]{2,1,0:T(8,128)(2,1)S(1)}, u32[]{:S(2)}, u32[]{:S(2)}) collective-permute-start(bf16[2,256,128]{2,1,0:T(8,128)(2,1)S(1)} %get-tuple-element.79), channel_id=1, source_target_pairs={{0,16},{16,0},{1,17},{17,1},{2,18},{18,2},{3,19},{19,3},{4,20},{20... | collective-permute-start | bytes 393224 | tf_op jit(solution)/shard_map/ppermute | solution.py:311
  126.6 1.3 collective-permute-done.8.got_ref
  127.9 3.5 %collective-permute-start.9 = (bf16[256,128]{1,0:T(8,128)(2,1)S(1)}, bf16[256,128]{1,0:T(8,128)(2,1)S(1)}, u32[]{:S(2)}, u32[]{:S(2)}) collective-permute-start(bf16[256,128]{1,0:T(8,128)(2,1)S(1)} %fusion.3), channel_id=1, source_target_pairs={{0,1},{1,0},{2,3},{3,2},{4,5},{5,4},{6,7},{7,6},{8,9},{9,8},{10,11... | collective-permute-start | bytes 196616 | tf_op jit(solution)/shard_map/ppermute | solution.py:308
  131.4 2.7 %collective-permute-done.9.pair_ref = bf16[256,128]{1,0:T(8,128)(2,1)S(1)} collective-permute-done((bf16[256,128]{1,0:T(8,128)(2,1)S(1)}, bf16[256,128]{1,0:T(8,128)(2,1)S(1)}, u32[]{:S(2)}, u32[]{:S(2)}) %collective-permute-start.9) | collective-permute-done | bytes 65568 | tf_op jit(solution)/shard_map/ppermute | solution.py:308
  134.1 6.9 %all-to-all-done.2.landed_ref = bf16[32,16,128]{2,1,0:T(8,128)(2,1)S(1)} async-done(((bf16[32,16,128]{2,1,0:T(8,128)(2,1)}), bf16[32,16,128]{2,1,0:T(8,128)(2,1)S(1)}, u32[]{:S(2)}, u32[]{:S(2)}) %all-to-all-start.2) | async-done | bytes 131104 | tf_op jit(solution)/shard_map/all_to_all | solution.py:315
  140.9 0.9 scatter.1
  141.8 27.8 %all_to_all.20.back_ref = bf16[32,8,128]{2,1,0:T(8,128)(2,1)S(1)} all-to-all(bf16[32,8,128]{2,1,0:T(8,128)(2,1)S(1)} %scatter.1), channel_id=1, replica_groups={{640,672,704,736,768,800,832,864,896,928,960,992,0,32,64,96,128,160,192..., dimensions={0} | all-to-all | bytes 131072 | tf_op jit(solution)/shard_map/all_to_all | solution.py:315
  169.7 0.7 unpack.1
  (2 shorter events, 0.1 us)
Async XLA Ops:
  2.2 42.1 %all-to-all-start = ((bf16[32,8,128]{2,1,0:T(8,128)(2,1)}), bf16[32,8,128]{2,1,0:T(8,128)(2,1)S(1)}, u32[]{:S(2)}, u32[]{:S(2)}) async-start(bf16[32,8,128]{2,1,0:T(8,128)(2,1)} %get-tuple-element.45), calls=%async_computation | async-start | bytes 131072 | tf_op jit(solution)/shard_map/all_to_all | solution.py:315
  33.3 6.2 %collective-permute-start = (bf16[256,128]{1,0:T(8,128)(2,1)S(1)}, bf16[256,128]{1,0:T(8,128)(2,1)S(1)}, u32[]{:S(2)}, u32[]{:S(2)}) collective-permute-start(bf16[256,128]{1,0:T(8,128)(2,1)S(1)} %get-tuple-element.55.own_a), channel_id=1, source_target_pairs={{0,1},{1,0},{2,3},{3,2},{4,5},{5,4},{6,7},{7,6},{8,9},{9,8},{10,11... | collective-permute-start | bytes 196616 | tf_op jit(solution)/shard_map/ppermute | solution.py:308
  45.7 33.6 %all-to-all-start.1 = ((bf16[32,16,128]{2,1,0:T(8,128)(2,1)}), bf16[32,16,128]{2,1,0:T(8,128)(2,1)S(1)}, u32[]{:S(2)}, u32[]{:S(2)}) async-start(bf16[32,16,128]{2,1,0:T(8,128)(2,1)} %gather.1), calls=%async_computation.1 | async-start | bytes 262144 | tf_op jit(solution)/shard_map/all_to_all | solution.py:315
  64.3 4.3 %collective-permute-start.1 = (bf16[256,128]{1,0:T(8,128)(2,1)S(1)}, bf16[256,128]{1,0:T(8,128)(2,1)S(1)}, u32[]{:S(2)}, u32[]{:S(2)}) collective-permute-start(bf16[256,128]{1,0:T(8,128)(2,1)S(1)} %get-tuple-element.55.own_a), channel_id=1, source_target_pairs={{0,16},{16,0},{1,17},{17,1},{2,18},{18,2},{3,19},{19,3},{4,20},{20... | collective-permute-start | bytes 196616 | tf_op jit(solution)/shard_map/ppermute | solution.py:311
  66.2 3.3 %collective-permute-start.2 = (bf16[256,128]{1,0:T(8,128)(2,1)S(1)}, bf16[256,128]{1,0:T(8,128)(2,1)S(1)}, u32[]{:S(2)}, u32[]{:S(2)}) collective-permute-start(bf16[256,128]{1,0:T(8,128)(2,1)S(1)} %collective-permute-done.own_b), channel_id=1, source_target_pairs={{0,16},{16,0},{1,17},{17,1},{2,18},{18,2},{3,19},{19,3},{4,20},{20... | collective-permute-start | bytes 196616 | tf_op jit(solution)/shard_map/ppermute | solution.py:311
  79.3 6.8 %collective-permute-start.3 = (bf16[32,16,128]{2,1,0:T(8,128)(2,1)S(1)}, bf16[32,16,128]{2,1,0:T(8,128)(2,1)S(1)}, u32[]{:S(2)}, u32[]{:S(2)}) collective-permute-start(bf16[32,16,128]{2,1,0:T(8,128)(2,1)S(1)} %all-to-all-done.1.x_ref), channel_id=1, source_target_pairs={{0,1},{1,0},{2,3},{3,2},{4,5},{5,4},{6,7},{7,6},{8,9},{9,8},{10,11... | collective-permute-start | bytes 393224 | tf_op jit(solution)/shard_map/ppermute | solution.py:308
  82.8 5.3 %collective-permute-start.4 = (bf16[32,16,128]{2,1,0:T(8,128)(2,1)S(1)}, bf16[32,16,128]{2,1,0:T(8,128)(2,1)S(1)}, u32[]{:S(2)}, u32[]{:S(2)}) collective-permute-start(bf16[32,16,128]{2,1,0:T(8,128)(2,1)S(1)} %all-to-all-done.1.x_ref), channel_id=1, source_target_pairs={{0,16},{16,0},{1,17},{17,1},{2,18},{18,2},{3,19},{19,3},{4,20},{20... | collective-permute-start | bytes 393224 | tf_op jit(solution)/shard_map/ppermute | solution.py:311
  86.2 3.2 %collective-permute-start.5 = (bf16[32,16,128]{2,1,0:T(8,128)(2,1)S(1)}, bf16[32,16,128]{2,1,0:T(8,128)(2,1)S(1)}, u32[]{:S(2)}, u32[]{:S(2)}) collective-permute-start(bf16[32,16,128]{2,1,0:T(8,128)(2,1)S(1)} %collective-permute-done.3.y_ref), channel_id=1, source_target_pairs={{0,16},{16,0},{1,17},{17,1},{2,18},{18,2},{3,19},{19,3},{4,20},{20... | collective-permute-start | bytes 393224 | tf_op jit(solution)/shard_map/ppermute | solution.py:311
  94.6 3.4 %collective-permute-start.6 = (bf16[2,32,16,128]{3,2,1,0:T(8,128)(2,1)S(1)}, bf16[2,32,16,128]{3,2,1,0:T(8,128)(2,1)S(1)}, u32[]{:S(2)}, u32[]{:S(2)}) collective-permute-start(bf16[2,32,16,128]{3,2,1,0:T(8,128)(2,1)S(1)} %get-tuple-element.75), channel_id=1, source_target_pairs={{0,16},{16,0},{1,17},{17,1},{2,18},{18,2},{3,19},{19,3},{4,20},{20... | collective-permute-start | bytes 786440 | tf_op jit(solution)/shard_map/ppermute | solution.py:311
  98.0 7.4 %collective-permute-start.7 = (bf16[32,16,128]{2,1,0:T(8,128)(2,1)S(1)}, bf16[32,16,128]{2,1,0:T(8,128)(2,1)S(1)}, u32[]{:S(2)}, u32[]{:S(2)}) collective-permute-start(bf16[32,16,128]{2,1,0:T(8,128)(2,1)S(1)} %fusion), channel_id=1, source_target_pairs={{0,1},{1,0},{2,3},{3,2},{4,5},{5,4},{6,7},{7,6},{8,9},{9,8},{10,11... | collective-permute-start | bytes 393224 | tf_op jit(solution)/shard_map/ppermute | solution.py:308
  106.2 34.7 %all-to-all-start.2 = ((bf16[32,16,128]{2,1,0:T(8,128)(2,1)}), bf16[32,16,128]{2,1,0:T(8,128)(2,1)S(1)}, u32[]{:S(2)}, u32[]{:S(2)}) async-start(bf16[32,16,128]{2,1,0:T(8,128)(2,1)} %fusion.2), calls=%async_computation.2 | async-start | bytes 262144 | tf_op jit(solution)/shard_map/all_to_all | solution.py:315
  124.6 3.2 %collective-permute-start.8 = (bf16[2,256,128]{2,1,0:T(8,128)(2,1)S(1)}, bf16[2,256,128]{2,1,0:T(8,128)(2,1)S(1)}, u32[]{:S(2)}, u32[]{:S(2)}) collective-permute-start(bf16[2,256,128]{2,1,0:T(8,128)(2,1)S(1)} %get-tuple-element.79), channel_id=1, source_target_pairs={{0,16},{16,0},{1,17},{17,1},{2,18},{18,2},{3,19},{19,3},{4,20},{20... | collective-permute-start | bytes 393224 | tf_op jit(solution)/shard_map/ppermute | solution.py:311
  127.9 6.2 %collective-permute-start.9 = (bf16[256,128]{1,0:T(8,128)(2,1)S(1)}, bf16[256,128]{1,0:T(8,128)(2,1)S(1)}, u32[]{:S(2)}, u32[]{:S(2)}) collective-permute-start(bf16[256,128]{1,0:T(8,128)(2,1)S(1)} %fusion.3), channel_id=1, source_target_pairs={{0,1},{1,0},{2,3},{3,2},{4,5},{5,4},{6,7},{7,6},{8,9},{9,8},{10,11... | collective-permute-start | bytes 196616 | tf_op jit(solution)/shard_map/ppermute | solution.py:308

commit v6 on v5

--- a/solution.py
+++ b/solution.py
@@ -23,15 +23,19 @@
     return count * 5 // 8
 
 
+def stride_of(count):
+    return count // 2 - 1
+
+
 def offset_of(info, picks, block, slot):
     return picks[(block * info[4] + info[2]) * 2 + slot]
 
 
 def rank_of_pick(info, picks, rank, slot, count):
     first = first_rank(count)
-    block = (first + rank) % count
+    block = (first + stride_of(count) * rank) % count
     picked = jnp.maximum(block - offset_of(info, picks, block, slot), 0)
-    return jnp.where(picked >= first, picked - first, picked - first + count)
+    return lax.rem((picked - first + count) * stride_of(count), count)
 
 
 def dot(a, b, dims=NN):
@@ -311,7 +315,8 @@
         return lax.ppermute(x, "core", SWAP)
 
     def across(x):
-        order = [(first_rank(z_count) + i) % z_count for i in range(z_count)]
+        first, stride = first_rank(z_count), stride_of(z_count)
+        order = [(first + stride * i) % z_count for i in range(z_count)]
         return lax.all_to_all(
             x, "z", split_axis=0, concat_axis=0, axis_index_groups=[order], tiled=True
         )

time: 171 us -> 172 us (level)
  no operation moved by 1% of the time
where the time goes in v6:
time: 172 us; the launch traced here: 171 us
  starting transfers between devices  94.5 us (55%)
  waiting for transfers between devices  29.7 us (17%)
  blocking collectives  27.8 us (16%)
  Pallas kernels  16.1 us (9%)
    all_to_all x3, starting transfers between devices, across(): lax.all_to_all(x, 'z', split_axis=0, concat_axis=0, axis_index_groups=[or...  68.5 us
    all_to_all x1, blocking collectives, across(): lax.all_to_all(x, 'z', split_axis=0, concat_axis=0, axis_index_groups=[or...  27.8 us
    all_to_all x3, waiting for transfers between devices, across(): lax.all_to_all(x, 'z', split_axis=0, concat_axis=0, axis_index_groups=[or...  19.9 us
    pallas_call x8, Pallas kernels, call(): pl.pallas_call(kernel, out_shape=out_shape, in_specs=[smem] * len(scalars...  16.1 us
    ppermute x4, starting transfers between devices, to_pair(): return lax.ppermute(x, 'pair', SWAP)  13.9 us
    ppermute x6, starting transfers between devices, to_core(): return lax.ppermute(x, 'core', SWAP)  12.1 us
    ppermute x4, waiting for transfers between devices, to_pair(): return lax.ppermute(x, 'pair', SWAP)  4.91 us
    ppermute x6, waiting for transfers between devices, to_core(): return lax.ppermute(x, 'core', SWAP)  4.86 us
  transfers between devices with their start and end apart: 13, of which 11 were waited for; matrix products, arithmetic and copies ran while one was open for 1% of the time, Pallas kernels for 4%

profile of v6, /device:TPU:6, one launch (start us, length us, event | category | flops | bytes accessed | tf_op | source)
XLA Modules:
  0.0 170.7 jit_solution(5310709497369601282)
XLA Ops:
  0.6 1.5 pack.1
  2.2 31.1 %all-to-all-start = ((bf16[32,8,128]{2,1,0:T(8,128)(2,1)}), bf16[32,8,128]{2,1,0:T(8,128)(2,1)S(1)}, u32[]{:S(2)}, u32[]{:S(2)}) async-start(bf16[32,8,128]{2,1,0:T(8,128)(2,1)} %get-tuple-element.45), calls=%async_computation | async-start | bytes 131072 | tf_op jit(solution)/shard_map/all_to_all | solution.py:320
  33.3 3.5 %collective-permute-start = (bf16[256,128]{1,0:T(8,128)(2,1)S(1)}, bf16[256,128]{1,0:T(8,128)(2,1)S(1)}, u32[]{:S(2)}, u32[]{:S(2)}) collective-permute-start(bf16[256,128]{1,0:T(8,128)(2,1)S(1)} %get-tuple-element.55.own_a), channel_id=1, source_target_pairs={{0,1},{1,0},{2,3},{3,2},{4,5},{5,4},{6,7},{7,6},{8,9},{9,8},{10,11... | collective-permute-start | bytes 196616 | tf_op jit(solution)/shard_map/ppermute | solution.py:312
  36.8 0.8 copy.9
  37.6 0.1 reshape.17.picks
  37.7 1.1 stack_heads.1
  38.9 0.1 stack.19.info
  39.0 0.4 collective-permute-done.own_b
  39.4 4.9 %all-to-all-done.banded_ref = bf16[32,8,128]{2,1,0:T(8,128)(2,1)S(1)} async-done(((bf16[32,8,128]{2,1,0:T(8,128)(2,1)}), bf16[32,8,128]{2,1,0:T(8,128)(2,1)S(1)}, u32[]{:S(2)}, u32[]{:S(2)}) %all-to-all-start) | async-done | bytes 65568 | tf_op jit(solution)/shard_map/all_to_all | solution.py:320
  44.3 1.5 gather.1
  45.8 18.6 %all-to-all-start.1 = ((bf16[32,16,128]{2,1,0:T(8,128)(2,1)}), bf16[32,16,128]{2,1,0:T(8,128)(2,1)S(1)}, u32[]{:S(2)}, u32[]{:S(2)}) async-start(bf16[32,16,128]{2,1,0:T(8,128)(2,1)} %gather.1), calls=%async_computation.1 | async-start | bytes 262144 | tf_op jit(solution)/shard_map/all_to_all | solution.py:320
  64.5 1.9 %collective-permute-start.1 = (bf16[256,128]{1,0:T(8,128)(2,1)S(1)}, bf16[256,128]{1,0:T(8,128)(2,1)S(1)}, u32[]{:S(2)}, u32[]{:S(2)}) collective-permute-start(bf16[256,128]{1,0:T(8,128)(2,1)S(1)} %get-tuple-element.55.own_a), channel_id=1, source_target_pairs={{0,16},{16,0},{1,17},{17,1},{2,18},{18,2},{3,19},{19,3},{4,20},{20... | collective-permute-start | bytes 196616 | tf_op jit(solution)/shard_map/ppermute | solution.py:315
  66.4 2.4 %collective-permute-start.2 = (bf16[256,128]{1,0:T(8,128)(2,1)S(1)}, bf16[256,128]{1,0:T(8,128)(2,1)S(1)}, u32[]{:S(2)}, u32[]{:S(2)}) collective-permute-start(bf16[256,128]{1,0:T(8,128)(2,1)S(1)} %collective-permute-done.own_b), channel_id=1, source_target_pairs={{0,16},{16,0},{1,17},{17,1},{2,18},{18,2},{3,19},{19,3},{4,20},{20... | collective-permute-start | bytes 196616 | tf_op jit(solution)/shard_map/ppermute | solution.py:315
  68.8 0.0 collective-permute-done.1.own_c
  68.8 0.9 collective-permute-done.2.own_d
  69.7 1.5 own_scores.1
  71.1 7.9 %all-to-all-done.1.x_ref = bf16[32,16,128]{2,1,0:T(8,128)(2,1)S(1)} async-done(((bf16[32,16,128]{2,1,0:T(8,128)(2,1)}), bf16[32,16,128]{2,1,0:T(8,128)(2,1)S(1)}, u32[]{:S(2)}, u32[]{:S(2)}) %all-to-all-start.1) | async-done | bytes 131104 | tf_op jit(solution)/shard_map/all_to_all | solution.py:320
  79.1 3.5 %collective-permute-start.3 = (bf16[32,16,128]{2,1,0:T(8,128)(2,1)S(1)}, bf16[32,16,128]{2,1,0:T(8,128)(2,1)S(1)}, u32[]{:S(2)}, u32[]{:S(2)}) collective-permute-start(bf16[32,16,128]{2,1,0:T(8,128)(2,1)S(1)} %all-to-all-done.1.x_ref), channel_id=1, source_target_pairs={{0,1},{1,0},{2,3},{3,2},{4,5},{5,4},{6,7},{7,6},{8,9},{9,8},{10,11... | collective-permute-start | bytes 393224 | tf_op jit(solution)/shard_map/ppermute | solution.py:312
  82.6 1.9 %collective-permute-start.4 = (bf16[32,16,128]{2,1,0:T(8,128)(2,1)S(1)}, bf16[32,16,128]{2,1,0:T(8,128)(2,1)S(1)}, u32[]{:S(2)}, u32[]{:S(2)}) collective-permute-start(bf16[32,16,128]{2,1,0:T(8,128)(2,1)S(1)} %all-to-all-done.1.x_ref), channel_id=1, source_target_pairs={{0,16},{16,0},{1,17},{17,1},{2,18},{18,2},{3,19},{19,3},{4,20},{20... | collective-permute-start | bytes 393224 | tf_op jit(solution)/shard_map/ppermute | solution.py:315
  84.5 1.4 collective-permute-done.3.y_ref
  85.9 1.9 %collective-permute-start.5 = (bf16[32,16,128]{2,1,0:T(8,128)(2,1)S(1)}, bf16[32,16,128]{2,1,0:T(8,128)(2,1)S(1)}, u32[]{:S(2)}, u32[]{:S(2)}) collective-permute-start(bf16[32,16,128]{2,1,0:T(8,128)(2,1)S(1)} %collective-permute-done.3.y_ref), channel_id=1, source_target_pairs={{0,16},{16,0},{1,17},{17,1},{2,18},{18,2},{3,19},{19,3},{4,20},{20... | collective-permute-start | bytes 393224 | tf_op jit(solution)/shard_map/ppermute | solution.py:315
  87.9 0.0 collective-permute-done.4.xc_ref
  87.9 1.3 collective-permute-done.5.yc_ref
  89.2 5.2 %picked_grads.1 = (f32[32,16,128]{2,1,0:T(8,128)S(1)}, f32[32,16,128]{2,1,0:T(8,128)S(1)}, bf16[2,32,16,128]{3,2,1,0:T(8,128)(2,1)S(1)}, bf16[1024,1024]{1,0:T(8...) custom-call(s32[5]{0:T(128)S(1)} %stack.19.info, ...), custom_call_target="tpu_custom_call" | custom-call | tf_op jit(solution)/shard_map/picked_grads/pallas_call | solution.py:222
  94.4 2.1 %collective-permute-start.6 = (bf16[2,32,16,128]{3,2,1,0:T(8,128)(2,1)S(1)}, bf16[2,32,16,128]{3,2,1,0:T(8,128)(2,1)S(1)}, u32[]{:S(2)}, u32[]{:S(2)}) collective-permute-start(bf16[2,32,16,128]{3,2,1,0:T(8,128)(2,1)S(1)} %get-tuple-element.75), channel_id=1, source_target_pairs={{0,16},{16,0},{1,17},{17,1},{2,18},{18,2},{3,19},{19,3},{4,20},{20... | collective-permute-start | bytes 786440 | tf_op jit(solution)/shard_map/ppermute | solution.py:315
  96.4 1.4 collective-permute-done.6
  97.8 3.5 %collective-permute-start.7 = (bf16[32,16,128]{2,1,0:T(8,128)(2,1)S(1)}, bf16[32,16,128]{2,1,0:T(8,128)(2,1)S(1)}, u32[]{:S(2)}, u32[]{:S(2)}) collective-permute-start(bf16[32,16,128]{2,1,0:T(8,128)(2,1)S(1)} %fusion), channel_id=1, source_target_pairs={{0,1},{1,0},{2,3},{3,2},{4,5},{5,4},{6,7},{7,6},{8,9},{9,8},{10,11... | collective-permute-start | bytes 393224 | tf_op jit(solution)/shard_map/ppermute | solution.py:312
  101.3 3.6 %row_outputs.1 = (bf16[256,512]{1,0:T(8,128)(2,1)}, f32[256,512]{1,0:T(8,128)}, f32[256,128]{1,0:T(8,128)S(1)}, f32[256,128]{1,0:T(8,128)S(1)}, bf16[2,256,128]{2,1,0:T(8,128)(2,1)S(1)}) custom-call(s32[5]{0:T(128)S(1)} %stack.19.info, bf16[1024,128]{1,0:T(8,128)(2,1)S(1)} %get-tuple-element.49.q_all, bf16[1024,128]{1,0:T(8,128)(2,1)S(1)} %get-tuple-element.50.g_all, ...), custom_call_target="tpu_custom_call" | custom-call | tf_op jit(solution)/shard_map/row_outputs/pallas_call | solution.py:222
  104.9 0.4 collective-permute-done.7
  105.3 0.7 fusion.2
  106.0 18.7 %all-to-all-start.2 = ((bf16[32,16,128]{2,1,0:T(8,128)(2,1)}), bf16[32,16,128]{2,1,0:T(8,128)(2,1)S(1)}, u32[]{:S(2)}, u32[]{:S(2)}) async-start(bf16[32,16,128]{2,1,0:T(8,128)(2,1)} %fusion.2), calls=%async_computation.2 | async-start | bytes 262144 | tf_op jit(solution)/shard_map/all_to_all | solution.py:320
  124.7 1.9 %collective-permute-start.8 = (bf16[2,256,128]{2,1,0:T(8,128)(2,1)S(1)}, bf16[2,256,128]{2,1,0:T(8,128)(2,1)S(1)}, u32[]{:S(2)}, u32[]{:S(2)}) collective-permute-start(bf16[2,256,128]{2,1,0:T(8,128)(2,1)S(1)} %get-tuple-element.79), channel_id=1, source_target_pairs={{0,16},{16,0},{1,17},{17,1},{2,18},{18,2},{3,19},{19,3},{4,20},{20... | collective-permute-start | bytes 393224 | tf_op jit(solution)/shard_map/ppermute | solution.py:315
  126.6 1.3 collective-permute-done.8.got_ref
  128.0 3.5 %collective-permute-start.9 = (bf16[256,128]{1,0:T(8,128)(2,1)S(1)}, bf16[256,128]{1,0:T(8,128)(2,1)S(1)}, u32[]{:S(2)}, u32[]{:S(2)}) collective-permute-start(bf16[256,128]{1,0:T(8,128)(2,1)S(1)} %fusion.3), channel_id=1, source_target_pairs={{0,1},{1,0},{2,3},{3,2},{4,5},{5,4},{6,7},{7,6},{8,9},{9,8},{10,11... | collective-permute-start | bytes 196616 | tf_op jit(solution)/shard_map/ppermute | solution.py:312
  131.5 2.7 %collective-permute-done.9.pair_ref = bf16[256,128]{1,0:T(8,128)(2,1)S(1)} collective-permute-done((bf16[256,128]{1,0:T(8,128)(2,1)S(1)}, bf16[256,128]{1,0:T(8,128)(2,1)S(1)}, u32[]{:S(2)}, u32[]{:S(2)}) %collective-permute-start.9) | collective-permute-done | bytes 65568 | tf_op jit(solution)/shard_map/ppermute | solution.py:312
  134.1 7.1 %all-to-all-done.2.landed_ref = bf16[32,16,128]{2,1,0:T(8,128)(2,1)S(1)} async-done(((bf16[32,16,128]{2,1,0:T(8,128)(2,1)}), bf16[32,16,128]{2,1,0:T(8,128)(2,1)S(1)}, u32[]{:S(2)}, u32[]{:S(2)}) %all-to-all-start.2) | async-done | bytes 131104 | tf_op jit(solution)/shard_map/all_to_all | solution.py:320
  141.2 0.9 scatter.1
  142.1 27.8 %all_to_all.20.back_ref = bf16[32,8,128]{2,1,0:T(8,128)(2,1)S(1)} all-to-all(bf16[32,8,128]{2,1,0:T(8,128)(2,1)S(1)} %scatter.1), channel_id=1, replica_groups={{640,96,576,32,512,992,448,928,384,864,320,800,256,736,192,672,128,608,..., dimensions={0} | all-to-all | bytes 131072 | tf_op jit(solution)/shard_map/all_to_all | solution.py:320
  170.0 0.7 unpack.1
  (2 shorter events, 0.1 us)
Async XLA Ops:
  2.2 42.1 %all-to-all-start = ((bf16[32,8,128]{2,1,0:T(8,128)(2,1)}), bf16[32,8,128]{2,1,0:T(8,128)(2,1)S(1)}, u32[]{:S(2)}, u32[]{:S(2)}) async-start(bf16[32,8,128]{2,1,0:T(8,128)(2,1)} %get-tuple-element.45), calls=%async_computation | async-start | bytes 131072 | tf_op jit(solution)/shard_map/all_to_all | solution.py:320
  33.3 6.2 %collective-permute-start = (bf16[256,128]{1,0:T(8,128)(2,1)S(1)}, bf16[256,128]{1,0:T(8,128)(2,1)S(1)}, u32[]{:S(2)}, u32[]{:S(2)}) collective-permute-start(bf16[256,128]{1,0:T(8,128)(2,1)S(1)} %get-tuple-element.55.own_a), channel_id=1, source_target_pairs={{0,1},{1,0},{2,3},{3,2},{4,5},{5,4},{6,7},{7,6},{8,9},{9,8},{10,11... | collective-permute-start | bytes 196616 | tf_op jit(solution)/shard_map/ppermute | solution.py:312
  45.8 33.3 %all-to-all-start.1 = ((bf16[32,16,128]{2,1,0:T(8,128)(2,1)}), bf16[32,16,128]{2,1,0:T(8,128)(2,1)S(1)}, u32[]{:S(2)}, u32[]{:S(2)}) async-start(bf16[32,16,128]{2,1,0:T(8,128)(2,1)} %gather.1), calls=%async_computation.1 | async-start | bytes 262144 | tf_op jit(solution)/shard_map/all_to_all | solution.py:320
  64.5 4.3 %collective-permute-start.1 = (bf16[256,128]{1,0:T(8,128)(2,1)S(1)}, bf16[256,128]{1,0:T(8,128)(2,1)S(1)}, u32[]{:S(2)}, u32[]{:S(2)}) collective-permute-start(bf16[256,128]{1,0:T(8,128)(2,1)S(1)} %get-tuple-element.55.own_a), channel_id=1, source_target_pairs={{0,16},{16,0},{1,17},{17,1},{2,18},{18,2},{3,19},{19,3},{4,20},{20... | collective-permute-start | bytes 196616 | tf_op jit(solution)/shard_map/ppermute | solution.py:315
  66.4 3.3 %collective-permute-start.2 = (bf16[256,128]{1,0:T(8,128)(2,1)S(1)}, bf16[256,128]{1,0:T(8,128)(2,1)S(1)}, u32[]{:S(2)}, u32[]{:S(2)}) collective-permute-start(bf16[256,128]{1,0:T(8,128)(2,1)S(1)} %collective-permute-done.own_b), channel_id=1, source_target_pairs={{0,16},{16,0},{1,17},{17,1},{2,18},{18,2},{3,19},{19,3},{4,20},{20... | collective-permute-start | bytes 196616 | tf_op jit(solution)/shard_map/ppermute | solution.py:315
  79.1 6.8 %collective-permute-start.3 = (bf16[32,16,128]{2,1,0:T(8,128)(2,1)S(1)}, bf16[32,16,128]{2,1,0:T(8,128)(2,1)S(1)}, u32[]{:S(2)}, u32[]{:S(2)}) collective-permute-start(bf16[32,16,128]{2,1,0:T(8,128)(2,1)S(1)} %all-to-all-done.1.x_ref), channel_id=1, source_target_pairs={{0,1},{1,0},{2,3},{3,2},{4,5},{5,4},{6,7},{7,6},{8,9},{9,8},{10,11... | collective-permute-start | bytes 393224 | tf_op jit(solution)/shard_map/ppermute | solution.py:312
  82.6 5.3 %collective-permute-start.4 = (bf16[32,16,128]{2,1,0:T(8,128)(2,1)S(1)}, bf16[32,16,128]{2,1,0:T(8,128)(2,1)S(1)}, u32[]{:S(2)}, u32[]{:S(2)}) collective-permute-start(bf16[32,16,128]{2,1,0:T(8,128)(2,1)S(1)} %all-to-all-done.1.x_ref), channel_id=1, source_target_pairs={{0,16},{16,0},{1,17},{17,1},{2,18},{18,2},{3,19},{19,3},{4,20},{20... | collective-permute-start | bytes 393224 | tf_op jit(solution)/shard_map/ppermute | solution.py:315
  85.9 3.2 %collective-permute-start.5 = (bf16[32,16,128]{2,1,0:T(8,128)(2,1)S(1)}, bf16[32,16,128]{2,1,0:T(8,128)(2,1)S(1)}, u32[]{:S(2)}, u32[]{:S(2)}) collective-permute-start(bf16[32,16,128]{2,1,0:T(8,128)(2,1)S(1)} %collective-permute-done.3.y_ref), channel_id=1, source_target_pairs={{0,16},{16,0},{1,17},{17,1},{2,18},{18,2},{3,19},{19,3},{4,20},{20... | collective-permute-start | bytes 393224 | tf_op jit(solution)/shard_map/ppermute | solution.py:315
  94.4 3.4 %collective-permute-start.6 = (bf16[2,32,16,128]{3,2,1,0:T(8,128)(2,1)S(1)}, bf16[2,32,16,128]{3,2,1,0:T(8,128)(2,1)S(1)}, u32[]{:S(2)}, u32[]{:S(2)}) collective-permute-start(bf16[2,32,16,128]{3,2,1,0:T(8,128)(2,1)S(1)} %get-tuple-element.75), channel_id=1, source_target_pairs={{0,16},{16,0},{1,17},{17,1},{2,18},{18,2},{3,19},{19,3},{4,20},{20... | collective-permute-start | bytes 786440 | tf_op jit(solution)/shard_map/ppermute | solution.py:315
  97.8 7.4 %collective-permute-start.7 = (bf16[32,16,128]{2,1,0:T(8,128)(2,1)S(1)}, bf16[32,16,128]{2,1,0:T(8,128)(2,1)S(1)}, u32[]{:S(2)}, u32[]{:S(2)}) collective-permute-start(bf16[32,16,128]{2,1,0:T(8,128)(2,1)S(1)} %fusion), channel_id=1, source_target_pairs={{0,1},{1,0},{2,3},{3,2},{4,5},{5,4},{6,7},{7,6},{8,9},{9,8},{10,11... | collective-permute-start | bytes 393224 | tf_op jit(solution)/shard_map/ppermute | solution.py:312
  106.0 35.3 %all-to-all-start.2 = ((bf16[32,16,128]{2,1,0:T(8,128)(2,1)}), bf16[32,16,128]{2,1,0:T(8,128)(2,1)S(1)}, u32[]{:S(2)}, u32[]{:S(2)}) async-start(bf16[32,16,128]{2,1,0:T(8,128)(2,1)} %fusion.2), calls=%async_computation.2 | async-start | bytes 262144 | tf_op jit(solution)/shard_map/all_to_all | solution.py:320
  124.7 3.2 %collective-permute-start.8 = (bf16[2,256,128]{2,1,0:T(8,128)(2,1)S(1)}, bf16[2,256,128]{2,1,0:T(8,128)(2,1)S(1)}, u32[]{:S(2)}, u32[]{:S(2)}) collective-permute-start(bf16[2,256,128]{2,1,0:T(8,128)(2,1)S(1)} %get-tuple-element.79), channel_id=1, source_target_pairs={{0,16},{16,0},{1,17},{17,1},{2,18},{18,2},{3,19},{19,3},{4,20},{20... | collective-permute-start | bytes 393224 | tf_op jit(solution)/shard_map/ppermute | solution.py:315
  128.0 6.2 %collective-permute-start.9 = (bf16[256,128]{1,0:T(8,128)(2,1)S(1)}, bf16[256,128]{1,0:T(8,128)(2,1)S(1)}, u32[]{:S(2)}, u32[]{:S(2)}) collective-permute-start(bf16[256,128]{1,0:T(8,128)(2,1)S(1)} %fusion.3), channel_id=1, source_target_pairs={{0,1},{1,0},{2,3},{3,2},{4,5},{5,4},{6,7},{7,6},{8,9},{9,8},{10,11... | collective-permute-start | bytes 196616 | tf_op jit(solution)/shard_map/ppermute | solution.py:312

commit v7 on v5

--- a/solution.py
+++ b/solution.py
@@ -17,6 +17,7 @@
 NT = (((1,), (1,)), ((), ()))
 NN = (((1,), (0,)), ((), ()))
 LIMIT = 4 << 20
+STEP = 128
 
 
 def first_rank(count):
@@ -127,8 +128,8 @@
         tuple(part[:, j].reshape(rows, dim) for part in half) for j in range(picked) for half in halves
     ]
     load_tiles(pieces, is_low, key_scr, value_scr)
-    spans = spans_of(key_scr, rows)
-    usable = [offset_of(info, picks, info[3], i // 2) <= info[3] for i in range(len(spans))]
+    spans = spans_of(key_scr, STEP)
+    usable = [offset_of(info, picks, info[3], i * STEP // BLOCK) <= info[3] for i in range(len(spans))]
     for h in range(heads):
         col = slice(h * rows, (h + 1) * rows)
         q, g = q_all[col, :], g_all[col, :]
@@ -160,7 +161,7 @@
             low_ref[span, col] = p.astype(BF16)
             ds_ref[span, col] = (p * (dp_scr[span, :] - delta)).astype(BF16)
     parts = []
-    for span in spans:
+    for span in spans_of(key_scr, rows):
         k = dot(ds_ref[span, :], q_all[...]) * scaling
         v = dot(low_ref[span, :], g_all[...])
         parts.append(join_features(is_low, k, v))
@@ -334,6 +335,12 @@
     many = picked * BLOCK
     banded = across(striped)
     own_pair = to_pair(own)
+    banded, own, own_pair = lax.optimization_barrier((banded, own, own_pair))
+    scratch = (pltpu.VMEM(banded_shape.shape, F32),)
+    outgoing = call(gather, "gather", striped_shape, (info, picks), (banded,), scratch)
+    outgoing, own, own_pair, queries, grad_output = lax.optimization_barrier(
+        (outgoing, own, own_pair, queries, grad_output)
+    )
     q_all, g_all = call(
         stack_heads,
         "stack_heads",
@@ -343,12 +350,6 @@
         (pltpu.SemaphoreType.DMA((2 * heads,)),),
         space=pltpu.HBM,
     )
-    banded, own, own_pair, q_all, g_all = lax.optimization_barrier(
-        (banded, own, own_pair, q_all, g_all)
-    )
-    scratch = (pltpu.VMEM(banded_shape.shape, F32),)
-    outgoing = call(gather, "gather", striped_shape, (info, picks), (banded,), scratch)
-    outgoing, own, own_pair = lax.optimization_barrier((outgoing, own, own_pair))
     fetched = across(outgoing)
     own_block = call(
         functools.partial(own_scores, heads),

time: 171 us -> 171 us (level)
  transfers between devices with their start and end apart: 13 -> 13, of which waited for: 11 -> 10; matrix products, arithmetic and copies ran while one was open for 1% -> 1% of each run, Pallas kernels for 4% -> 4%
where the time goes in v7:
time: 171 us; the launch traced here: 170 us
  starting transfers between devices  94.2 us (55%)
  waiting for transfers between devices  29.8 us (17%)
  blocking collectives  27.8 us (16%)
  Pallas kernels  15.8 us (9%)
    all_to_all x3, starting transfers between devices, across(): lax.all_to_all(x, 'z', split_axis=0, concat_axis=0, axis_index_groups=[or...  68.1 us
    all_to_all x1, blocking collectives, across(): lax.all_to_all(x, 'z', split_axis=0, concat_axis=0, axis_index_groups=[or...  27.8 us
    all_to_all x3, waiting for transfers between devices, across(): lax.all_to_all(x, 'z', split_axis=0, concat_axis=0, axis_index_groups=[or...  19.8 us
    pallas_call x8, Pallas kernels, call(): pl.pallas_call(kernel, out_shape=out_shape, in_specs=[smem] * len(scalars...  15.8 us
    ppermute x4, starting transfers between devices, to_pair(): return lax.ppermute(x, 'pair', SWAP)  13.9 us
    ppermute x6, starting transfers between devices, to_core(): return lax.ppermute(x, 'core', SWAP)  12.1 us
    ppermute x4, waiting for transfers between devices, to_pair(): return lax.ppermute(x, 'pair', SWAP)  6.06 us
    ppermute x6, waiting for transfers between devices, to_core(): return lax.ppermute(x, 'core', SWAP)  3.99 us
  transfers between devices with their start and end apart: 13, of which 10 were waited for; matrix products, arithmetic and copies ran while one was open for 1% of the time, Pallas kernels for 4%

profile of v7, /device:TPU:6, one launch (start us, length us, event | category | flops | bytes accessed | tf_op | source)
XLA Modules:
  0.0 170.2 jit_solution(8417633508264878868)
XLA Ops:
  0.6 1.5 pack.1
  2.2 31.1 %all-to-all-start = ((bf16[32,8,128]{2,1,0:T(8,128)(2,1)}), bf16[32,8,128]{2,1,0:T(8,128)(2,1)S(1)}, u32[]{:S(2)}, u32[]{:S(2)}) async-start(bf16[32,8,128]{2,1,0:T(8,128)(2,1)} %get-tuple-element.45), calls=%async_computation | async-start | bytes 131072 | tf_op jit(solution)/shard_map/all_to_all | solution.py:316
  33.3 3.5 %collective-permute-start = (bf16[256,128]{1,0:T(8,128)(2,1)S(1)}, bf16[256,128]{1,0:T(8,128)(2,1)S(1)}, u32[]{:S(2)}, u32[]{:S(2)}) collective-permute-start(bf16[256,128]{1,0:T(8,128)(2,1)S(1)} %get-tuple-element.55.own_a), channel_id=1, source_target_pairs={{0,1},{1,0},{2,3},{3,2},{4,5},{5,4},{6,7},{7,6},{8,9},{9,8},{10,11... | collective-permute-start | bytes 196616 | tf_op jit(solution)/shard_map/ppermute | solution.py:309
  36.8 0.8 copy.9
  37.6 0.1 reshape.17.picks
  37.7 0.1 stack.19.info
  37.8 1.6 collective-permute-done.own_b
  39.4 4.9 %all-to-all-done.banded_ref = bf16[32,8,128]{2,1,0:T(8,128)(2,1)S(1)} async-done(((bf16[32,8,128]{2,1,0:T(8,128)(2,1)}), bf16[32,8,128]{2,1,0:T(8,128)(2,1)S(1)}, u32[]{:S(2)}, u32[]{:S(2)}) %all-to-all-start) | async-done | bytes 65568 | tf_op jit(solution)/shard_map/all_to_all | solution.py:316
  44.3 1.4 gather.1
  45.7 18.6 %all-to-all-start.1 = ((bf16[32,16,128]{2,1,0:T(8,128)(2,1)}), bf16[32,16,128]{2,1,0:T(8,128)(2,1)S(1)}, u32[]{:S(2)}, u32[]{:S(2)}) async-start(bf16[32,16,128]{2,1,0:T(8,128)(2,1)} %gather.1), calls=%async_computation.1 | async-start | bytes 262144 | tf_op jit(solution)/shard_map/all_to_all | solution.py:316
  64.3 1.9 %collective-permute-start.1 = (bf16[256,128]{1,0:T(8,128)(2,1)S(1)}, bf16[256,128]{1,0:T(8,128)(2,1)S(1)}, u32[]{:S(2)}, u32[]{:S(2)}) collective-permute-start(bf16[256,128]{1,0:T(8,128)(2,1)S(1)} %get-tuple-element.55.own_a), channel_id=1, source_target_pairs={{0,16},{16,0},{1,17},{17,1},{2,18},{18,2},{3,19},{19,3},{4,20},{20... | collective-permute-start | bytes 196616 | tf_op jit(solution)/shard_map/ppermute | solution.py:312
  66.2 2.4 %collective-permute-start.2 = (bf16[256,128]{1,0:T(8,128)(2,1)S(1)}, bf16[256,128]{1,0:T(8,128)(2,1)S(1)}, u32[]{:S(2)}, u32[]{:S(2)}) collective-permute-start(bf16[256,128]{1,0:T(8,128)(2,1)S(1)} %collective-permute-done.own_b), channel_id=1, source_target_pairs={{0,16},{16,0},{1,17},{17,1},{2,18},{18,2},{3,19},{19,3},{4,20},{20... | collective-permute-start | bytes 196616 | tf_op jit(solution)/shard_map/ppermute | solution.py:312
  68.6 1.1 stack_heads.1
  69.8 0.0 collective-permute-done.1.own_c
  69.8 0.0 collective-permute-done.2.own_d
  69.8 1.5 own_scores.1
  71.3 8.0 %all-to-all-done.1.x_ref = bf16[32,16,128]{2,1,0:T(8,128)(2,1)S(1)} async-done(((bf16[32,16,128]{2,1,0:T(8,128)(2,1)}), bf16[32,16,128]{2,1,0:T(8,128)(2,1)S(1)}, u32[]{:S(2)}, u32[]{:S(2)}) %all-to-all-start.1) | async-done | bytes 131104 | tf_op jit(solution)/shard_map/all_to_all | solution.py:316
  79.3 3.5 %collective-permute-start.3 = (bf16[32,16,128]{2,1,0:T(8,128)(2,1)S(1)}, bf16[32,16,128]{2,1,0:T(8,128)(2,1)S(1)}, u32[]{:S(2)}, u32[]{:S(2)}) collective-permute-start(bf16[32,16,128]{2,1,0:T(8,128)(2,1)S(1)} %all-to-all-done.1.x_ref), channel_id=1, source_target_pairs={{0,1},{1,0},{2,3},{3,2},{4,5},{5,4},{6,7},{7,6},{8,9},{9,8},{10,11... | collective-permute-start | bytes 393224 | tf_op jit(solution)/shard_map/ppermute | solution.py:309
  82.8 1.9 %collective-permute-start.4 = (bf16[32,16,128]{2,1,0:T(8,128)(2,1)S(1)}, bf16[32,16,128]{2,1,0:T(8,128)(2,1)S(1)}, u32[]{:S(2)}, u32[]{:S(2)}) collective-permute-start(bf16[32,16,128]{2,1,0:T(8,128)(2,1)S(1)} %all-to-all-done.1.x_ref), channel_id=1, source_target_pairs={{0,16},{16,0},{1,17},{17,1},{2,18},{18,2},{3,19},{19,3},{4,20},{20... | collective-permute-start | bytes 393224 | tf_op jit(solution)/shard_map/ppermute | solution.py:312
  84.7 1.4 collective-permute-done.3.y_ref
  86.2 1.9 %collective-permute-start.5 = (bf16[32,16,128]{2,1,0:T(8,128)(2,1)S(1)}, bf16[32,16,128]{2,1,0:T(8,128)(2,1)S(1)}, u32[]{:S(2)}, u32[]{:S(2)}) collective-permute-start(bf16[32,16,128]{2,1,0:T(8,128)(2,1)S(1)} %collective-permute-done.3.y_ref), channel_id=1, source_target_pairs={{0,16},{16,0},{1,17},{17,1},{2,18},{18,2},{3,19},{19,3},{4,20},{20... | collective-permute-start | bytes 393224 | tf_op jit(solution)/shard_map/ppermute | solution.py:312
  88.1 0.0 collective-permute-done.4.xc_ref
  88.1 1.3 collective-permute-done.5.yc_ref
  89.4 5.0 %picked_grads.1 = (f32[32,16,128]{2,1,0:T(8,128)S(1)}, f32[32,16,128]{2,1,0:T(8,128)S(1)}, bf16[2,32,16,128]{3,2,1,0:T(8,128)(2,1)S(1)}, bf16[1024,1024]{1,0:T(8...) custom-call(s32[5]{0:T(128)S(1)} %stack.19.info, ...), custom_call_target="tpu_custom_call" | custom-call | tf_op jit(solution)/shard_map/picked_grads/pallas_call | solution.py:219
  94.4 2.1 %collective-permute-start.6 = (bf16[2,32,16,128]{3,2,1,0:T(8,128)(2,1)S(1)}, bf16[2,32,16,128]{3,2,1,0:T(8,128)(2,1)S(1)}, u32[]{:S(2)}, u32[]{:S(2)}) collective-permute-start(bf16[2,32,16,128]{3,2,1,0:T(8,128)(2,1)S(1)} %get-tuple-element.75), channel_id=1, source_target_pairs={{0,16},{16,0},{1,17},{17,1},{2,18},{18,2},{3,19},{19,3},{4,20},{20... | collective-permute-start | bytes 786440 | tf_op jit(solution)/shard_map/ppermute | solution.py:312
  96.5 1.4 collective-permute-done.6
  97.9 3.5 %collective-permute-start.7 = (bf16[32,16,128]{2,1,0:T(8,128)(2,1)S(1)}, bf16[32,16,128]{2,1,0:T(8,128)(2,1)S(1)}, u32[]{:S(2)}, u32[]{:S(2)}) collective-permute-start(bf16[32,16,128]{2,1,0:T(8,128)(2,1)S(1)} %fusion), channel_id=1, source_target_pairs={{0,1},{1,0},{2,3},{3,2},{4,5},{5,4},{6,7},{7,6},{8,9},{9,8},{10,11... | collective-permute-start | bytes 393224 | tf_op jit(solution)/shard_map/ppermute | solution.py:309
  101.3 3.6 %row_outputs.1 = (bf16[256,512]{1,0:T(8,128)(2,1)}, f32[256,512]{1,0:T(8,128)}, f32[256,128]{1,0:T(8,128)S(1)}, f32[256,128]{1,0:T(8,128)S(1)}, bf16[2,256,128]{2,1,0:T(8,128)(2,1)S(1)}) custom-call(s32[5]{0:T(128)S(1)} %stack.19.info, bf16[1024,128]{1,0:T(8,128)(2,1)S(1)} %get-tuple-element.52.q_all, bf16[1024,128]{1,0:T(8,128)(2,1)S(1)} %get-tuple-element.53.g_all, ...), custom_call_target="tpu_custom_call" | custom-call | tf_op jit(solution)/shard_map/row_outputs/pallas_call | solution.py:219
  104.9 0.4 collective-permute-done.7
  105.3 0.7 fusion.2
  106.0 18.4 %all-to-all-start.2 = ((bf16[32,16,128]{2,1,0:T(8,128)(2,1)}), bf16[32,16,128]{2,1,0:T(8,128)(2,1)S(1)}, u32[]{:S(2)}, u32[]{:S(2)}) async-start(bf16[32,16,128]{2,1,0:T(8,128)(2,1)} %fusion.2), calls=%async_computation.2 | async-start | bytes 262144 | tf_op jit(solution)/shard_map/all_to_all | solution.py:316
  124.4 1.9 %collective-permute-start.8 = (bf16[2,256,128]{2,1,0:T(8,128)(2,1)S(1)}, bf16[2,256,128]{2,1,0:T(8,128)(2,1)S(1)}, u32[]{:S(2)}, u32[]{:S(2)}) collective-permute-start(bf16[2,256,128]{2,1,0:T(8,128)(2,1)S(1)} %get-tuple-element.79), channel_id=1, source_target_pairs={{0,16},{16,0},{1,17},{17,1},{2,18},{18,2},{3,19},{19,3},{4,20},{20... | collective-permute-start | bytes 393224 | tf_op jit(solution)/shard_map/ppermute | solution.py:312
  126.4 1.3 collective-permute-done.8.got_ref
  127.7 3.5 %collective-permute-start.9 = (bf16[256,128]{1,0:T(8,128)(2,1)S(1)}, bf16[256,128]{1,0:T(8,128)(2,1)S(1)}, u32[]{:S(2)}, u32[]{:S(2)}) collective-permute-start(bf16[256,128]{1,0:T(8,128)(2,1)S(1)} %fusion.3), channel_id=1, source_target_pairs={{0,1},{1,0},{2,3},{3,2},{4,5},{5,4},{6,7},{7,6},{8,9},{9,8},{10,11... | collective-permute-start | bytes 196616 | tf_op jit(solution)/shard_map/ppermute | solution.py:309
  131.2 2.7 %collective-permute-done.9.pair_ref = bf16[256,128]{1,0:T(8,128)(2,1)S(1)} collective-permute-done((bf16[256,128]{1,0:T(8,128)(2,1)S(1)}, bf16[256,128]{1,0:T(8,128)(2,1)S(1)}, u32[]{:S(2)}, u32[]{:S(2)}) %collective-permute-start.9) | collective-permute-done | bytes 65568 | tf_op jit(solution)/shard_map/ppermute | solution.py:309
  133.9 6.9 %all-to-all-done.2.landed_ref = bf16[32,16,128]{2,1,0:T(8,128)(2,1)S(1)} async-done(((bf16[32,16,128]{2,1,0:T(8,128)(2,1)}), bf16[32,16,128]{2,1,0:T(8,128)(2,1)S(1)}, u32[]{:S(2)}, u32[]{:S(2)}) %all-to-all-start.2) | async-done | bytes 131104 | tf_op jit(solution)/shard_map/all_to_all | solution.py:316
  140.7 0.9 scatter.1
  141.6 27.8 %all_to_all.20.back_ref = bf16[32,8,128]{2,1,0:T(8,128)(2,1)S(1)} all-to-all(bf16[32,8,128]{2,1,0:T(8,128)(2,1)S(1)} %scatter.1), channel_id=1, replica_groups={{640,672,704,736,768,800,832,864,896,928,960,992,0,32,64,96,128,160,192..., dimensions={0} | all-to-all | bytes 131072 | tf_op jit(solution)/shard_map/all_to_all | solution.py:316
  169.5 0.7 unpack.1
  (2 shorter events, 0.1 us)
Async XLA Ops:
  2.2 42.1 %all-to-all-start = ((bf16[32,8,128]{2,1,0:T(8,128)(2,1)}), bf16[32,8,128]{2,1,0:T(8,128)(2,1)S(1)}, u32[]{:S(2)}, u32[]{:S(2)}) async-start(bf16[32,8,128]{2,1,0:T(8,128)(2,1)} %get-tuple-element.45), calls=%async_computation | async-start | bytes 131072 | tf_op jit(solution)/shard_map/all_to_all | solution.py:316
  33.3 6.2 %collective-permute-start = (bf16[256,128]{1,0:T(8,128)(2,1)S(1)}, bf16[256,128]{1,0:T(8,128)(2,1)S(1)}, u32[]{:S(2)}, u32[]{:S(2)}) collective-permute-start(bf16[256,128]{1,0:T(8,128)(2,1)S(1)} %get-tuple-element.55.own_a), channel_id=1, source_target_pairs={{0,1},{1,0},{2,3},{3,2},{4,5},{5,4},{6,7},{7,6},{8,9},{9,8},{10,11... | collective-permute-start | bytes 196616 | tf_op jit(solution)/shard_map/ppermute | solution.py:309
  45.7 33.6 %all-to-all-start.1 = ((bf16[32,16,128]{2,1,0:T(8,128)(2,1)}), bf16[32,16,128]{2,1,0:T(8,128)(2,1)S(1)}, u32[]{:S(2)}, u32[]{:S(2)}) async-start(bf16[32,16,128]{2,1,0:T(8,128)(2,1)} %gather.1), calls=%async_computation.1 | async-start | bytes 262144 | tf_op jit(solution)/shard_map/all_to_all | solution.py:316
  64.3 5.5 %collective-permute-start.1 = (bf16[256,128]{1,0:T(8,128)(2,1)S(1)}, bf16[256,128]{1,0:T(8,128)(2,1)S(1)}, u32[]{:S(2)}, u32[]{:S(2)}) collective-permute-start(bf16[256,128]{1,0:T(8,128)(2,1)S(1)} %get-tuple-element.55.own_a), channel_id=1, source_target_pairs={{0,16},{16,0},{1,17},{17,1},{2,18},{18,2},{3,19},{19,3},{4,20},{20... | collective-permute-start | bytes 196616 | tf_op jit(solution)/shard_map/ppermute | solution.py:312
  66.2 3.6 %collective-permute-start.2 = (bf16[256,128]{1,0:T(8,128)(2,1)S(1)}, bf16[256,128]{1,0:T(8,128)(2,1)S(1)}, u32[]{:S(2)}, u32[]{:S(2)}) collective-permute-start(bf16[256,128]{1,0:T(8,128)(2,1)S(1)} %collective-permute-done.own_b), channel_id=1, source_target_pairs={{0,16},{16,0},{1,17},{17,1},{2,18},{18,2},{3,19},{19,3},{4,20},{20... | collective-permute-start | bytes 196616 | tf_op jit(solution)/shard_map/ppermute | solution.py:312
  79.3 6.8 %collective-permute-start.3 = (bf16[32,16,128]{2,1,0:T(8,128)(2,1)S(1)}, bf16[32,16,128]{2,1,0:T(8,128)(2,1)S(1)}, u32[]{:S(2)}, u32[]{:S(2)}) collective-permute-start(bf16[32,16,128]{2,1,0:T(8,128)(2,1)S(1)} %all-to-all-done.1.x_ref), channel_id=1, source_target_pairs={{0,1},{1,0},{2,3},{3,2},{4,5},{5,4},{6,7},{7,6},{8,9},{9,8},{10,11... | collective-permute-start | bytes 393224 | tf_op jit(solution)/shard_map/ppermute | solution.py:309
  82.8 5.3 %collective-permute-start.4 = (bf16[32,16,128]{2,1,0:T(8,128)(2,1)S(1)}, bf16[32,16,128]{2,1,0:T(8,128)(2,1)S(1)}, u32[]{:S(2)}, u32[]{:S(2)}) collective-permute-start(bf16[32,16,128]{2,1,0:T(8,128)(2,1)S(1)} %all-to-all-done.1.x_ref), channel_id=1, source_target_pairs={{0,16},{16,0},{1,17},{17,1},{2,18},{18,2},{3,19},{19,3},{4,20},{20... | collective-permute-start | bytes 393224 | tf_op jit(solution)/shard_map/ppermute | solution.py:312
  86.2 3.2 %collective-permute-start.5 = (bf16[32,16,128]{2,1,0:T(8,128)(2,1)S(1)}, bf16[32,16,128]{2,1,0:T(8,128)(2,1)S(1)}, u32[]{:S(2)}, u32[]{:S(2)}) collective-permute-start(bf16[32,16,128]{2,1,0:T(8,128)(2,1)S(1)} %collective-permute-done.3.y_ref), channel_id=1, source_target_pairs={{0,16},{16,0},{1,17},{17,1},{2,18},{18,2},{3,19},{19,3},{4,20},{20... | collective-permute-start | bytes 393224 | tf_op jit(solution)/shard_map/ppermute | solution.py:312
  94.4 3.4 %collective-permute-start.6 = (bf16[2,32,16,128]{3,2,1,0:T(8,128)(2,1)S(1)}, bf16[2,32,16,128]{3,2,1,0:T(8,128)(2,1)S(1)}, u32[]{:S(2)}, u32[]{:S(2)}) collective-permute-start(bf16[2,32,16,128]{3,2,1,0:T(8,128)(2,1)S(1)} %get-tuple-element.75), channel_id=1, source_target_pairs={{0,16},{16,0},{1,17},{17,1},{2,18},{18,2},{3,19},{19,3},{4,20},{20... | collective-permute-start | bytes 786440 | tf_op jit(solution)/shard_map/ppermute | solution.py:312
  97.9 7.4 %collective-permute-start.7 = (bf16[32,16,128]{2,1,0:T(8,128)(2,1)S(1)}, bf16[32,16,128]{2,1,0:T(8,128)(2,1)S(1)}, u32[]{:S(2)}, u32[]{:S(2)}) collective-permute-start(bf16[32,16,128]{2,1,0:T(8,128)(2,1)S(1)} %fusion), channel_id=1, source_target_pairs={{0,1},{1,0},{2,3},{3,2},{4,5},{5,4},{6,7},{7,6},{8,9},{9,8},{10,11... | collective-permute-start | bytes 393224 | tf_op jit(solution)/shard_map/ppermute | solution.py:309
  106.0 34.7 %all-to-all-start.2 = ((bf16[32,16,128]{2,1,0:T(8,128)(2,1)}), bf16[32,16,128]{2,1,0:T(8,128)(2,1)S(1)}, u32[]{:S(2)}, u32[]{:S(2)}) async-start(bf16[32,16,128]{2,1,0:T(8,128)(2,1)} %fusion.2), calls=%async_computation.2 | async-start | bytes 262144 | tf_op jit(solution)/shard_map/all_to_all | solution.py:316
  124.4 3.2 %collective-permute-start.8 = (bf16[2,256,128]{2,1,0:T(8,128)(2,1)S(1)}, bf16[2,256,128]{2,1,0:T(8,128)(2,1)S(1)}, u32[]{:S(2)}, u32[]{:S(2)}) collective-permute-start(bf16[2,256,128]{2,1,0:T(8,128)(2,1)S(1)} %get-tuple-element.79), channel_id=1, source_target_pairs={{0,16},{16,0},{1,17},{17,1},{2,18},{18,2},{3,19},{19,3},{4,20},{20... | collective-permute-start | bytes 393224 | tf_op jit(solution)/shard_map/ppermute | solution.py:312
  127.7 6.2 %collective-permute-start.9 = (bf16[256,128]{1,0:T(8,128)(2,1)S(1)}, bf16[256,128]{1,0:T(8,128)(2,1)S(1)}, u32[]{:S(2)}, u32[]{:S(2)}) collective-permute-start(bf16[256,128]{1,0:T(8,128)(2,1)S(1)} %fusion.3), channel_id=1, source_target_pairs={{0,1},{1,0},{2,3},{3,2},{4,5},{5,4},{6,7},{7,6},{8,9},{9,8},{10,11... | collective-permute-start | bytes 196616 | tf_op jit(solution)/shard_map/ppermute | solution.py:309
